TPU v7x, 256 devices: a whole 4x4x8 slice. The times are simulated.
256 devices in a mesh: dp: 16 (over x, z_hi, core), seq: 16 (over y, z_lo).
Axes of the slice: x: 4, y: 4, z: 8 (z_hi: 2, z_lo: 4; z = z_hi * 4 + z_lo), core: 2. Of those that a mesh axis runs over, the one named last changes fastest.
Arguments:
- tokens: bfloat16 [16, 2048, 1024], P('dp', 'seq'), may hold values from -6 to 6
- in_gain: float32 [1024], replicated, may hold values from 0.1 to 1.9
- w_proj: bfloat16 [1024, 4096], replicated, may hold values from -0.1875 to 0.1875
- out_gain: float32 [1024], replicated, may hold values from 0.1 to 1.9
- w_out: bfloat16 [1024, 1024], replicated, may hold values from -0.1875 to 0.1875
- rab_slope: float32 [8], replicated, may hold values from -1 to 0.2
- hist_blocks: int32 [16, 3], P('dp'), may hold values from 1 to 10, 16 in all within a row
- hist_tail: int32 [16, 3], P('dp'), may hold values from 1 to 128
- node_table: bfloat16 [4096, 1024], P('dp'), may hold values from -0.1875 to 0.1875
- subtree_map: int32 [64], replicated, may hold values from 0 to 63, each once
- beam_nodes: int32 [48, 1024], P('dp', 'seq'), may hold values from 0 to 4095
Outputs:
- layer_out: bfloat16 [16, 2048, 1024], P('dp', 'seq')
- beam_scores: float32 [48, 1024], P('dp', 'seq')
Inputs may be any that keep to these rules, and one draw needn't show every extreme that they name: `hist_blocks`: each row sums to 16; its largest entry is exactly 10. `subtree_map`: a permutation of 0 to 63.
All inputs are finite; a program needn't handle non-finite values.
Results may differ from a plain program's by a relative error of at most 0.0059.
Values may be sent and summed in bfloat16 or wider, within the bound.
No kernel may reach another device: no remote copies, remote signals or barrier semaphores. Data moves between devices by JAX's collectives and lax.ppermute only.
A program may use at most 128 MiB of HBM per device.

v0:
```python
import jax
import jax.numpy as jnp
from jax import lax
from jax.experimental import pallas as pl
from jax.experimental.pallas import tpu as pltpu
from jax.sharding import PartitionSpec as P


BLK = 128
SUBT = 64
USERS = 3
D = 1024
HEADS = 8
HD = 128
NSEQ = 16
MAXD = 10
UNROLL = 4
MASKED = -1e30
ROW_K, ROW_V, ROW_Q, ROWS_A = 0, 128, 256, 384
ROW_E, ROW_X, ROWS_B = 128, 144, 160
FAR = (2, 3, 6, 7)
NEAR = (0, 1, 4, 5)
SETS = [[0, 1, 2, 3, 8, 9, 10, 11], [4, 5, 6, 7, 12, 13, 14, 15]]
LIST = 128
GRANT = pltpu.CompilerParams(vmem_limit_bytes=16 << 20)


def head_of(seq):
    return (seq // 8) * 4 + seq % 4


def set_of(seq):
    return (seq // 4) % 2


def spread(q):
    return (q // 4) * 8 + q % 4


def place_of(q):
    return q % 2 + (q // 4) * 2 + ((q // 2) % 2) * 4


def silu(x):
    half = 0.5 * x
    return half + half * jnp.tanh(half)


def layer_norm(rows):
    centred = rows - jnp.mean(rows, axis=-1, keepdims=True)
    spread_ = jnp.mean(centred * centred, axis=-1, keepdims=True)
    return centred * lax.rsqrt(spread_ + 1e-05)


def user_starts(blocks_ref):
    one = blocks_ref[0, 0]
    return (0, one, one + blocks_ref[0, 1])


def project_kernel(blocks_ref, tail_ref, x_ref, gain_ref, w_ref, gate_ref, extra_ref, *refs):
    out_refs, weights, sems = refs[:HEADS], refs[HEADS], refs[HEADS + 1]
    me = lax.axis_index("seq")
    order = FAR + NEAR

    def copies(at):
        head = head_of(me) ^ order[at]
        return [
            pltpu.make_async_copy(
                w_ref.at[:, pl.ds(pl.multiple_of((group * HEADS + head) * HD, HD), HD)],
                weights.at[at, :, group * HD : (group + 1) * HD],
                sems.at[at, group],
            )
            for group in range(4)
        ]

    for at in range(HEADS):
        for copy in copies(at):
            copy.start()
    normed = (layer_norm(x_ref[...].astype(jnp.float32)) * gain_ref[...]).astype(jnp.bfloat16)
    for at, out_ref in enumerate(out_refs):
        for copy in copies(at):
            copy.wait()
        parts = silu(jnp.dot(normed, weights[at], preferred_element_type=jnp.float32))
        head = head_of(me) ^ order[at]
        gate_ref[:, pl.ds(pl.multiple_of(head * HD, HD), HD)] = parts[:, :HD].astype(jnp.bfloat16)
        out_ref[ROW_K:ROW_V, :] = parts[:, 2 * HD : 3 * HD].T.astype(jnp.bfloat16)
        out_ref[ROW_V:ROW_Q, :] = parts[:, 3 * HD :].astype(jnp.bfloat16)
        out_ref[ROW_Q:ROWS_A, :] = parts[:, HD : 2 * HD].astype(jnp.bfloat16)

    starts = user_starts(blocks_ref)
    last = jnp.int32(-1)
    for user in range(USERS):
        last = jnp.where(starts[user] + blocks_ref[0, user] - 1 == me, tail_ref[0, user] - 1, last)
    pick = (lax.broadcasted_iota(jnp.int32, (16, BLK), 1) == last).astype(jnp.bfloat16)
    gate_row = jnp.dot(pick, gate_ref[...], preferred_element_type=jnp.float32)[0:1]
    token_row = jnp.dot(pick, x_ref[...], preferred_element_type=jnp.float32)[0:1]
    pieces = [row[:, h * HD : (h + 1) * HD] for row in (gate_row, token_row) for h in range(HEADS)]
    extra_ref[...] = jnp.concatenate(pieces, axis=0).astype(jnp.bfloat16)


def prepare_kernel(
    blocks_ref, slope_ref, ids_ref, map_ref, bias_ref, list_ref, place_ref
):
    me, dp = lax.axis_index("seq"), lax.axis_index("dp")
    starts = user_starts(blocks_ref)
    slope = slope_ref[head_of(me)]
    offset = lax.broadcasted_iota(jnp.int32, (BLK, BLK), 0) - lax.broadcasted_iota(jnp.int32, (BLK, BLK), 1)
    for d in range(MAXD):
        gap = offset + d * BLK
        table = slope * jnp.log1p(jnp.maximum(gap, 0).astype(jnp.float32))
        bias_ref[d] = jnp.where(gap >= 0, table, MASKED) if d == 0 else table

    def fill(t, counts):
        b = (t // 4) * 8 + set_of(me) * 4 + t % 4
        begin = jnp.where(b >= starts[2], starts[2], jnp.where(b >= starts[1], starts[1], 0))

        def put(j, counts):
            apart = j ^ me
            cross = (apart // 4) % 2
            q = (apart // 8) * 4 + apart % 4
            late = cross * ((q // 2) % 2)
            code = (place_of(t ^ head_of(me)) * 16 + cross * 8 + place_of(q)) * 16 + b - j
            first, second = counts
            list_ref[jnp.where(late == 1, LIST + second, first)] = code
            return (first + 1 - late, second + late)

        return lax.fori_loop(begin, b + 1, put, counts)

    counts = lax.fori_loop(0, 8, fill, (jnp.int32(0), jnp.int32(0)))
    for which, count in enumerate(counts):
        for pad in range(UNROLL - 1):
            list_ref[which * LIST + count + pad] = 8 * 256
        list_ref[which * LIST + LIST - 1] = (count + UNROLL - 1) // UNROLL

    my_x, my_zh, my_c = dp // 4, (dp // 2) % 2, dp % 2
    subtree = lax.broadcasted_iota(jnp.int32, (64, 64), 0)
    diagonal = subtree == lax.broadcasted_iota(jnp.int32, (64, 64), 1)
    places = jnp.sum(jnp.where(diagonal, map_ref[...], 0), axis=1, keepdims=True)
    for user in range(USERS):
        end = starts[user] + blocks_ref[0, user] - 1
        ids = ids_ref[user : user + 1, :]
        block = jnp.sum(jnp.where(subtree == ids // SUBT, places, 0), axis=0, keepdims=True)
        row = block * SUBT + ids % SUBT
        owner, inside = row // 256, row % 256
        shard, at = inside // 32, inside % 32
        x_rel = (my_x - owner // 4 + 4) % 4
        zh_rel = (my_zh - (owner // 2) % 2 + 2) % 2
        c_rel = (my_c - owner % 2 + 2) % 2
        lane = c_rel * 64 + zh_rel * 32 + at
        source = (shard // 4) * 8 + set_of(end) * 4 + shard % 4
        place_ref[2 * user : 2 * user + 1, :] = source * 16 + user * 4 + x_rel
        place_ref[2 * user + 1 : 2 * user + 2, :] = lane


def run_pairs(list_ref, which, query, keys, values, bias_ref, acc):
    scale = HD ** (-0.5)

    def some(step, carry):
        products, targets = [], []
        for t in range(UNROLL):
            code = list_ref[which * LIST + step * UNROLL + t]
            mine, slot, d = code // 256, (code // 16) % 16, code % 16
            scores = jnp.dot(query(jnp.minimum(mine, 7)), keys(slot), preferred_element_type=jnp.float32)
            weights = silu(scores * scale + bias_ref[d]).astype(jnp.bfloat16)
            products.append(jnp.dot(weights, values(slot), preferred_element_type=jnp.float32))
            targets.append(mine)
        for mine, product in zip(targets, products):
            acc[mine] += product
        return carry

    lax.fori_loop(0, list_ref[which * LIST + LIST - 1], some, 0)


def sort_kernel(*refs):
    got_refs, kv_ref, queries_ref = refs[:4], refs[4], refs[5]
    for at, got_ref in enumerate(got_refs):
        kv_ref[at] = got_ref[ROW_K:ROW_Q, :]
        queries_ref[at] = got_ref[ROW_Q:ROWS_A, :]


def attend_first_kernel(
    list_ref, bias_ref, near_ref, far_ref, cross_ref, near_q_ref, far_q_ref, acc_ref, queries_ref, keep, acc
):
    for at in range(4):
        keep[at] = near_ref[at]
        keep[4 + at] = far_ref[at]
        keep[8 + at] = cross_ref[at]
        queries_ref[at] = near_q_ref[at]
        queries_ref[4 + at] = far_q_ref[at]
    acc[...] = jnp.zeros_like(acc)
    run_pairs(
        list_ref,
        0,
        lambda mine: queries_ref[mine],
        lambda slot: keep[slot, ROW_K:ROW_V, :],
        lambda slot: keep[slot, ROW_V:ROW_Q, :],
        bias_ref,
        acc,
    )
    acc_ref[...] = acc[0:8]


def attend_last_kernel(blocks_ref, tail_ref, list_ref, bias_ref, queries_ref, cross_ref, acc_ref, extra_ref, out_ref, acc):
    me = lax.axis_index("seq")
    mine = head_of(me)
    starts = user_starts(blocks_ref)
    acc[0:8] = acc_ref[...]
    acc[8] = jnp.zeros((BLK, HD), jnp.float32)

    def at(slot):
        return slot % 4

    run_pairs(
        list_ref,
        1,
        lambda own: queries_ref[own],
        lambda slot: cross_ref[at(slot), ROW_K:ROW_V, :],
        lambda slot: cross_ref[at(slot), ROW_V:ROW_Q, :],
        bias_ref,
        acc,
    )
    rows = []
    for user in range(USERS):
        end = starts[user] + blocks_ref[0, user] - 1
        here = set_of(end) == set_of(me)
        value = acc[place_of(head_of(end) ^ mine), pl.ds(tail_ref[0, user] - 1, 1), :]
        rows.append(jnp.where(here, value, 0.0))
    last = jnp.concatenate(rows + [jnp.zeros((16 - USERS, HD), jnp.float32)], axis=0).astype(jnp.bfloat16)
    row_at = lax.broadcasted_iota(jnp.int32, (BLK, HD), 0)
    for t in range(8):
        b = (t // 4) * 8 + set_of(me) * 4 + t % 4
        valid = jnp.int32(BLK)
        for user in range(USERS):
            valid = jnp.where(starts[user] + blocks_ref[0, user] - 1 == b, tail_ref[0, user], valid)
        out_ref[t, 0:ROW_E, :] = jnp.where(row_at < valid, acc[place_of(mine ^ t)], 0.0).astype(jnp.bfloat16)
        out_ref[t, ROW_E:ROW_X, :] = last
        out_ref[t, ROW_X:ROWS_B, :] = extra_ref[...]


def state_kernel(blocks_ref, mixed_ref, gain_ref, w_ref, ta_ref, tb_ref, tc_ref, td_ref, score_ref, table, sems):
    copies = [
        pltpu.make_async_copy(t_ref, table.at[x], sems.at[x]) for x, t_ref in enumerate((ta_ref, tb_ref, tc_ref, td_ref))
    ]
    for copy in copies:
        copy.start()
    starts = user_starts(blocks_ref)
    tail = jnp.concatenate([mixed_ref[h, ROW_E:ROW_X, :].astype(jnp.float32) for h in range(HEADS)], axis=1)
    gates, tokens = [], []
    for user in range(USERS):
        end = starts[user] + blocks_ref[0, user] - 1
        rows = mixed_ref[head_of(end), ROW_X:ROWS_B, :].astype(jnp.float32)
        gates.append(jnp.concatenate([rows[h : h + 1] for h in range(HEADS)], axis=1))
        tokens.append(jnp.concatenate([rows[HEADS + h : HEADS + h + 1] for h in range(HEADS)], axis=1))
    zeros = jnp.zeros((16 - USERS, D), jnp.float32)
    gate_tail = jnp.concatenate(gates + [zeros], axis=0)
    token_tail = jnp.concatenate(tokens + [zeros], axis=0)
    gated = (layer_norm(tail) * gain_ref[...] * gate_tail).astype(jnp.bfloat16)
    states = (token_tail + jnp.dot(gated, w_ref[...], preferred_element_type=jnp.float32)).astype(jnp.bfloat16)
    for copy in copies:
        copy.wait()
    parts = [
        lax.dot_general(states, table[x], (((1,), (1,)), ((), ())), preferred_element_type=jnp.float32) for x in range(4)
    ]
    rows = [part[user : user + 1] for user in range(USERS) for part in parts]
    block = jnp.concatenate(rows + [jnp.zeros((4, 128), jnp.float32)], axis=0)
    for to in range(NSEQ):
        score_ref[to] = block


def layer_kernel(mixed_ref, gate_ref, x_ref, gain_ref, w_ref, out_ref):
    mixed = jnp.concatenate([mixed_ref[h, 0:ROW_E, :].astype(jnp.float32) for h in range(HEADS)], axis=1)
    gated = (layer_norm(mixed) * gain_ref[...] * gate_ref[...].astype(jnp.float32)).astype(jnp.bfloat16)
    out_ref[...] = (
        x_ref[...].astype(jnp.float32) + jnp.dot(gated, w_ref[...], preferred_element_type=jnp.float32)
    ).astype(jnp.bfloat16)


def pick_kernel(score_ref, place_ref, out_ref):
    scores = score_ref[...].reshape(NSEQ * 16, 128)
    row_at = lax.broadcasted_iota(jnp.int32, (NSEQ * 16, 64), 0)
    lane_at = lax.broadcasted_iota(jnp.int32, (128, 64), 0)
    for user in range(USERS):
        row, lane = place_ref[2 * user : 2 * user + 1, :], place_ref[2 * user + 1 : 2 * user + 2, :]
        found = jnp.dot(
            scores,
            (lane_at == lane).astype(jnp.float32),
            preferred_element_type=jnp.float32,
            precision=lax.Precision.HIGHEST,
        )
        out_ref[user : user + 1, :] = jnp.sum(jnp.where(row_at == row, found, 0.0), axis=0, keepdims=True)


def vmem():
    return pl.BlockSpec(memory_space=pltpu.VMEM)


def in_hbm(value):
    return pltpu.with_memory_space_constraint(value, pltpu.HBM)


def smem():
    return pl.BlockSpec(memory_space=pltpu.SMEM)


def dp_shift(value, move):
    return lax.ppermute(value, "dp", [(i, move(i)) for i in range(16)])


def seq_xor(value, apart):
    return lax.ppermute(value, "seq", [(i, i ^ apart) for i in range(NSEQ)])


def sds(shape, dtype=jnp.bfloat16):
    return jax.ShapeDtypeStruct(shape, dtype)


def cost(flops, read):
    return pl.CostEstimate(flops=flops, bytes_accessed=read, transcendentals=0)


def layer(
    tokens,
    in_gain,
    w_proj,
    out_gain,
    w_out,
    rab_slope,
    hist_blocks,
    hist_tail,
    node_table,
    subtree_map,
    beam_nodes,
):
    x_rows = tokens[0]
    seq = lax.axis_index("seq")
    mine = head_of(seq)

    gate, extra, *sent = pl.pallas_call(
        project_kernel,
        in_specs=[smem(), smem(), vmem(), vmem(), pl.BlockSpec(memory_space=pltpu.HBM)],
        out_specs=[vmem()] * (2 + HEADS),
        out_shape=[pltpu.HBM((BLK, D), jnp.bfloat16), sds((16, HD))] + [sds((ROWS_A, HD))] * HEADS,
        scratch_shapes=[pltpu.VMEM((HEADS, D, 4 * HD), jnp.bfloat16), pltpu.SemaphoreType.DMA((HEADS, 4))],
        name="project",
        cost_estimate=cost(2 * BLK * D * 4 * D, 10 << 20),
        compiler_params=GRANT,
    )(*(in_hbm(value) for value in (hist_blocks, hist_tail, x_rows, in_gain[None, :], w_proj)))
    far_got, near_got = [], [sent[4]]
    for q, value in zip(FAR, sent[:4]):
        far_got.append(seq_xor(value, spread(q)))
    for q, value in zip(NEAR[1:], sent[5:]):
        near_got.append(seq_xor(value, spread(q)))

    bias, pairs, places = pl.pallas_call(
        prepare_kernel,
        in_specs=[smem(), smem(), vmem(), vmem()],
        out_specs=[vmem(), smem(), vmem()],
        out_shape=[
            sds((MAXD, BLK, BLK), jnp.float32),
            sds((2 * LIST,), jnp.int32),
            sds((8, 64), jnp.int32),
        ],
        name="prepare",
        cost_estimate=cost(1 << 28, 4 << 20),
        compiler_params=GRANT,
    )(hist_blocks, rab_slope, beam_nodes, subtree_map[None, :])

    def sort(got):
        return pl.pallas_call(
            sort_kernel,
            in_specs=[vmem()] * 4,
            out_specs=[vmem()] * 2,
            out_shape=[sds((4, ROW_Q, HD)), sds((4, BLK, HD))],
            cost_estimate=cost(1 << 10, 1 << 19),
            compiler_params=GRANT,
        )(*got)

    near_kv, near_q = sort(near_got)
    near_cross = seq_xor(near_kv, 4)
    far_kv, far_q = sort(far_got)
    far_cross = seq_xor(far_kv, 4)

    own = lax.dynamic_slice_in_dim(node_table, mine * 32, 32, 0)
    pair = jnp.concatenate([own, dp_shift(own, lambda i: i ^ 2)], axis=0)
    quad = jnp.concatenate([pair, dp_shift(pair, lambda i: i ^ 1)], axis=0)
    table = [quad]
    for n in (1, 2, 3):
        table.append(dp_shift(quad, lambda i, n=n: (i + 4 * n) % 16))

    part, queries = pl.pallas_call(
        attend_first_kernel,
        in_specs=[smem()] + [vmem()] * 6,
        out_specs=[vmem(), vmem()],
        out_shape=[sds((8, BLK, HD), jnp.float32), sds((8, BLK, HD))],
        scratch_shapes=[pltpu.VMEM((12, ROW_Q, HD), jnp.bfloat16), pltpu.VMEM((9, BLK, HD), jnp.float32)],
        name="attend_first",
        cost_estimate=cost(1 << 31, 4 << 20),
        compiler_params=GRANT,
    )(pairs, bias, near_kv, far_kv, near_cross, near_q, far_q)

    back = pl.pallas_call(
        attend_last_kernel,
        in_specs=[smem()] * 3 + [vmem()] * 5,
        out_specs=vmem(),
        out_shape=sds((8, ROWS_B, HD)),
        scratch_shapes=[pltpu.VMEM((9, BLK, HD), jnp.float32)],
        name="attend_last",
        cost_estimate=cost(1 << 30, 2 << 20),
        compiler_params=GRANT,
    )(hist_blocks, hist_tail, pairs, bias, queries, far_cross, part, extra)

    mixed = lax.all_to_all(back, "seq", 0, 0, tiled=True, axis_index_groups=SETS)

    sent = pl.pallas_call(
        state_kernel,
        in_specs=[smem()] + [vmem()] * 3 + [pl.BlockSpec(memory_space=pltpu.HBM)] * 4,
        out_specs=vmem(),
        out_shape=pltpu.HBM((NSEQ, 16, 128), jnp.float32),
        scratch_shapes=[pltpu.VMEM((4, BLK, D), jnp.bfloat16), pltpu.SemaphoreType.DMA((4,))],
        name="state",
        cost_estimate=cost(2 * 16 * D * D, 3 << 20),
        compiler_params=GRANT,
    )(hist_blocks, mixed, out_gain[None, :], w_out, *(in_hbm(piece) for piece in table))
    scores = lax.all_to_all(sent, "seq", 0, 0, tiled=True)

    layer_rows = pl.pallas_call(
        layer_kernel,
        in_specs=[vmem()] * 5,
        out_specs=vmem(),
        out_shape=sds((BLK, D)),
        name="layer",
        cost_estimate=cost(2 * BLK * D * D, 3 << 20),
        compiler_params=GRANT,
    )(mixed, gate, x_rows, out_gain[None, :], w_out)

    beam_scores = pl.pallas_call(
        pick_kernel,
        in_specs=[vmem()] * 2,
        out_specs=vmem(),
        out_shape=sds((USERS, 64), jnp.float32),
        name="pick",
        cost_estimate=cost(1 << 20, 1 << 17),
        compiler_params=GRANT,
    )(scores, places)
    return (layer_rows[None], beam_scores)


def solution(mesh):
    placed = (
        P("dp", "seq", None),
        P(),
        P(),
        P(),
        P(),
        P(),
        P("dp", None),
        P("dp", None),
        P("dp", None),
        P(),
        P("dp", "seq"),
    )
    return jax.shard_map(
        layer,
        mesh=mesh,
        in_specs=placed,
        out_specs=(P("dp", "seq", None), P("dp", "seq")),
        check_vma=False,
    )
```

profile of v0, /device:TPU:0, one launch (start us, length us, event | category | flops | bytes accessed | tf_op | source)
XLA Modules:
  0.0 98.1 jit_solution(7108018047788819912)
XLA Ops:
  0.6 0.0 copy-start
  0.7 6.5 %project.1 = (bf16[128,1024]{1,0:T(8,128)(2,1)}, bf16[16,128]{1,0:T(8,128)(2,1)S(1)}, bf16[384,128]{1,0:T(8,128)(2,1)}, bf16[384,128]{1,0:T(8,128)(2,1)S(1)}, bf...) custom-call(s32[1,3]{1,0:T(1,128)} %blocks_ref.7, ...), custom_call_target="tpu_custom_call" | custom-call | flops 1073741824 | bytes 10485760 | tf_op jit(solution)/shard_map/project/pallas_call | solution.py:338
  7.2 0.0 copy-start.1
  7.2 0.0 copy-start.4
  7.2 0.3 collective-permute-start
  7.5 3.2 %collective-permute-start.1 = (bf16[384,128]{1,0:T(8,128)(2,1)S(1)}, bf16[384,128]{1,0:T(8,128)(2,1)S(1)}, u32[]{:S(2)}, u32[]{:S(2)}) collective-permute-start(bf16[384,128]{1,0:T(8,128)(2,1)S(1)} %get-tuple-element.25), channel_id=1, source_target_pairs={{0,8},{1,9},{2,10},{3,11},{4,12},{5,13},{6,14},{7,15},{8,0},{9,1},... | collective-permute-start | bytes 294920 | tf_op jit(solution)/shard_map/ppermute | solution.py:310
  10.7 1.6 %collective-permute-start.2 = (bf16[384,128]{1,0:T(8,128)(2,1)S(1)}, bf16[384,128]{1,0:T(8,128)(2,1)S(1)}, u32[]{:S(2)}, u32[]{:S(2)}) collective-permute-start(bf16[384,128]{1,0:T(8,128)(2,1)S(1)} %get-tuple-element.26), channel_id=1, source_target_pairs={{0,9},{1,8},{2,11},{3,10},{4,13},{5,12},{6,15},{7,14},{8,1},{9,0},... | collective-permute-start | bytes 294920 | tf_op jit(solution)/shard_map/ppermute | solution.py:310
  12.3 0.0 collective-permute-done.refs_1_
  12.3 2.3 %collective-permute-done.1.refs_2_ = bf16[384,128]{1,0:T(8,128)(2,1)S(1)} collective-permute-done((bf16[384,128]{1,0:T(8,128)(2,1)S(1)}, bf16[384,128]{1,0:T(8,128)(2,1)S(1)}, u32[]{:S(2)}, u32[]{:S(2)}) %collective-permute-start.1) | collective-permute-done | bytes 98336 | tf_op jit(solution)/shard_map/ppermute | solution.py:310
  14.6 3.1 %collective-permute-done.2.refs_3_ = bf16[384,128]{1,0:T(8,128)(2,1)S(1)} collective-permute-done((bf16[384,128]{1,0:T(8,128)(2,1)S(1)}, bf16[384,128]{1,0:T(8,128)(2,1)S(1)}, u32[]{:S(2)}, u32[]{:S(2)}) %collective-permute-start.2) | collective-permute-done | bytes 98336 | tf_op jit(solution)/shard_map/ppermute | solution.py:310
  17.7 0.7 shard_map.122
  18.4 0.7 collective-permute-start.7
  19.1 3.3 %collective-permute-start.3 = (bf16[384,128]{1,0:T(8,128)(2,1)}, bf16[384,128]{1,0:T(8,128)(2,1)S(1)}, u32[]{:S(2)}, u32[]{:S(2)}) collective-permute-start(bf16[384,128]{1,0:T(8,128)(2,1)} %get-tuple-element.28), channel_id=1, source_target_pairs={{0,2},{1,3},{2,0},{3,1},{4,6},{5,7},{6,4},{7,5},{8,10},{9,11},{10,... | collective-permute-start | bytes 294920 | tf_op jit(solution)/shard_map/ppermute | solution.py:310
  22.4 0.0 collective-permute-start.4
  22.4 2.8 %collective-permute-start.5 = (bf16[384,128]{1,0:T(8,128)(2,1)S(1)}, bf16[384,128]{1,0:T(8,128)(2,1)S(1)}, u32[]{:S(2)}, u32[]{:S(2)}) collective-permute-start(bf16[384,128]{1,0:T(8,128)(2,1)S(1)} %get-tuple-element.30), channel_id=1, source_target_pairs={{0,10},{1,11},{2,8},{3,9},{4,14},{5,15},{6,12},{7,13},{8,2},{9,3},... | collective-permute-start | bytes 294920 | tf_op jit(solution)/shard_map/ppermute | solution.py:310
  25.2 2.5 %collective-permute-start.6 = (bf16[384,128]{1,0:T(8,128)(2,1)S(1)}, bf16[384,128]{1,0:T(8,128)(2,1)S(1)}, u32[]{:S(2)}, u32[]{:S(2)}) collective-permute-start(bf16[384,128]{1,0:T(8,128)(2,1)S(1)} %get-tuple-element.31), channel_id=1, source_target_pairs={{0,11},{1,10},{2,9},{3,8},{4,15},{5,14},{6,13},{7,12},{8,3},{9,2},... | collective-permute-start | bytes 294920 | tf_op jit(solution)/shard_map/ppermute | solution.py:310
  27.7 5.5 %collective-permute-done.3.refs_0_ = bf16[384,128]{1,0:T(8,128)(2,1)S(1)} collective-permute-done((bf16[384,128]{1,0:T(8,128)(2,1)}, bf16[384,128]{1,0:T(8,128)(2,1)S(1)}, u32[]{:S(2)}, u32[]{:S(2)}) %collective-permute-start.3) | collective-permute-done | bytes 98336 | tf_op jit(solution)/shard_map/ppermute | solution.py:310
  33.2 0.0 collective-permute-done.4.refs_1_
  33.2 5.0 %collective-permute-done.5.refs_2_ = bf16[384,128]{1,0:T(8,128)(2,1)S(1)} collective-permute-done((bf16[384,128]{1,0:T(8,128)(2,1)S(1)}, bf16[384,128]{1,0:T(8,128)(2,1)S(1)}, u32[]{:S(2)}, u32[]{:S(2)}) %collective-permute-start.5) | collective-permute-done | bytes 98336 | tf_op jit(solution)/shard_map/ppermute | solution.py:310
  38.3 0.0 collective-permute-done.6.refs_3_
  38.3 0.1 collective-permute-start.8
  38.4 5.8 %collective-permute-start.9 = (bf16[32,1024]{1,0:T(8,128)(2,1)S(1)}, bf16[32,1024]{1,0:T(8,128)(2,1)S(1)}, u32[]{:S(2)}, u32[]{:S(2)}) collective-permute-start(bf16[32,1024]{1,0:T(8,128)(2,1)S(1)} %constant_dynamic-slice_fusion), channel_id=1, source_target_pairs={{0,32},{16,48},{32,0},{48,16},{64,96},{80,112},{96,64},{112,80},{1... | collective-permute-start | bytes 196616 | tf_op jit(solution)/shard_map/ppermute | solution.py:306
  44.2 0.0 copy-done.5
  44.2 3.2 %prepare.1 = (f32[10,128,128]{2,1,0:T(8,128)S(1)}, s32[256]{0:T(256)S(1)}, s32[8,64]{1,0:T(8,128)S(1)}) custom-call(s32[1,3]{1,0:T(1,128)S(1)} %copy-done.5, f32[8]{0:T(128)S(1)} %copy-done.8, s32[3,64]{1,0:T(4,128)S(1)} %copy-done.7, s32[1,64]{1,0:T(1,128)S(1)} %bitcast.9), custom_call_target="tpu_custom_call" | custom-call | flops 268435456 | bytes 4194304 | tf_op jit(solution)/shard_map/prepare/pallas_call | solution.py:354
  47.4 0.0 collective-permute-done.7.cross_ref
  47.4 0.0 copy-start.2
  47.4 3.6 %attend_first.1 = (f32[8,128,128]{2,1,0:T(8,128)S(1)}, bf16[8,128,128]{2,1,0:T(8,128)(2,1)S(1)}) custom-call(s32[256]{0:T(256)S(1)} %get-tuple-element.21.list_ref, f32[10,128,128]{2,1,0:T(8,128)S(1)} %get-tuple-element.22.bias_ref, bf16[4,256,128]{2,1,0:T(8,128)(2,1)} %get-tuple-element.27.near_ref, bf16[4,256,128]{2,1,0:T(8,128)(2,1)S(1)} %get-tuple-element.32.far_ref, ...), custom_call_target="tpu_custom_call" | custom-call | flops 2147483648 | bytes 4194304 | tf_op jit(solution)/shard_map/attend_first/pallas_call | solution.py:390
  51.0 0.0 collective-permute-done.8.cross_ref
  51.1 1.9 %attend_last.1 = bf16[8,160,128]{2,1,0:T(8,128)(2,1)} custom-call(s32[1,3]{1,0:T(1,128)S(1)} %copy-done.5, s32[1,3]{1,0:T(1,128)S(1)} %copy-done.6, s32[256]{0:T(256)S(1)} %get-tuple-element.21.list_ref, f32[10,128,128]{2,1,0:T(8,128)S(1)} %get-tuple-element.22.bias_ref, bf16[8,128,128]{2,1,0:T(8,128)(2,1)S(1)} %get-tuple-element.35.queries_ref, ...), custom_call_target="tpu_custom_call" | custom-call | flops 1073741824 | bytes 2097152 | tf_op jit(solution)/shard_map/attend_last/pallas_call | solution.py:401
  53.0 6.4 %all-to-all-start = ((bf16[8,160,128]{2,1,0:T(8,128)(2,1)}), bf16[8,160,128]{2,1,0:T(8,128)(2,1)S(1)}, u32[]{:S(2)}, u32[]{:S(2)}) async-start(bf16[8,160,128]{2,1,0:T(8,128)(2,1)} %attend_last.1), calls=%async_computation | async-start | bytes 655360 | tf_op jit(solution)/shard_map/all_to_all | solution.py:412
  59.4 0.0 collective-permute-done.9
  59.4 0.1 collective-permute-start.10
  59.5 1.3 %collective-permute-done.10 = bf16[64,1024]{1,0:T(8,128)(2,1)S(1)} collective-permute-done((bf16[64,1024]{1,0:T(8,128)(2,1)S(1)}, bf16[64,1024]{1,0:T(8,128)(2,1)S(1)}, u32[]{:S(2)}, u32[]{:S(2)}) %collective-permute-start.10) | collective-permute-done | bytes 131104 | tf_op jit(solution)/shard_map/ppermute | solution.py:306
  60.9 1.0 %collective-permute-start.11 = (bf16[128,1024]{1,0:T(8,128)(2,1)S(1)}, bf16[128,1024]{1,0:T(8,128)(2,1)S(1)}, u32[]{:S(2)}, u32[]{:S(2)}) collective-permute-start(bf16[128,1024]{1,0:T(8,128)(2,1)S(1)} %pad_maximum_fusion.ta_ref), channel_id=1, source_target_pairs={{0,64},{16,80},{32,96},{48,112},{64,128},{80,144},{96,160},{112,17... | collective-permute-start | bytes 786440 | tf_op jit(solution)/shard_map/ppermute | solution.py:306
  61.9 3.2 %collective-permute-start.12 = (bf16[128,1024]{1,0:T(8,128)(2,1)S(1)}, bf16[128,1024]{1,0:T(8,128)(2,1)S(1)}, u32[]{:S(2)}, u32[]{:S(2)}) collective-permute-start(bf16[128,1024]{1,0:T(8,128)(2,1)S(1)} %pad_maximum_fusion.ta_ref), channel_id=1, source_target_pairs={{0,128},{16,144},{32,160},{48,176},{64,192},{80,208},{96,224},{112... | collective-permute-start | bytes 786440 | tf_op jit(solution)/shard_map/ppermute | solution.py:306
  65.1 0.8 collective-permute-start.13
  65.9 4.6 %collective-permute-done.11.tb_ref = bf16[128,1024]{1,0:T(8,128)(2,1)S(1)} collective-permute-done((bf16[128,1024]{1,0:T(8,128)(2,1)S(1)}, bf16[128,1024]{1,0:T(8,128)(2,1)S(1)}, u32[]{:S(2)}, u32[]{:S(2)}) %collective-permute-start.11) | collective-permute-done | bytes 262176 | tf_op jit(solution)/shard_map/ppermute | solution.py:306
  70.5 6.5 %collective-permute-done.12.tc_ref = bf16[128,1024]{1,0:T(8,128)(2,1)S(1)} collective-permute-done((bf16[128,1024]{1,0:T(8,128)(2,1)S(1)}, bf16[128,1024]{1,0:T(8,128)(2,1)S(1)}, u32[]{:S(2)}, u32[]{:S(2)}) %collective-permute-start.12) | collective-permute-done | bytes 262176 | tf_op jit(solution)/shard_map/ppermute | solution.py:306
  77.1 0.7 copy-done.12
  77.8 0.0 collective-permute-done.13.td_ref
  77.8 0.0 all-to-all-done.mixed_ref
  77.8 3.2 %state.1 = f32[16,16,128]{2,1,0:T(8,128)} custom-call(s32[1,3]{1,0:T(1,128)S(1)} %copy-done.5, bf16[8,160,128]{2,1,0:T(8,128)(2,1)S(1)} %all-to-all-done.mixed_ref, f32[1,1024]{1,0:T(1,128)S(1)} %bitcast.7, bf16[1024,1024]{1,0:T(8,128)(2,1)S(1)} %copy-done.1, bf16[128,1024]{1,0:T(8,128)(2,1)} %copy-done.10, bf16[128,1024]{1,0:T(8,128)(2,1)} %copy-done.11, ...), custom_call_target="tpu_custom_call" | custom-call | flops 33554432 | bytes 3145728 | tf_op jit(solution)/shard_map/state/pallas_call | solution.py:414
  81.0 7.6 %all-to-all-start.1 = ((f32[16,16,128]{2,1,0:T(8,128)}), f32[16,16,128]{2,1,0:T(8,128)S(1)}, u32[]{:S(2)}, u32[]{:S(2)}) async-start(f32[16,16,128]{2,1,0:T(8,128)} %state.1), calls=%async_computation.1 | async-start | bytes 262144 | tf_op jit(solution)/shard_map/all_to_all | solution.py:424
  88.6 0.0 copy-start.3
  88.6 0.9 copy-done.3
  89.6 1.3 %layer.1 = bf16[128,1024]{1,0:T(8,128)(2,1)} custom-call(bf16[8,160,128]{2,1,0:T(8,128)(2,1)S(1)} %all-to-all-done.mixed_ref, bf16[128,1024]{1,0:T(8,128)(2,1)S(1)} %copy-done.3, bf16[128,1024]{1,0:T(8,128)(2,1)S(1)} %bitcast.6, f32[1,1024]{1,0:T(1,128)S(1)} %bitcast.8, bf16[1024,1024]{1,0:T(8,128)(2,1)S(1)} %copy-done.1), custom_call_target="tpu_custom_call" | custom-call | flops 268435456 | bytes 3145728 | tf_op jit(solution)/shard_map/layer/pallas_call | solution.py:426
  90.9 6.1 %all-to-all-done.1.score_ref = f32[16,16,128]{2,1,0:T(8,128)S(1)} async-done(((f32[16,16,128]{2,1,0:T(8,128)}), f32[16,16,128]{2,1,0:T(8,128)S(1)}, u32[]{:S(2)}, u32[]{:S(2)}) %all-to-all-start.1) | async-done | bytes 131104 | tf_op jit(solution)/shard_map/all_to_all | solution.py:424
  97.0 1.1 %pick.1 = f32[3,64]{1,0:T(4,128)} custom-call(f32[16,16,128]{2,1,0:T(8,128)S(1)} %all-to-all-done.1.score_ref, s32[8,64]{1,0:T(8,128)S(1)} %get-tuple-element.39.place_ref), custom_call_target="tpu_custom_call" | custom-call | flops 1048576 | bytes 131072 | tf_op jit(solution)/shard_map/pick/pallas_call | solution.py:436
  (22 shorter events, 0.1 us)
Async XLA Ops:
  0.6 37.8 %copy-start = (bf16[256,1024]{1,0:T(8,128)(2,1)S(1)}, bf16[256,1024]{1,0:T(8,128)(2,1)}, u32[]{:S(2)}) copy-start(bf16[256,1024]{1,0:T(8,128)(2,1)} %param.19) | copy-start | bytes 1572868
  0.6 43.6 %copy-start.5 = (s32[1,3]{1,0:T(1,128)S(1)}, s32[1,3]{1,0:T(1,128)}, u32[]{:S(2)}) copy-start(s32[1,3]{1,0:T(1,128)} %blocks_ref.7) | copy-start | bytes 40
  0.7 43.6 %copy-start.9 = (s32[64]{0:T(128)S(1)}, s32[64]{0:T(128)}, u32[]{:S(2)}) copy-start(s32[64]{0:T(128)} %param.20) | copy-start | bytes 772
  0.7 43.6 %copy-start.8 = (f32[8]{0:T(128)S(1)}, f32[8]{0:T(128)}, u32[]{:S(2)}) copy-start(f32[8]{0:T(128)} %slope_ref.1) | copy-start | bytes 100
  0.7 43.6 %copy-start.7 = (s32[3,64]{1,0:T(4,128)S(1)}, s32[3,64]{1,0:T(4,128)}, u32[]{:S(2)}) copy-start(s32[3,64]{1,0:T(4,128)} %ids_ref.1) | copy-start | bytes 2308
  0.7 50.4 %copy-start.6 = (s32[1,3]{1,0:T(1,128)S(1)}, s32[1,3]{1,0:T(1,128)}, u32[]{:S(2)}) copy-start(s32[1,3]{1,0:T(1,128)} %tail_ref.3) | copy-start | bytes 40
  7.2 70.6 %copy-start.1 = (bf16[1024,1024]{1,0:T(8,128)(2,1)S(1)}, bf16[1024,1024]{1,0:T(8,128)(2,1)}, u32[]{:S(2)}) copy-start(bf16[1024,1024]{1,0:T(8,128)(2,1)} %w_ref.5) | copy-start | bytes 6291460
  7.2 70.6 %copy-start.4 = (f32[1024]{0:T(1024)S(1)}, f32[1024]{0:T(1024)}, u32[]{:S(2)}) copy-start(f32[1024]{0:T(1024)} %param.14) | copy-start | bytes 12292
  7.2 5.1 %collective-permute-start = (bf16[384,128]{1,0:T(8,128)(2,1)S(1)}, bf16[384,128]{1,0:T(8,128)(2,1)S(1)}, u32[]{:S(2)}, u32[]{:S(2)}) collective-permute-start(bf16[384,128]{1,0:T(8,128)(2,1)S(1)} %get-tuple-element.24), channel_id=1, source_target_pairs={{0,1},{1,0},{2,3},{3,2},{4,5},{5,4},{6,7},{7,6},{8,9},{9,8},{10,11... | collective-permute-start | bytes 294920 | tf_op jit(solution)/shard_map/ppermute | solution.py:310
  7.5 7.1 %collective-permute-start.1 = (bf16[384,128]{1,0:T(8,128)(2,1)S(1)}, bf16[384,128]{1,0:T(8,128)(2,1)S(1)}, u32[]{:S(2)}, u32[]{:S(2)}) collective-permute-start(bf16[384,128]{1,0:T(8,128)(2,1)S(1)} %get-tuple-element.25), channel_id=1, source_target_pairs={{0,8},{1,9},{2,10},{3,11},{4,12},{5,13},{6,14},{7,15},{8,0},{9,1},... | collective-permute-start | bytes 294920 | tf_op jit(solution)/shard_map/ppermute | solution.py:310
  10.7 7.0 %collective-permute-start.2 = (bf16[384,128]{1,0:T(8,128)(2,1)S(1)}, bf16[384,128]{1,0:T(8,128)(2,1)S(1)}, u32[]{:S(2)}, u32[]{:S(2)}) collective-permute-start(bf16[384,128]{1,0:T(8,128)(2,1)S(1)} %get-tuple-element.26), channel_id=1, source_target_pairs={{0,9},{1,8},{2,11},{3,10},{4,13},{5,12},{6,15},{7,14},{8,1},{9,0},... | collective-permute-start | bytes 294920 | tf_op jit(solution)/shard_map/ppermute | solution.py:310
  18.4 29.0 %collective-permute-start.7 = (bf16[4,256,128]{2,1,0:T(8,128)(2,1)}, bf16[4,256,128]{2,1,0:T(8,128)(2,1)}, u32[]{:S(2)}, u32[]{:S(2)}) collective-permute-start(bf16[4,256,128]{2,1,0:T(8,128)(2,1)} %get-tuple-element.27.near_ref), channel_id=1, source_target_pairs={{0,4},{1,5},{2,6},{3,7},{4,0},{5,1},{6,2},{7,3},{8,12},{9,13},{10,... | collective-permute-start | bytes 786440 | tf_op jit(solution)/shard_map/ppermute | solution.py:310
  19.1 14.1 %collective-permute-start.3 = (bf16[384,128]{1,0:T(8,128)(2,1)}, bf16[384,128]{1,0:T(8,128)(2,1)S(1)}, u32[]{:S(2)}, u32[]{:S(2)}) collective-permute-start(bf16[384,128]{1,0:T(8,128)(2,1)} %get-tuple-element.28), channel_id=1, source_target_pairs={{0,2},{1,3},{2,0},{3,1},{4,6},{5,7},{6,4},{7,5},{8,10},{9,11},{10,... | collective-permute-start | bytes 294920 | tf_op jit(solution)/shard_map/ppermute | solution.py:310
  22.4 10.9 %collective-permute-start.4 = (bf16[384,128]{1,0:T(8,128)(2,1)S(1)}, bf16[384,128]{1,0:T(8,128)(2,1)S(1)}, u32[]{:S(2)}, u32[]{:S(2)}) collective-permute-start(bf16[384,128]{1,0:T(8,128)(2,1)S(1)} %get-tuple-element.29), channel_id=1, source_target_pairs={{0,3},{1,2},{2,1},{3,0},{4,7},{5,6},{6,5},{7,4},{8,11},{9,10},{10,... | collective-permute-start | bytes 294920 | tf_op jit(solution)/shard_map/ppermute | solution.py:310
  22.4 15.9 %collective-permute-start.5 = (bf16[384,128]{1,0:T(8,128)(2,1)S(1)}, bf16[384,128]{1,0:T(8,128)(2,1)S(1)}, u32[]{:S(2)}, u32[]{:S(2)}) collective-permute-start(bf16[384,128]{1,0:T(8,128)(2,1)S(1)} %get-tuple-element.30), channel_id=1, source_target_pairs={{0,10},{1,11},{2,8},{3,9},{4,14},{5,15},{6,12},{7,13},{8,2},{9,3},... | collective-permute-start | bytes 294920 | tf_op jit(solution)/shard_map/ppermute | solution.py:310
  25.2 13.1 %collective-permute-start.6 = (bf16[384,128]{1,0:T(8,128)(2,1)S(1)}, bf16[384,128]{1,0:T(8,128)(2,1)S(1)}, u32[]{:S(2)}, u32[]{:S(2)}) collective-permute-start(bf16[384,128]{1,0:T(8,128)(2,1)S(1)} %get-tuple-element.31), channel_id=1, source_target_pairs={{0,11},{1,10},{2,9},{3,8},{4,15},{5,14},{6,13},{7,12},{8,3},{9,2},... | collective-permute-start | bytes 294920 | tf_op jit(solution)/shard_map/ppermute | solution.py:310
  38.3 12.7 %collective-permute-start.8 = (bf16[4,256,128]{2,1,0:T(8,128)(2,1)S(1)}, bf16[4,256,128]{2,1,0:T(8,128)(2,1)S(1)}, u32[]{:S(2)}, u32[]{:S(2)}) collective-permute-start(bf16[4,256,128]{2,1,0:T(8,128)(2,1)S(1)} %get-tuple-element.32.far_ref), channel_id=1, source_target_pairs={{0,4},{1,5},{2,6},{3,7},{4,0},{5,1},{6,2},{7,3},{8,12},{9,13},{10,... | collective-permute-start | bytes 786440 | tf_op jit(solution)/shard_map/ppermute | solution.py:310
  38.4 21.0 %collective-permute-start.9 = (bf16[32,1024]{1,0:T(8,128)(2,1)S(1)}, bf16[32,1024]{1,0:T(8,128)(2,1)S(1)}, u32[]{:S(2)}, u32[]{:S(2)}) collective-permute-start(bf16[32,1024]{1,0:T(8,128)(2,1)S(1)} %constant_dynamic-slice_fusion), channel_id=1, source_target_pairs={{0,32},{16,48},{32,0},{48,16},{64,96},{80,112},{96,64},{112,80},{1... | collective-permute-start | bytes 196616 | tf_op jit(solution)/shard_map/ppermute | solution.py:306
  47.4 41.2 %copy-start.2 = (bf16[1,128,1024]{2,1,0:T(8,128)(2,1)S(1)}, bf16[1,128,1024]{2,1,0:T(8,128)(2,1)}, u32[]{:S(2)}) copy-start(bf16[1,128,1024]{2,1,0:T(8,128)(2,1)} %param.11) | copy-start | bytes 786436
  53.0 24.8 %all-to-all-start = ((bf16[8,160,128]{2,1,0:T(8,128)(2,1)}), bf16[8,160,128]{2,1,0:T(8,128)(2,1)S(1)}, u32[]{:S(2)}, u32[]{:S(2)}) async-start(bf16[8,160,128]{2,1,0:T(8,128)(2,1)} %attend_last.1), calls=%async_computation | async-start | bytes 655360 | tf_op jit(solution)/shard_map/all_to_all | solution.py:412
  59.4 1.4 %collective-permute-start.10 = (bf16[64,1024]{1,0:T(8,128)(2,1)S(1)}, bf16[64,1024]{1,0:T(8,128)(2,1)S(1)}, u32[]{:S(2)}, u32[]{:S(2)}) collective-permute-start(bf16[64,1024]{1,0:T(8,128)(2,1)S(1)} %pad_maximum_fusion.1), channel_id=1, source_target_pairs={{0,16},{16,0},{32,48},{48,32},{64,80},{80,64},{96,112},{112,96},{1... | collective-permute-start | bytes 393224 | tf_op jit(solution)/shard_map/ppermute | solution.py:306
  60.9 16.2 %copy-start.10 = (bf16[128,1024]{1,0:T(8,128)(2,1)}, bf16[128,1024]{1,0:T(8,128)(2,1)S(1)}, u32[]{:S(2)}) copy-start(bf16[128,1024]{1,0:T(8,128)(2,1)S(1)} %pad_maximum_fusion.ta_ref) | copy-start | bytes 786436
  60.9 9.6 %collective-permute-start.11 = (bf16[128,1024]{1,0:T(8,128)(2,1)S(1)}, bf16[128,1024]{1,0:T(8,128)(2,1)S(1)}, u32[]{:S(2)}, u32[]{:S(2)}) collective-permute-start(bf16[128,1024]{1,0:T(8,128)(2,1)S(1)} %pad_maximum_fusion.ta_ref), channel_id=1, source_target_pairs={{0,64},{16,80},{32,96},{48,112},{64,128},{80,144},{96,160},{112,17... | collective-permute-start | bytes 786440 | tf_op jit(solution)/shard_map/ppermute | solution.py:306
  61.9 15.2 %collective-permute-start.12 = (bf16[128,1024]{1,0:T(8,128)(2,1)S(1)}, bf16[128,1024]{1,0:T(8,128)(2,1)S(1)}, u32[]{:S(2)}, u32[]{:S(2)}) collective-permute-start(bf16[128,1024]{1,0:T(8,128)(2,1)S(1)} %pad_maximum_fusion.ta_ref), channel_id=1, source_target_pairs={{0,128},{16,144},{32,160},{48,176},{64,192},{80,208},{96,224},{112... | collective-permute-start | bytes 786440 | tf_op jit(solution)/shard_map/ppermute | solution.py:306
  65.1 12.7 %collective-permute-start.13 = (bf16[128,1024]{1,0:T(8,128)(2,1)S(1)}, bf16[128,1024]{1,0:T(8,128)(2,1)}, u32[]{:S(2)}, u32[]{:S(2)}) collective-permute-start(bf16[128,1024]{1,0:T(8,128)(2,1)S(1)} %pad_maximum_fusion.ta_ref), channel_id=1, source_target_pairs={{0,192},{16,208},{32,224},{48,240},{64,0},{80,16},{96,32},{112,48}... | collective-permute-start | bytes 786440 | tf_op jit(solution)/shard_map/ppermute | solution.py:306
  70.5 6.6 %copy-start.11 = (bf16[128,1024]{1,0:T(8,128)(2,1)}, bf16[128,1024]{1,0:T(8,128)(2,1)S(1)}, u32[]{:S(2)}) copy-start(bf16[128,1024]{1,0:T(8,128)(2,1)S(1)} %collective-permute-done.11.tb_ref) | copy-start | bytes 786436
  77.1 0.7 copy-start.12
  81.0 16.0 %all-to-all-start.1 = ((f32[16,16,128]{2,1,0:T(8,128)}), f32[16,16,128]{2,1,0:T(8,128)S(1)}, u32[]{:S(2)}, u32[]{:S(2)}) async-start(f32[16,16,128]{2,1,0:T(8,128)} %state.1), calls=%async_computation.1 | async-start | bytes 262144 | tf_op jit(solution)/shard_map/all_to_all | solution.py:424
  88.6 1.0 copy-start.3
where the time goes:
time: 99.4 us; the launch traced here: 98.1 us
  starting transfers between devices  39.4 us (40%)
  waiting for transfers between devices  34.6 us (35%)
  Pallas kernels  21.5 us (22%)
  local copies, waits for them, and re-layouts  1.71 us (2%)
    ppermute x9, waiting for transfers between devices, seq_xor(): return lax.ppermute(value, 'seq', [(i, i ^ apart) for i in range(NSEQ)])  16 us
    ppermute x9, starting transfers between devices, seq_xor(): return lax.ppermute(value, 'seq', [(i, i ^ apart) for i in range(NSEQ)])  14.5 us
    ppermute x5, waiting for transfers between devices, dp_shift(): return lax.ppermute(value, 'dp', [(i, move(i)) for i in range(16)])  12.5 us
    ppermute x5, starting transfers between devices, dp_shift(): return lax.ppermute(value, 'dp', [(i, move(i)) for i in range(16)])  10.9 us
    all_to_all x1, starting transfers between devices, layer(): scores = lax.all_to_all(sent, 'seq', 0, 0, tiled=True)  7.61 us
    pallas_call x1, Pallas kernels, layer(): pl.pallas_call(project_kernel, in_specs=[smem(), smem(), vmem(), vmem(),...  6.46 us
    all_to_all x1, starting transfers between devices, layer(): lax.all_to_all(back, 'seq', 0, 0, tiled=True, axis_index_groups=SETS)  6.43 us
    all_to_all x1, waiting for transfers between devices, layer(): scores = lax.all_to_all(sent, 'seq', 0, 0, tiled=True)  6.09 us
  transfers between devices with their start and end apart: 16, of which 8 were waited for; matrix products, arithmetic and copies ran while one was open for 0% of the time, Pallas kernels for 10%

commit v1 on v0

--- a/solution.py
+++ b/solution.py
@@ -237,12 +237,7 @@
         out_ref[t, ROW_X:ROWS_B, :] = extra_ref[...]
 
 
-def state_kernel(blocks_ref, mixed_ref, gain_ref, w_ref, ta_ref, tb_ref, tc_ref, td_ref, score_ref, table, sems):
-    copies = [
-        pltpu.make_async_copy(t_ref, table.at[x], sems.at[x]) for x, t_ref in enumerate((ta_ref, tb_ref, tc_ref, td_ref))
-    ]
-    for copy in copies:
-        copy.start()
+def state_kernel(blocks_ref, mixed_ref, gain_ref, w_ref, ta_ref, tb_ref, tc_ref, td_ref, score_ref):
     starts = user_starts(blocks_ref)
     tail = jnp.concatenate([mixed_ref[h, ROW_E:ROW_X, :].astype(jnp.float32) for h in range(HEADS)], axis=1)
     gates, tokens = [], []
@@ -256,10 +251,9 @@
     token_tail = jnp.concatenate(tokens + [zeros], axis=0)
     gated = (layer_norm(tail) * gain_ref[...] * gate_tail).astype(jnp.bfloat16)
     states = (token_tail + jnp.dot(gated, w_ref[...], preferred_element_type=jnp.float32)).astype(jnp.bfloat16)
-    for copy in copies:
-        copy.wait()
     parts = [
-        lax.dot_general(states, table[x], (((1,), (1,)), ((), ())), preferred_element_type=jnp.float32) for x in range(4)
+        lax.dot_general(states, t_ref[...], (((1,), (1,)), ((), ())), preferred_element_type=jnp.float32)
+        for t_ref in (ta_ref, tb_ref, tc_ref, td_ref)
     ]
     rows = [part[user : user + 1] for user in range(USERS) for part in parts]
     block = jnp.concatenate(rows + [jnp.zeros((4, 128), jnp.float32)], axis=0)
@@ -413,14 +407,13 @@
 
     sent = pl.pallas_call(
         state_kernel,
-        in_specs=[smem()] + [vmem()] * 3 + [pl.BlockSpec(memory_space=pltpu.HBM)] * 4,
+        in_specs=[smem()] + [vmem()] * 7,
         out_specs=vmem(),
         out_shape=pltpu.HBM((NSEQ, 16, 128), jnp.float32),
-        scratch_shapes=[pltpu.VMEM((4, BLK, D), jnp.bfloat16), pltpu.SemaphoreType.DMA((4,))],
         name="state",
         cost_estimate=cost(2 * 16 * D * D, 3 << 20),
         compiler_params=GRANT,
-    )(hist_blocks, mixed, out_gain[None, :], w_out, *(in_hbm(piece) for piece in table))
+    )(hist_blocks, mixed, out_gain[None, :], w_out, *table)
     scores = lax.all_to_all(sent, "seq", 0, 0, tiled=True)
 
     layer_rows = pl.pallas_call(

time: 99.4 us -> 103 us (1.036)
  local copies, waits for them, and re-layouts: 1.71 us -> 6.46 us
  waiting for transfers between devices: 34.6 us -> 33.4 us
  Pallas kernels: 21.5 us -> 20.3 us
    unnamed x26 -> x34, local copies, waits for them, and re-layouts: 1.7 us -> 6.44 us
    ppermute x5, waiting for transfers between devices: 12.5 us -> 11.3 us  [dp_shift(): return lax.ppermute(value, 'dp', [(i, move(i)) for i in range(16)])]
    pallas_call x1, Pallas kernels: 3.2 us -> 2.01 us  [layer(): pl.pallas_call(state_kernel, in_specs=[smem()] + [vmem()] * 7, out_specs=...]
  transfers between devices with their start and end apart: 16 -> 16, of which waited for: 8 -> 8; matrix products, arithmetic and copies ran while one was open for 0% -> 1% of each run, Pallas kernels for 10% -> 10%
where the time goes in v1:
time: 103 us; the launch traced here: 101 us
  starting transfers between devices  39.4 us (38%)
  waiting for transfers between devices  33.4 us (32%)
  Pallas kernels  20.3 us (20%)
  local copies, waits for them, and re-layouts  6.46 us (6%)
    ppermute x9, waiting for transfers between devices, seq_xor(): return lax.ppermute(value, 'seq', [(i, i ^ apart) for i in range(NSEQ)])  16 us
    ppermute x9, starting transfers between devices, seq_xor(): return lax.ppermute(value, 'seq', [(i, i ^ apart) for i in range(NSEQ)])  14.5 us
    ppermute x5, waiting for transfers between devices, dp_shift(): return lax.ppermute(value, 'dp', [(i, move(i)) for i in range(16)])  11.3 us
    ppermute x5, starting transfers between devices, dp_shift(): return lax.ppermute(value, 'dp', [(i, move(i)) for i in range(16)])  10.9 us
    all_to_all x1, starting transfers between devices, layer(): scores = lax.all_to_all(sent, 'seq', 0, 0, tiled=True)  7.6 us
    pallas_call x1, Pallas kernels, layer(): pl.pallas_call(project_kernel, in_specs=[smem(), smem(), vmem(), vmem(),...  6.46 us
    unnamed x34, local copies, waits for them, and re-layouts  6.44 us
    all_to_all x1, starting transfers between devices, layer(): lax.all_to_all(back, 'seq', 0, 0, tiled=True, axis_index_groups=SETS)  6.43 us
  transfers between devices with their start and end apart: 16, of which 8 were waited for; matrix products, arithmetic and copies ran while one was open for 1% of the time, Pallas kernels for 10%

profile of v1, /device:TPU:0, one launch (start us, length us, event | category | flops | bytes accessed | tf_op | source)
XLA Modules:
  0.0 101.3 jit_solution(10429774420495377427)
XLA Ops:
  0.6 0.0 copy-start
  0.7 6.5 %project.1 = (bf16[128,1024]{1,0:T(8,128)(2,1)}, bf16[16,128]{1,0:T(8,128)(2,1)S(1)}, bf16[384,128]{1,0:T(8,128)(2,1)}, bf16[384,128]{1,0:T(8,128)(2,1)S(1)}, bf...) custom-call(s32[1,3]{1,0:T(1,128)} %blocks_ref.7, ...), custom_call_target="tpu_custom_call" | custom-call | flops 1073741824 | bytes 10485760 | tf_op jit(solution)/shard_map/project/pallas_call | solution.py:332
  7.2 0.0 copy-start.1
  7.2 0.0 copy-start.10
  7.2 0.3 collective-permute-start
  7.5 3.2 %collective-permute-start.1 = (bf16[384,128]{1,0:T(8,128)(2,1)S(1)}, bf16[384,128]{1,0:T(8,128)(2,1)S(1)}, u32[]{:S(2)}, u32[]{:S(2)}) collective-permute-start(bf16[384,128]{1,0:T(8,128)(2,1)S(1)} %get-tuple-element.25), channel_id=1, source_target_pairs={{0,8},{1,9},{2,10},{3,11},{4,12},{5,13},{6,14},{7,15},{8,0},{9,1},... | collective-permute-start | bytes 294920 | tf_op jit(solution)/shard_map/ppermute | solution.py:304
  10.7 1.6 %collective-permute-start.2 = (bf16[384,128]{1,0:T(8,128)(2,1)S(1)}, bf16[384,128]{1,0:T(8,128)(2,1)S(1)}, u32[]{:S(2)}, u32[]{:S(2)}) collective-permute-start(bf16[384,128]{1,0:T(8,128)(2,1)S(1)} %get-tuple-element.26), channel_id=1, source_target_pairs={{0,9},{1,8},{2,11},{3,10},{4,13},{5,12},{6,15},{7,14},{8,1},{9,0},... | collective-permute-start | bytes 294920 | tf_op jit(solution)/shard_map/ppermute | solution.py:304
  12.3 2.3 %collective-permute-done.1.refs_2_ = bf16[384,128]{1,0:T(8,128)(2,1)S(1)} collective-permute-done((bf16[384,128]{1,0:T(8,128)(2,1)S(1)}, bf16[384,128]{1,0:T(8,128)(2,1)S(1)}, u32[]{:S(2)}, u32[]{:S(2)}) %collective-permute-start.1) | collective-permute-done | bytes 98336 | tf_op jit(solution)/shard_map/ppermute | solution.py:304
  14.6 3.1 %collective-permute-done.2.refs_3_ = bf16[384,128]{1,0:T(8,128)(2,1)S(1)} collective-permute-done((bf16[384,128]{1,0:T(8,128)(2,1)S(1)}, bf16[384,128]{1,0:T(8,128)(2,1)S(1)}, u32[]{:S(2)}, u32[]{:S(2)}) %collective-permute-start.2) | collective-permute-done | bytes 98336 | tf_op jit(solution)/shard_map/ppermute | solution.py:304
  17.7 0.7 shard_map.122
  18.4 0.7 collective-permute-start.7
  19.1 3.3 %collective-permute-start.3 = (bf16[384,128]{1,0:T(8,128)(2,1)}, bf16[384,128]{1,0:T(8,128)(2,1)S(1)}, u32[]{:S(2)}, u32[]{:S(2)}) collective-permute-start(bf16[384,128]{1,0:T(8,128)(2,1)} %get-tuple-element.28), channel_id=1, source_target_pairs={{0,2},{1,3},{2,0},{3,1},{4,6},{5,7},{6,4},{7,5},{8,10},{9,11},{10,... | collective-permute-start | bytes 294920 | tf_op jit(solution)/shard_map/ppermute | solution.py:304
  22.4 2.8 %collective-permute-start.5 = (bf16[384,128]{1,0:T(8,128)(2,1)S(1)}, bf16[384,128]{1,0:T(8,128)(2,1)S(1)}, u32[]{:S(2)}, u32[]{:S(2)}) collective-permute-start(bf16[384,128]{1,0:T(8,128)(2,1)S(1)} %get-tuple-element.30), channel_id=1, source_target_pairs={{0,10},{1,11},{2,8},{3,9},{4,14},{5,15},{6,12},{7,13},{8,2},{9,3},... | collective-permute-start | bytes 294920 | tf_op jit(solution)/shard_map/ppermute | solution.py:304
  25.2 2.5 %collective-permute-start.6 = (bf16[384,128]{1,0:T(8,128)(2,1)S(1)}, bf16[384,128]{1,0:T(8,128)(2,1)S(1)}, u32[]{:S(2)}, u32[]{:S(2)}) collective-permute-start(bf16[384,128]{1,0:T(8,128)(2,1)S(1)} %get-tuple-element.31), channel_id=1, source_target_pairs={{0,11},{1,10},{2,9},{3,8},{4,15},{5,14},{6,13},{7,12},{8,3},{9,2},... | collective-permute-start | bytes 294920 | tf_op jit(solution)/shard_map/ppermute | solution.py:304
  27.7 5.5 %collective-permute-done.3.refs_0_ = bf16[384,128]{1,0:T(8,128)(2,1)S(1)} collective-permute-done((bf16[384,128]{1,0:T(8,128)(2,1)}, bf16[384,128]{1,0:T(8,128)(2,1)S(1)}, u32[]{:S(2)}, u32[]{:S(2)}) %collective-permute-start.3) | collective-permute-done | bytes 98336 | tf_op jit(solution)/shard_map/ppermute | solution.py:304
  33.2 5.0 %collective-permute-done.5.refs_2_ = bf16[384,128]{1,0:T(8,128)(2,1)S(1)} collective-permute-done((bf16[384,128]{1,0:T(8,128)(2,1)S(1)}, bf16[384,128]{1,0:T(8,128)(2,1)S(1)}, u32[]{:S(2)}, u32[]{:S(2)}) %collective-permute-start.5) | collective-permute-done | bytes 98336 | tf_op jit(solution)/shard_map/ppermute | solution.py:304
  38.3 0.1 collective-permute-start.8
  38.4 5.8 %collective-permute-start.9 = (bf16[32,1024]{1,0:T(8,128)(2,1)S(1)}, bf16[32,1024]{1,0:T(8,128)(2,1)S(1)}, u32[]{:S(2)}, u32[]{:S(2)}) collective-permute-start(bf16[32,1024]{1,0:T(8,128)(2,1)S(1)} %constant_dynamic-slice_fusion), channel_id=1, source_target_pairs={{0,32},{16,48},{32,0},{48,16},{64,96},{80,112},{96,64},{112,80},{1... | collective-permute-start | bytes 196616 | tf_op jit(solution)/shard_map/ppermute | solution.py:300
  44.3 3.2 %prepare.1 = (f32[10,128,128]{2,1,0:T(8,128)S(1)}, s32[256]{0:T(256)S(1)}, s32[8,64]{1,0:T(8,128)S(1)}) custom-call(s32[1,3]{1,0:T(1,128)S(1)} %copy-done.11, f32[8]{0:T(128)S(1)} %copy-done.14, s32[3,64]{1,0:T(4,128)S(1)} %copy-done.13, s32[1,64]{1,0:T(1,128)S(1)} %bitcast.9), custom_call_target="tpu_custom_call" | custom-call | flops 268435456 | bytes 4194304 | tf_op jit(solution)/shard_map/prepare/pallas_call | solution.py:348
  47.4 0.0 collective-permute-done.7.cross_ref
  47.4 0.0 copy-start.2
  47.4 3.6 %attend_first.1 = (f32[8,128,128]{2,1,0:T(8,128)S(1)}, bf16[8,128,128]{2,1,0:T(8,128)(2,1)S(1)}) custom-call(s32[256]{0:T(256)S(1)} %get-tuple-element.21.list_ref, f32[10,128,128]{2,1,0:T(8,128)S(1)} %get-tuple-element.22.bias_ref, bf16[4,256,128]{2,1,0:T(8,128)(2,1)} %get-tuple-element.27.near_ref, bf16[4,256,128]{2,1,0:T(8,128)(2,1)S(1)} %get-tuple-element.32.far_ref, ...), custom_call_target="tpu_custom_call" | custom-call | flops 2147483648 | bytes 4194304 | tf_op jit(solution)/shard_map/attend_first/pallas_call | solution.py:384
  51.1 0.0 collective-permute-done.8.cross_ref
  51.1 1.9 %attend_last.1 = bf16[8,160,128]{2,1,0:T(8,128)(2,1)} custom-call(s32[1,3]{1,0:T(1,128)S(1)} %copy-done.11, s32[1,3]{1,0:T(1,128)S(1)} %copy-done.12, s32[256]{0:T(256)S(1)} %get-tuple-element.21.list_ref, f32[10,128,128]{2,1,0:T(8,128)S(1)} %get-tuple-element.22.bias_ref, bf16[8,128,128]{2,1,0:T(8,128)(2,1)S(1)} %get-tuple-element.35.queries_ref, ...), custom_call_target="tpu_custom_call" | custom-call | flops 1073741824 | bytes 2097152 | tf_op jit(solution)/shard_map/attend_last/pallas_call | solution.py:395
  53.0 6.4 %all-to-all-start = ((bf16[8,160,128]{2,1,0:T(8,128)(2,1)}), bf16[8,160,128]{2,1,0:T(8,128)(2,1)S(1)}, u32[]{:S(2)}, u32[]{:S(2)}) async-start(bf16[8,160,128]{2,1,0:T(8,128)(2,1)} %attend_last.1), calls=%async_computation | async-start | bytes 655360 | tf_op jit(solution)/shard_map/all_to_all | solution.py:406
  59.4 0.0 collective-permute-done.9
  59.5 0.1 collective-permute-start.10
  59.6 0.5 copy-done.16
  60.1 0.8 collective-permute-done.10
  60.9 0.9 pad_maximum_fusion.ta_ref
  61.7 1.0 %collective-permute-start.11 = (bf16[128,1024]{1,0:T(8,128)(2,1)S(1)}, bf16[128,1024]{1,0:T(8,128)(2,1)S(1)}, u32[]{:S(2)}, u32[]{:S(2)}) collective-permute-start(bf16[128,1024]{1,0:T(8,128)(2,1)S(1)} %pad_maximum_fusion.ta_ref), channel_id=1, source_target_pairs={{0,64},{16,80},{32,96},{48,112},{64,128},{80,144},{96,160},{112,17... | collective-permute-start | bytes 786440 | tf_op jit(solution)/shard_map/ppermute | solution.py:300
  62.8 3.2 %collective-permute-start.12 = (bf16[128,1024]{1,0:T(8,128)(2,1)S(1)}, bf16[128,1024]{1,0:T(8,128)(2,1)S(1)}, u32[]{:S(2)}, u32[]{:S(2)}) collective-permute-start(bf16[128,1024]{1,0:T(8,128)(2,1)S(1)} %pad_maximum_fusion.ta_ref), channel_id=1, source_target_pairs={{0,128},{16,144},{32,160},{48,176},{64,192},{80,208},{96,224},{112... | collective-permute-start | bytes 786440 | tf_op jit(solution)/shard_map/ppermute | solution.py:300
  66.0 0.8 collective-permute-start.13
  66.8 4.6 %collective-permute-done.11.tb_ref = bf16[128,1024]{1,0:T(8,128)(2,1)S(1)} collective-permute-done((bf16[128,1024]{1,0:T(8,128)(2,1)S(1)}, bf16[128,1024]{1,0:T(8,128)(2,1)S(1)}, u32[]{:S(2)}, u32[]{:S(2)}) %collective-permute-start.11) | collective-permute-done | bytes 262176 | tf_op jit(solution)/shard_map/ppermute | solution.py:300
  71.4 0.7 copy-done.4
  72.1 5.8 %collective-permute-done.12.tc_ref = bf16[128,1024]{1,0:T(8,128)(2,1)S(1)} collective-permute-done((bf16[128,1024]{1,0:T(8,128)(2,1)S(1)}, bf16[128,1024]{1,0:T(8,128)(2,1)S(1)}, u32[]{:S(2)}, u32[]{:S(2)}) %collective-permute-start.12) | collective-permute-done | bytes 262176 | tf_op jit(solution)/shard_map/ppermute | solution.py:300
  77.9 0.7 copy-done.6
  78.7 0.7 copy-done.8
  79.4 0.9 copy-done.5
  80.3 0.9 copy-done.7
  81.3 0.9 copy-done.9
  82.2 2.0 %state.1 = f32[16,16,128]{2,1,0:T(8,128)} custom-call(s32[1,3]{1,0:T(1,128)S(1)} %copy-done.11, bf16[8,160,128]{2,1,0:T(8,128)(2,1)S(1)} %all-to-all-done.mixed_ref, f32[1,1024]{1,0:T(1,128)S(1)} %bitcast.7, bf16[1024,1024]{1,0:T(8,128)(2,1)S(1)} %copy-done.1, bf16[128,1024]{1,0:T(8,128)(2,1)S(1)} %pad_maximum_fusion.ta_ref, ...), custom_call_target="tpu_custom_call" | custom-call | flops 33554432 | bytes 3145728 | tf_op jit(solution)/shard_map/state/pallas_call | solution.py:408
  84.2 7.6 %all-to-all-start.1 = ((f32[16,16,128]{2,1,0:T(8,128)}), f32[16,16,128]{2,1,0:T(8,128)S(1)}, u32[]{:S(2)}, u32[]{:S(2)}) async-start(f32[16,16,128]{2,1,0:T(8,128)} %state.1), calls=%async_computation.1 | async-start | bytes 262144 | tf_op jit(solution)/shard_map/all_to_all | solution.py:417
  91.8 0.0 copy-start.3
  91.8 0.9 copy-done.3
  92.8 1.3 %layer.1 = bf16[128,1024]{1,0:T(8,128)(2,1)} custom-call(bf16[8,160,128]{2,1,0:T(8,128)(2,1)S(1)} %all-to-all-done.mixed_ref, bf16[128,1024]{1,0:T(8,128)(2,1)S(1)} %copy-done.3, bf16[128,1024]{1,0:T(8,128)(2,1)S(1)} %bitcast.6, f32[1,1024]{1,0:T(1,128)S(1)} %bitcast.8, bf16[1024,1024]{1,0:T(8,128)(2,1)S(1)} %copy-done.1), custom_call_target="tpu_custom_call" | custom-call | flops 268435456 | bytes 3145728 | tf_op jit(solution)/shard_map/layer/pallas_call | solution.py:419
  94.1 6.1 %all-to-all-done.1.score_ref = f32[16,16,128]{2,1,0:T(8,128)S(1)} async-done(((f32[16,16,128]{2,1,0:T(8,128)}), f32[16,16,128]{2,1,0:T(8,128)S(1)}, u32[]{:S(2)}, u32[]{:S(2)}) %all-to-all-start.1) | async-done | bytes 131104 | tf_op jit(solution)/shard_map/all_to_all | solution.py:417
  100.2 1.1 %pick.1 = f32[3,64]{1,0:T(4,128)} custom-call(f32[16,16,128]{2,1,0:T(8,128)S(1)} %all-to-all-done.1.score_ref, s32[8,64]{1,0:T(8,128)S(1)} %get-tuple-element.39.place_ref), custom_call_target="tpu_custom_call" | custom-call | flops 1048576 | bytes 131072 | tf_op jit(solution)/shard_map/pick/pallas_call | solution.py:429
  (30 shorter events, 0.1 us)
Async XLA Ops:
  0.6 37.8 %copy-start = (bf16[256,1024]{1,0:T(8,128)(2,1)S(1)}, bf16[256,1024]{1,0:T(8,128)(2,1)}, u32[]{:S(2)}) copy-start(bf16[256,1024]{1,0:T(8,128)(2,1)} %param.19) | copy-start | bytes 1572868
  0.6 43.6 %copy-start.11 = (s32[1,3]{1,0:T(1,128)S(1)}, s32[1,3]{1,0:T(1,128)}, u32[]{:S(2)}) copy-start(s32[1,3]{1,0:T(1,128)} %blocks_ref.7) | copy-start | bytes 40
  0.7 43.6 %copy-start.15 = (s32[64]{0:T(128)S(1)}, s32[64]{0:T(128)}, u32[]{:S(2)}) copy-start(s32[64]{0:T(128)} %param.20) | copy-start | bytes 772
  0.7 43.6 %copy-start.14 = (f32[8]{0:T(128)S(1)}, f32[8]{0:T(128)}, u32[]{:S(2)}) copy-start(f32[8]{0:T(128)} %slope_ref.1) | copy-start | bytes 100
  0.7 43.6 %copy-start.13 = (s32[3,64]{1,0:T(4,128)S(1)}, s32[3,64]{1,0:T(4,128)}, u32[]{:S(2)}) copy-start(s32[3,64]{1,0:T(4,128)} %ids_ref.1) | copy-start | bytes 2308
  0.7 50.4 %copy-start.12 = (s32[1,3]{1,0:T(1,128)S(1)}, s32[1,3]{1,0:T(1,128)}, u32[]{:S(2)}) copy-start(s32[1,3]{1,0:T(1,128)} %tail_ref.3) | copy-start | bytes 40
  7.2 72.2 %copy-start.1 = (bf16[1024,1024]{1,0:T(8,128)(2,1)S(1)}, bf16[1024,1024]{1,0:T(8,128)(2,1)}, u32[]{:S(2)}) copy-start(bf16[1024,1024]{1,0:T(8,128)(2,1)} %w_ref.5) | copy-start | bytes 6291460
  7.2 72.2 %copy-start.10 = (f32[1024]{0:T(1024)S(1)}, f32[1024]{0:T(1024)}, u32[]{:S(2)}) copy-start(f32[1024]{0:T(1024)} %param.14) | copy-start | bytes 12292
  7.2 5.1 %collective-permute-start = (bf16[384,128]{1,0:T(8,128)(2,1)S(1)}, bf16[384,128]{1,0:T(8,128)(2,1)S(1)}, u32[]{:S(2)}, u32[]{:S(2)}) collective-permute-start(bf16[384,128]{1,0:T(8,128)(2,1)S(1)} %get-tuple-element.24), channel_id=1, source_target_pairs={{0,1},{1,0},{2,3},{3,2},{4,5},{5,4},{6,7},{7,6},{8,9},{9,8},{10,11... | collective-permute-start | bytes 294920 | tf_op jit(solution)/shard_map/ppermute | solution.py:304
  7.5 7.1 %collective-permute-start.1 = (bf16[384,128]{1,0:T(8,128)(2,1)S(1)}, bf16[384,128]{1,0:T(8,128)(2,1)S(1)}, u32[]{:S(2)}, u32[]{:S(2)}) collective-permute-start(bf16[384,128]{1,0:T(8,128)(2,1)S(1)} %get-tuple-element.25), channel_id=1, source_target_pairs={{0,8},{1,9},{2,10},{3,11},{4,12},{5,13},{6,14},{7,15},{8,0},{9,1},... | collective-permute-start | bytes 294920 | tf_op jit(solution)/shard_map/ppermute | solution.py:304
  10.7 7.0 %collective-permute-start.2 = (bf16[384,128]{1,0:T(8,128)(2,1)S(1)}, bf16[384,128]{1,0:T(8,128)(2,1)S(1)}, u32[]{:S(2)}, u32[]{:S(2)}) collective-permute-start(bf16[384,128]{1,0:T(8,128)(2,1)S(1)} %get-tuple-element.26), channel_id=1, source_target_pairs={{0,9},{1,8},{2,11},{3,10},{4,13},{5,12},{6,15},{7,14},{8,1},{9,0},... | collective-permute-start | bytes 294920 | tf_op jit(solution)/shard_map/ppermute | solution.py:304
  18.4 29.0 %collective-permute-start.7 = (bf16[4,256,128]{2,1,0:T(8,128)(2,1)}, bf16[4,256,128]{2,1,0:T(8,128)(2,1)}, u32[]{:S(2)}, u32[]{:S(2)}) collective-permute-start(bf16[4,256,128]{2,1,0:T(8,128)(2,1)} %get-tuple-element.27.near_ref), channel_id=1, source_target_pairs={{0,4},{1,5},{2,6},{3,7},{4,0},{5,1},{6,2},{7,3},{8,12},{9,13},{10,... | collective-permute-start | bytes 786440 | tf_op jit(solution)/shard_map/ppermute | solution.py:304
  19.1 14.1 %collective-permute-start.3 = (bf16[384,128]{1,0:T(8,128)(2,1)}, bf16[384,128]{1,0:T(8,128)(2,1)S(1)}, u32[]{:S(2)}, u32[]{:S(2)}) collective-permute-start(bf16[384,128]{1,0:T(8,128)(2,1)} %get-tuple-element.28), channel_id=1, source_target_pairs={{0,2},{1,3},{2,0},{3,1},{4,6},{5,7},{6,4},{7,5},{8,10},{9,11},{10,... | collective-permute-start | bytes 294920 | tf_op jit(solution)/shard_map/ppermute | solution.py:304
  22.4 10.9 %collective-permute-start.4 = (bf16[384,128]{1,0:T(8,128)(2,1)S(1)}, bf16[384,128]{1,0:T(8,128)(2,1)S(1)}, u32[]{:S(2)}, u32[]{:S(2)}) collective-permute-start(bf16[384,128]{1,0:T(8,128)(2,1)S(1)} %get-tuple-element.29), channel_id=1, source_target_pairs={{0,3},{1,2},{2,1},{3,0},{4,7},{5,6},{6,5},{7,4},{8,11},{9,10},{10,... | collective-permute-start | bytes 294920 | tf_op jit(solution)/shard_map/ppermute | solution.py:304
  22.4 15.9 %collective-permute-start.5 = (bf16[384,128]{1,0:T(8,128)(2,1)S(1)}, bf16[384,128]{1,0:T(8,128)(2,1)S(1)}, u32[]{:S(2)}, u32[]{:S(2)}) collective-permute-start(bf16[384,128]{1,0:T(8,128)(2,1)S(1)} %get-tuple-element.30), channel_id=1, source_target_pairs={{0,10},{1,11},{2,8},{3,9},{4,14},{5,15},{6,12},{7,13},{8,2},{9,3},... | collective-permute-start | bytes 294920 | tf_op jit(solution)/shard_map/ppermute | solution.py:304
  25.2 13.1 %collective-permute-start.6 = (bf16[384,128]{1,0:T(8,128)(2,1)S(1)}, bf16[384,128]{1,0:T(8,128)(2,1)S(1)}, u32[]{:S(2)}, u32[]{:S(2)}) collective-permute-start(bf16[384,128]{1,0:T(8,128)(2,1)S(1)} %get-tuple-element.31), channel_id=1, source_target_pairs={{0,11},{1,10},{2,9},{3,8},{4,15},{5,14},{6,13},{7,12},{8,3},{9,2},... | collective-permute-start | bytes 294920 | tf_op jit(solution)/shard_map/ppermute | solution.py:304
  38.3 12.8 %collective-permute-start.8 = (bf16[4,256,128]{2,1,0:T(8,128)(2,1)S(1)}, bf16[4,256,128]{2,1,0:T(8,128)(2,1)S(1)}, u32[]{:S(2)}, u32[]{:S(2)}) collective-permute-start(bf16[4,256,128]{2,1,0:T(8,128)(2,1)S(1)} %get-tuple-element.32.far_ref), channel_id=1, source_target_pairs={{0,4},{1,5},{2,6},{3,7},{4,0},{5,1},{6,2},{7,3},{8,12},{9,13},{10,... | collective-permute-start | bytes 786440 | tf_op jit(solution)/shard_map/ppermute | solution.py:304
  38.4 21.0 %collective-permute-start.9 = (bf16[32,1024]{1,0:T(8,128)(2,1)S(1)}, bf16[32,1024]{1,0:T(8,128)(2,1)S(1)}, u32[]{:S(2)}, u32[]{:S(2)}) collective-permute-start(bf16[32,1024]{1,0:T(8,128)(2,1)S(1)} %constant_dynamic-slice_fusion), channel_id=1, source_target_pairs={{0,32},{16,48},{32,0},{48,16},{64,96},{80,112},{96,64},{112,80},{1... | collective-permute-start | bytes 196616 | tf_op jit(solution)/shard_map/ppermute | solution.py:300
  47.4 44.4 %copy-start.2 = (bf16[1,128,1024]{2,1,0:T(8,128)(2,1)S(1)}, bf16[1,128,1024]{2,1,0:T(8,128)(2,1)}, u32[]{:S(2)}) copy-start(bf16[1,128,1024]{2,1,0:T(8,128)(2,1)} %param.11) | copy-start | bytes 786436
  53.0 26.4 %all-to-all-start = ((bf16[8,160,128]{2,1,0:T(8,128)(2,1)}), bf16[8,160,128]{2,1,0:T(8,128)(2,1)S(1)}, u32[]{:S(2)}, u32[]{:S(2)}) async-start(bf16[8,160,128]{2,1,0:T(8,128)(2,1)} %attend_last.1), calls=%async_computation | async-start | bytes 655360 | tf_op jit(solution)/shard_map/all_to_all | solution.py:406
  59.4 0.6 copy-start.16
  59.5 1.4 %collective-permute-start.10 = (bf16[64,1024]{1,0:T(8,128)(2,1)S(1)}, bf16[64,1024]{1,0:T(8,128)(2,1)S(1)}, u32[]{:S(2)}, u32[]{:S(2)}) collective-permute-start(bf16[64,1024]{1,0:T(8,128)(2,1)S(1)} %pad_maximum_fusion.1), channel_id=1, source_target_pairs={{0,16},{16,0},{32,48},{48,32},{64,80},{80,64},{96,112},{112,96},{1... | collective-permute-start | bytes 393224 | tf_op jit(solution)/shard_map/ppermute | solution.py:300
  61.7 9.6 %collective-permute-start.11 = (bf16[128,1024]{1,0:T(8,128)(2,1)S(1)}, bf16[128,1024]{1,0:T(8,128)(2,1)S(1)}, u32[]{:S(2)}, u32[]{:S(2)}) collective-permute-start(bf16[128,1024]{1,0:T(8,128)(2,1)S(1)} %pad_maximum_fusion.ta_ref), channel_id=1, source_target_pairs={{0,64},{16,80},{32,96},{48,112},{64,128},{80,144},{96,160},{112,17... | collective-permute-start | bytes 786440 | tf_op jit(solution)/shard_map/ppermute | solution.py:300
  62.8 15.2 %collective-permute-start.12 = (bf16[128,1024]{1,0:T(8,128)(2,1)S(1)}, bf16[128,1024]{1,0:T(8,128)(2,1)S(1)}, u32[]{:S(2)}, u32[]{:S(2)}) collective-permute-start(bf16[128,1024]{1,0:T(8,128)(2,1)S(1)} %pad_maximum_fusion.ta_ref), channel_id=1, source_target_pairs={{0,128},{16,144},{32,160},{48,176},{64,192},{80,208},{96,224},{112... | collective-permute-start | bytes 786440 | tf_op jit(solution)/shard_map/ppermute | solution.py:300
  66.0 12.7 %collective-permute-start.13 = (bf16[128,1024]{1,0:T(8,128)(2,1)S(1)}, bf16[128,1024]{1,0:T(8,128)(2,1)S(1)}, u32[]{:S(2)}, u32[]{:S(2)}) collective-permute-start(bf16[128,1024]{1,0:T(8,128)(2,1)S(1)} %pad_maximum_fusion.ta_ref), channel_id=1, source_target_pairs={{0,192},{16,208},{32,224},{48,240},{64,0},{80,16},{96,32},{112,48}... | collective-permute-start | bytes 786440 | tf_op jit(solution)/shard_map/ppermute | solution.py:300
  71.4 0.7 copy-start.4
  77.9 0.7 copy-start.6
  78.7 0.7 copy-start.8
  79.4 1.0 copy-start.5
  80.3 0.9 copy-start.7
  81.3 0.9 copy-start.9
  84.2 16.0 %all-to-all-start.1 = ((f32[16,16,128]{2,1,0:T(8,128)}), f32[16,16,128]{2,1,0:T(8,128)S(1)}, u32[]{:S(2)}, u32[]{:S(2)}) async-start(f32[16,16,128]{2,1,0:T(8,128)} %state.1), calls=%async_computation.1 | async-start | bytes 262144 | tf_op jit(solution)/shard_map/all_to_all | solution.py:417
  91.8 1.0 copy-start.3

commit v2 on v1

--- a/solution.py
+++ b/solution.py
@@ -57,42 +57,58 @@
     return (0, one, one + blocks_ref[0, 1])
 
 
-def project_kernel(blocks_ref, tail_ref, x_ref, gain_ref, w_ref, gate_ref, extra_ref, *refs):
-    out_refs, weights, sems = refs[:HEADS], refs[HEADS], refs[HEADS + 1]
-    me = lax.axis_index("seq")
-    order = FAR + NEAR
+def message(parts, out_ref):
+    out_ref[ROW_K:ROW_V, :] = parts[:, HD : 2 * HD].T.astype(jnp.bfloat16)
+    out_ref[ROW_V:ROW_Q, :] = parts[:, 2 * HD :].astype(jnp.bfloat16)
+    out_ref[ROW_Q:ROWS_A, :] = parts[:, :HD].astype(jnp.bfloat16)
+
+
+def project_far_kernel(x_ref, gain_ref, w_ref, normed_ref, *refs):
+    out_refs, weights, sems = refs[:4], refs[4], refs[5]
+    mine = head_of(lax.axis_index("seq"))
 
     def copies(at):
-        head = head_of(me) ^ order[at]
+        head = mine ^ FAR[at]
         return [
             pltpu.make_async_copy(
-                w_ref.at[:, pl.ds(pl.multiple_of((group * HEADS + head) * HD, HD), HD)],
+                w_ref.at[:, pl.ds(pl.multiple_of(((group + 1) * HEADS + head) * HD, HD), HD)],
                 weights.at[at, :, group * HD : (group + 1) * HD],
                 sems.at[at, group],
             )
-            for group in range(4)
+            for group in range(3)
         ]
 
-    for at in range(HEADS):
+    for at in range(4):
         for copy in copies(at):
             copy.start()
     normed = (layer_norm(x_ref[...].astype(jnp.float32)) * gain_ref[...]).astype(jnp.bfloat16)
+    normed_ref[...] = normed
     for at, out_ref in enumerate(out_refs):
         for copy in copies(at):
             copy.wait()
-        parts = silu(jnp.dot(normed, weights[at], preferred_element_type=jnp.float32))
-        head = head_of(me) ^ order[at]
-        gate_ref[:, pl.ds(pl.multiple_of(head * HD, HD), HD)] = parts[:, :HD].astype(jnp.bfloat16)
-        out_ref[ROW_K:ROW_V, :] = parts[:, 2 * HD : 3 * HD].T.astype(jnp.bfloat16)
-        out_ref[ROW_V:ROW_Q, :] = parts[:, 3 * HD :].astype(jnp.bfloat16)
-        out_ref[ROW_Q:ROWS_A, :] = parts[:, HD : 2 * HD].astype(jnp.bfloat16)
+        message(silu(jnp.dot(normed, weights[at], preferred_element_type=jnp.float32)), out_ref)
+
+
+def project_near_kernel(blocks_ref, tail_ref, x_ref, normed_ref, w_ref, gate_ref, extra_ref, *out_refs):
+    me = lax.axis_index("seq")
+    normed = normed_ref[...]
+    for q, out_ref in zip(NEAR, out_refs):
+        head = head_of(me) ^ q
+
+        def part(group, head=head):
+            columns = pl.ds(pl.multiple_of((group * HEADS + head) * HD, HD), HD)
+            return silu(jnp.dot(normed, w_ref[:, columns], preferred_element_type=jnp.float32))
+
+        message(jnp.concatenate([part(1), part(2), part(3)], axis=1), out_ref)
+    gate = silu(jnp.dot(normed, w_ref[:, :D], preferred_element_type=jnp.float32)).astype(jnp.bfloat16)
+    gate_ref[...] = gate
 
     starts = user_starts(blocks_ref)
     last = jnp.int32(-1)
     for user in range(USERS):
         last = jnp.where(starts[user] + blocks_ref[0, user] - 1 == me, tail_ref[0, user] - 1, last)
     pick = (lax.broadcasted_iota(jnp.int32, (16, BLK), 1) == last).astype(jnp.bfloat16)
-    gate_row = jnp.dot(pick, gate_ref[...], preferred_element_type=jnp.float32)[0:1]
+    gate_row = jnp.dot(pick, gate, preferred_element_type=jnp.float32)[0:1]
     token_row = jnp.dot(pick, x_ref[...], preferred_element_type=jnp.float32)[0:1]
     pieces = [row[:, h * HD : (h + 1) * HD] for row in (gate_row, token_row) for h in range(HEADS)]
     extra_ref[...] = jnp.concatenate(pieces, axis=0).astype(jnp.bfloat16)
@@ -237,7 +253,7 @@
         out_ref[t, ROW_X:ROWS_B, :] = extra_ref[...]
 
 
-def state_kernel(blocks_ref, mixed_ref, gain_ref, w_ref, ta_ref, tb_ref, tc_ref, td_ref, score_ref):
+def state_kernel(blocks_ref, mixed_ref, gain_ref, w_ref, ta_ref, tb_ref, tc_ref, td_ref, te_ref, score_ref):
     starts = user_starts(blocks_ref)
     tail = jnp.concatenate([mixed_ref[h, ROW_E:ROW_X, :].astype(jnp.float32) for h in range(HEADS)], axis=1)
     gates, tokens = [], []
@@ -253,8 +269,9 @@
     states = (token_tail + jnp.dot(gated, w_ref[...], preferred_element_type=jnp.float32)).astype(jnp.bfloat16)
     parts = [
         lax.dot_general(states, t_ref[...], (((1,), (1,)), ((), ())), preferred_element_type=jnp.float32)
-        for t_ref in (ta_ref, tb_ref, tc_ref, td_ref)
+        for t_ref in (ta_ref, tb_ref, tc_ref, td_ref, te_ref)
     ]
+    parts[2:4] = [jnp.concatenate(parts[2:4], axis=1)]
     rows = [part[user : user + 1] for user in range(USERS) for part in parts]
     block = jnp.concatenate(rows + [jnp.zeros((4, 128), jnp.float32)], axis=0)
     for to in range(NSEQ):
@@ -329,20 +346,30 @@
     seq = lax.axis_index("seq")
     mine = head_of(seq)
 
-    gate, extra, *sent = pl.pallas_call(
-        project_kernel,
-        in_specs=[smem(), smem(), vmem(), vmem(), pl.BlockSpec(memory_space=pltpu.HBM)],
-        out_specs=[vmem()] * (2 + HEADS),
-        out_shape=[pltpu.HBM((BLK, D), jnp.bfloat16), sds((16, HD))] + [sds((ROWS_A, HD))] * HEADS,
-        scratch_shapes=[pltpu.VMEM((HEADS, D, 4 * HD), jnp.bfloat16), pltpu.SemaphoreType.DMA((HEADS, 4))],
-        name="project",
-        cost_estimate=cost(2 * BLK * D * 4 * D, 10 << 20),
-        compiler_params=GRANT,
-    )(*(in_hbm(value) for value in (hist_blocks, hist_tail, x_rows, in_gain[None, :], w_proj)))
-    far_got, near_got = [], [sent[4]]
-    for q, value in zip(FAR, sent[:4]):
+    normed, *far_sent = pl.pallas_call(
+        project_far_kernel,
+        in_specs=[vmem(), vmem(), pl.BlockSpec(memory_space=pltpu.HBM)],
+        out_specs=[vmem()] * 5,
+        out_shape=[sds((BLK, D))] + [sds((ROWS_A, HD))] * 4,
+        scratch_shapes=[pltpu.VMEM((4, D, 3 * HD), jnp.bfloat16), pltpu.SemaphoreType.DMA((4, 3))],
+        name="project_far",
+        cost_estimate=cost(2 * BLK * D * 12 * HD, 4 << 20),
+        compiler_params=GRANT,
+    )(*(in_hbm(value) for value in (x_rows, in_gain[None, :], w_proj)))
+    far_got = []
+    for q, value in zip(FAR, far_sent):
         far_got.append(seq_xor(value, spread(q)))
-    for q, value in zip(NEAR[1:], sent[5:]):
+    gate, extra, *near_sent = pl.pallas_call(
+        project_near_kernel,
+        in_specs=[smem(), smem(), vmem(), vmem(), vmem()],
+        out_specs=[vmem()] * 6,
+        out_shape=[pltpu.HBM((BLK, D), jnp.bfloat16), sds((16, HD))] + [sds((ROWS_A, HD))] * 4,
+        name="project_near",
+        cost_estimate=cost(2 * BLK * D * 20 * HD, 9 << 20),
+        compiler_params=GRANT,
+    )(hist_blocks, hist_tail, x_rows, normed, w_proj)
+    near_got = [near_sent[0]]
+    for q, value in zip(NEAR[1:], near_sent[1:]):
         near_got.append(seq_xor(value, spread(q)))
 
     bias, pairs, places = pl.pallas_call(
@@ -377,9 +404,11 @@
     own = lax.dynamic_slice_in_dim(node_table, mine * 32, 32, 0)
     pair = jnp.concatenate([own, dp_shift(own, lambda i: i ^ 2)], axis=0)
     quad = jnp.concatenate([pair, dp_shift(pair, lambda i: i ^ 1)], axis=0)
-    table = [quad]
-    for n in (1, 2, 3):
-        table.append(dp_shift(quad, lambda i, n=n: (i + 4 * n) % 16))
+    below = dp_shift(quad, lambda i: (i + 4) % 16)
+    above = dp_shift(quad, lambda i: (i + 12) % 16)
+    opposite_first = dp_shift(below[:64], lambda i: (i + 4) % 16)
+    opposite_last = dp_shift(above[64:], lambda i: (i + 12) % 16)
+    table = [quad, below, opposite_first, opposite_last, above]
 
     part, queries = pl.pallas_call(
         attend_first_kernel,
@@ -407,7 +436,7 @@
 
     sent = pl.pallas_call(
         state_kernel,
-        in_specs=[smem()] + [vmem()] * 7,
+        in_specs=[smem()] + [vmem()] * 8,
         out_specs=vmem(),
         out_shape=pltpu.HBM((NSEQ, 16, 128), jnp.float32),
         name="state",

time: 103 us -> 93.8 us (0.911)
  the two profiles are of different devices: /device:TPU:0 before, /device:TPU:6 now
where the time goes in v2:
time: 93.8 us; the launch traced here: 93.4 us
  starting transfers between devices  47.2 us (50%)
  Pallas kernels  20.3 us (22%)
  waiting for transfers between devices  17.3 us (18%)
  local copies, waits for them, and re-layouts  6.05 us (6%)
  other arithmetic  1.63 us (2%)
    ppermute x9, starting transfers between devices, seq_xor(): return lax.ppermute(value, 'seq', [(i, i ^ apart) for i in range(NSEQ)])  19.2 us
    ppermute x6, starting transfers between devices, dp_shift(): return lax.ppermute(value, 'dp', [(i, move(i)) for i in range(16)])  13.9 us
    ppermute x6, waiting for transfers between devices, dp_shift(): return lax.ppermute(value, 'dp', [(i, move(i)) for i in range(16)])  10.6 us
    all_to_all x1, starting transfers between devices, layer(): scores = lax.all_to_all(sent, 'seq', 0, 0, tiled=True)  7.32 us
    all_to_all x1, starting transfers between devices, layer(): lax.all_to_all(back, 'seq', 0, 0, tiled=True, axis_index_groups=SETS)  6.85 us
    all_to_all x1, waiting for transfers between devices, layer(): scores = lax.all_to_all(sent, 'seq', 0, 0, tiled=True)  6.12 us
    unnamed x46, local copies, waits for them, and re-layouts  6.02 us
    pallas_call x1, Pallas kernels, layer(): pl.pallas_call(project_far_kernel, in_specs=[vmem(), vmem(), pl.BlockSpec...  4.69 us
  transfers between devices with their start and end apart: 17, of which 5 were waited for; matrix products, arithmetic and copies ran while one was open for 2% of the time, Pallas kernels for 10%

profile of v2, /device:TPU:6, one launch (start us, length us, event | category | flops | bytes accessed | tf_op | source)
XLA Modules:
  0.0 93.4 jit_solution(8423313255541094521)
XLA Ops:
  0.6 0.0 copy-start
  0.7 4.7 %project_far.1 = (bf16[128,1024]{1,0:T(8,128)(2,1)S(1)}, bf16[384,128]{1,0:T(8,128)(2,1)}, bf16[384,128]{1,0:T(8,128)(2,1)}, bf16[384,128]{1,0:T(8,128)(2,1)S(1)}, bf16[384,128]{1,0:T(8,128)(2,1)S(1)}) custom-call(bf16[128,1024]{1,0:T(8,128)(2,1)} %bitcast.5, f32[1,1024]{1,0:T(1,128)} %bitcast.12, bf16[1024,4096]{1,0:T(8,128)(2,1)} %w_ref.5), custom_call_target="tpu_custom_call" | custom-call | flops 402653184 | bytes 4194304 | tf_op jit(solution)/shard_map/project_far/pallas_call | solution.py:349
  5.5 2.9 %project_near.1 = (bf16[128,1024]{1,0:T(8,128)(2,1)}, bf16[16,128]{1,0:T(8,128)(2,1)S(1)}, bf16[384,128]{1,0:T(8,128)(2,1)S(1)}, bf16[384,128]{1,0:T(8,128)(2,1)...) custom-call(s32[1,3]{1,0:T(1,128)S(1)} %copy-done.14, s32[1,3]{1,0:T(1,128)S(1)} %copy-done.15, ...), custom_call_target="tpu_custom_call" | custom-call | flops 671088640 | bytes 9437184 | tf_op jit(solution)/shard_map/project_near/pallas_call | solution.py:362
  8.4 2.0 %collective-permute-start = (bf16[384,128]{1,0:T(8,128)(2,1)}, bf16[384,128]{1,0:T(8,128)(2,1)S(1)}, u32[]{:S(2)}, u32[]{:S(2)}) collective-permute-start(bf16[384,128]{1,0:T(8,128)(2,1)} %get-tuple-element.26), channel_id=1, source_target_pairs={{0,1},{1,0},{2,3},{3,2},{4,5},{5,4},{6,7},{7,6},{8,9},{9,8},{10,11... | collective-permute-start | bytes 294920 | tf_op jit(solution)/shard_map/ppermute | solution.py:321
  10.4 3.2 %collective-permute-start.1 = (bf16[384,128]{1,0:T(8,128)(2,1)}, bf16[384,128]{1,0:T(8,128)(2,1)S(1)}, u32[]{:S(2)}, u32[]{:S(2)}) collective-permute-start(bf16[384,128]{1,0:T(8,128)(2,1)} %get-tuple-element.27), channel_id=1, source_target_pairs={{0,8},{1,9},{2,10},{3,11},{4,12},{5,13},{6,14},{7,15},{8,0},{9,1},... | collective-permute-start | bytes 294920 | tf_op jit(solution)/shard_map/ppermute | solution.py:321
  13.6 0.0 collective-permute-start.2
  13.6 3.2 %collective-permute-start.3 = (bf16[384,128]{1,0:T(8,128)(2,1)}, bf16[384,128]{1,0:T(8,128)(2,1)S(1)}, u32[]{:S(2)}, u32[]{:S(2)}) collective-permute-start(bf16[384,128]{1,0:T(8,128)(2,1)} %get-tuple-element.30), channel_id=1, source_target_pairs={{0,2},{1,3},{2,0},{3,1},{4,6},{5,7},{6,4},{7,5},{8,10},{9,11},{10,... | collective-permute-start | bytes 294920 | tf_op jit(solution)/shard_map/ppermute | solution.py:321
  16.8 1.3 %collective-permute-start.4 = (bf16[384,128]{1,0:T(8,128)(2,1)}, bf16[384,128]{1,0:T(8,128)(2,1)S(1)}, u32[]{:S(2)}, u32[]{:S(2)}) collective-permute-start(bf16[384,128]{1,0:T(8,128)(2,1)} %get-tuple-element.31), channel_id=1, source_target_pairs={{0,3},{1,2},{2,1},{3,0},{4,7},{5,6},{6,5},{7,4},{8,11},{9,10},{10,... | collective-permute-start | bytes 294920 | tf_op jit(solution)/shard_map/ppermute | solution.py:321
  18.1 0.0 collective-permute-done.refs_1_
  18.1 4.6 %collective-permute-start.5 = (bf16[384,128]{1,0:T(8,128)(2,1)}, bf16[384,128]{1,0:T(8,128)(2,1)S(1)}, u32[]{:S(2)}, u32[]{:S(2)}) collective-permute-start(bf16[384,128]{1,0:T(8,128)(2,1)} %copy-done.17), channel_id=1, source_target_pairs={{0,10},{1,11},{2,8},{3,9},{4,14},{5,15},{6,12},{7,13},{8,2},{9,3},... | collective-permute-start | bytes 294920 | tf_op jit(solution)/shard_map/ppermute | solution.py:321
  22.7 0.0 collective-permute-done.1.refs_2_
  22.7 1.5 %collective-permute-start.6 = (bf16[384,128]{1,0:T(8,128)(2,1)}, bf16[384,128]{1,0:T(8,128)(2,1)S(1)}, u32[]{:S(2)}, u32[]{:S(2)}) collective-permute-start(bf16[384,128]{1,0:T(8,128)(2,1)} %copy-done.16), channel_id=1, source_target_pairs={{0,11},{1,10},{2,9},{3,8},{4,15},{5,14},{6,13},{7,12},{8,3},{9,2},... | collective-permute-start | bytes 294920 | tf_op jit(solution)/shard_map/ppermute | solution.py:321
  24.2 0.0 collective-permute-done.2.refs_3_
  24.2 1.0 %collective-permute-start.7 = (bf16[4,256,128]{2,1,0:T(8,128)(2,1)S(1)}, bf16[4,256,128]{2,1,0:T(8,128)(2,1)S(1)}, u32[]{:S(2)}, u32[]{:S(2)}) collective-permute-start(bf16[4,256,128]{2,1,0:T(8,128)(2,1)S(1)} %get-tuple-element.29.near_ref), channel_id=1, source_target_pairs={{0,4},{1,5},{2,6},{3,7},{4,0},{5,1},{6,2},{7,3},{8,12},{9,13},{10,... | collective-permute-start | bytes 786440 | tf_op jit(solution)/shard_map/ppermute | solution.py:321
  25.2 0.0 collective-permute-done.3.refs_0_
  25.2 9.6 %collective-permute-start.9 = (bf16[32,1024]{1,0:T(8,128)(2,1)S(1)}, bf16[32,1024]{1,0:T(8,128)(2,1)S(1)}, u32[]{:S(2)}, u32[]{:S(2)}) collective-permute-start(bf16[32,1024]{1,0:T(8,128)(2,1)S(1)} %constant_dynamic-slice_fusion), channel_id=1, source_target_pairs={{0,32},{16,48},{32,0},{48,16},{64,96},{80,112},{96,64},{112,80},{1... | collective-permute-start | bytes 196616 | tf_op jit(solution)/shard_map/ppermute | solution.py:317
  34.8 3.1 %prepare.1 = (f32[10,128,128]{2,1,0:T(8,128)S(1)}, s32[256]{0:T(256)S(1)}, s32[8,64]{1,0:T(8,128)S(1)}) custom-call(s32[1,3]{1,0:T(1,128)S(1)} %copy-done.14, f32[8]{0:T(128)S(1)} %copy-done.19, s32[3,64]{1,0:T(4,128)S(1)} %copy-done.18, s32[1,64]{1,0:T(1,128)S(1)} %bitcast.10), custom_call_target="tpu_custom_call" | custom-call | flops 268435456 | bytes 4194304 | tf_op jit(solution)/shard_map/prepare/pallas_call | solution.py:375
  38.0 0.0 collective-permute-done.4.refs_1_
  38.0 0.0 collective-permute-done.6.refs_3_
  38.0 2.4 %collective-permute-start.8 = (bf16[4,256,128]{2,1,0:T(8,128)(2,1)S(1)}, bf16[4,256,128]{2,1,0:T(8,128)(2,1)S(1)}, u32[]{:S(2)}, u32[]{:S(2)}) collective-permute-start(bf16[4,256,128]{2,1,0:T(8,128)(2,1)S(1)} %get-tuple-element.34.far_ref), channel_id=1, source_target_pairs={{0,4},{1,5},{2,6},{3,7},{4,0},{5,1},{6,2},{7,3},{8,12},{9,13},{10,... | collective-permute-start | bytes 786440 | tf_op jit(solution)/shard_map/ppermute | solution.py:321
  40.5 0.0 collective-permute-done.9
  40.5 0.7 pad_maximum_fusion.1
  41.2 3.1 %attend_first.1 = (f32[8,128,128]{2,1,0:T(8,128)S(1)}, bf16[8,128,128]{2,1,0:T(8,128)(2,1)S(1)}) custom-call(s32[256]{0:T(256)S(1)} %get-tuple-element.22.list_ref, f32[10,128,128]{2,1,0:T(8,128)S(1)} %get-tuple-element.23.bias_ref, bf16[4,256,128]{2,1,0:T(8,128)(2,1)S(1)} %get-tuple-element.29.near_ref, bf16[4,256,128]{2,1,0:T(8,128)(2,1)S(1)} %get-tuple-element.34.far_ref, ...), custom_call_target="tpu_custom_call" | custom-call | flops 2147483648 | bytes 4194304 | tf_op jit(solution)/shard_map/attend_first/pallas_call | solution.py:413
  44.3 0.6 collective-permute-done.8.cross_ref
  44.8 1.9 %attend_last.1 = bf16[8,160,128]{2,1,0:T(8,128)(2,1)} custom-call(s32[1,3]{1,0:T(1,128)S(1)} %copy-done.14, s32[1,3]{1,0:T(1,128)S(1)} %copy-done.15, s32[256]{0:T(256)S(1)} %get-tuple-element.22.list_ref, f32[10,128,128]{2,1,0:T(8,128)S(1)} %get-tuple-element.23.bias_ref, bf16[8,128,128]{2,1,0:T(8,128)(2,1)S(1)} %get-tuple-element.37.queries_ref, ...), custom_call_target="tpu_custom_call" | custom-call | flops 1073741824 | bytes 2097152 | tf_op jit(solution)/shard_map/attend_last/pallas_call | solution.py:424
  46.7 6.8 %all-to-all-start = ((bf16[8,160,128]{2,1,0:T(8,128)(2,1)}), bf16[8,160,128]{2,1,0:T(8,128)(2,1)S(1)}, u32[]{:S(2)}, u32[]{:S(2)}) async-start(bf16[8,160,128]{2,1,0:T(8,128)(2,1)} %attend_last.1), calls=%async_computation | async-start | bytes 655360 | tf_op jit(solution)/shard_map/all_to_all | solution.py:435
  53.6 0.0 collective-permute-done.10
  53.6 1.0 %pad_maximum_fusion.ta_ref = bf16[128,1024]{1,0:T(8,128)(2,1)S(1)} fusion(bf16[64,1024]{1,0:T(8,128)(2,1)} %collective-permute-done.10, bf16[32,1024]{1,0:T(8,128)(2,1)} %copy-done.22, bf16[32,1024]{1,0:T(8,128)(2,1)} %copy-done.21), kind=kLoop, calls=%fused_computation | loop fusion | flops 786432 | bytes 524288 | tf_op jit(solution)/shard_map/concatenate | solution.py:406
  54.5 0.6 collective-permute-start.11
  55.1 1.5 %collective-permute-start.13 = (bf16[128,1024]{1,0:T(8,128)(2,1)S(1)}, bf16[128,1024]{1,0:T(8,128)(2,1)S(1)}, u32[]{:S(2)}, u32[]{:S(2)}) collective-permute-start(bf16[128,1024]{1,0:T(8,128)(2,1)S(1)} %pad_maximum_fusion.ta_ref), channel_id=1, source_target_pairs={{0,192},{16,208},{32,224},{48,240},{64,0},{80,16},{96,32},{112,48}... | collective-permute-start | bytes 786440 | tf_op jit(solution)/shard_map/ppermute | solution.py:317
  56.6 5.4 %collective-permute-done.11.tb_ref = bf16[128,1024]{1,0:T(8,128)(2,1)S(1)} collective-permute-done((bf16[128,1024]{1,0:T(8,128)(2,1)S(1)}, bf16[128,1024]{1,0:T(8,128)(2,1)S(1)}, u32[]{:S(2)}, u32[]{:S(2)}) %collective-permute-start.11) | collective-permute-done | bytes 262176 | tf_op jit(solution)/shard_map/ppermute | solution.py:317
  62.1 1.7 %collective-permute-start.12 = (bf16[64,1024]{1,0:T(8,128)(2,1)S(1)}, bf16[64,1024]{1,0:T(8,128)(2,1)S(1)}, u32[]{:S(2)}, u32[]{:S(2)}) collective-permute-start(bf16[64,1024]{1,0:T(8,128)(2,1)S(1)} %slice.8), channel_id=1, source_target_pairs={{0,64},{16,80},{32,96},{48,112},{64,128},{80,144},{96,160},{112,17... | collective-permute-start | bytes 393224 | tf_op jit(solution)/shard_map/ppermute | solution.py:317
  63.8 0.5 collective-permute-start.14
  64.3 3.1 %collective-permute-done.12.tc_ref = bf16[64,1024]{1,0:T(8,128)(2,1)S(1)} collective-permute-done((bf16[64,1024]{1,0:T(8,128)(2,1)S(1)}, bf16[64,1024]{1,0:T(8,128)(2,1)S(1)}, u32[]{:S(2)}, u32[]{:S(2)}) %collective-permute-start.12) | collective-permute-done | bytes 131104 | tf_op jit(solution)/shard_map/ppermute | solution.py:317
  67.4 0.6 copy-done.9
  68.1 2.0 %collective-permute-done.14.td_ref = bf16[64,1024]{1,0:T(8,128)(2,1)S(1)} collective-permute-done((bf16[64,1024]{1,0:T(8,128)(2,1)S(1)}, bf16[64,1024]{1,0:T(8,128)(2,1)S(1)}, u32[]{:S(2)}, u32[]{:S(2)}) %collective-permute-start.14) | collective-permute-done | bytes 131104 | tf_op jit(solution)/shard_map/ppermute | solution.py:317
  70.1 0.7 copy-done.11
  70.7 0.9 %copy-done.5 = bf16[128,1024]{1,0:T(8,128)(2,1)S(1)} copy-done((bf16[128,1024]{1,0:T(8,128)(2,1)S(1)}, bf16[128,1024]{1,0:T(8,128)(2,1)}, u32[]{:S(2)}) %copy-start.5) | copy-done | bytes 262168
  71.7 0.9 %copy-done.7 = bf16[128,1024]{1,0:T(8,128)(2,1)S(1)} copy-done((bf16[128,1024]{1,0:T(8,128)(2,1)S(1)}, bf16[128,1024]{1,0:T(8,128)(2,1)}, u32[]{:S(2)}) %copy-start.7) | copy-done | bytes 262168
  72.6 0.9 copy-done.10
  73.5 0.9 copy-done.12
  74.4 2.1 %state.1 = f32[16,16,128]{2,1,0:T(8,128)} custom-call(s32[1,3]{1,0:T(1,128)S(1)} %copy-done.14, bf16[8,160,128]{2,1,0:T(8,128)(2,1)S(1)} %all-to-all-done.mixed_ref, f32[1,1024]{1,0:T(1,128)S(1)} %bitcast.8, bf16[1024,1024]{1,0:T(8,128)(2,1)S(1)} %copy-done.2, bf16[128,1024]{1,0:T(8,128)(2,1)S(1)} %pad_maximum_fusion.ta_ref, ...), custom_call_target="tpu_custom_call" | custom-call | flops 33554432 | bytes 3145728 | tf_op jit(solution)/shard_map/state/pallas_call | solution.py:437
  76.6 7.3 %all-to-all-start.1 = ((f32[16,16,128]{2,1,0:T(8,128)}), f32[16,16,128]{2,1,0:T(8,128)S(1)}, u32[]{:S(2)}, u32[]{:S(2)}) async-start(f32[16,16,128]{2,1,0:T(8,128)} %state.1), calls=%async_computation.1 | async-start | bytes 262144 | tf_op jit(solution)/shard_map/all_to_all | solution.py:446
  83.9 0.0 copy-start.8
  83.9 0.9 %copy-done.8 = bf16[128,1024]{1,0:T(8,128)(2,1)S(1)} copy-done((bf16[128,1024]{1,0:T(8,128)(2,1)S(1)}, bf16[128,1024]{1,0:T(8,128)(2,1)}, u32[]{:S(2)}) %copy-start.8) | copy-done | bytes 262168
  84.8 1.3 %layer.1 = bf16[128,1024]{1,0:T(8,128)(2,1)} custom-call(bf16[8,160,128]{2,1,0:T(8,128)(2,1)S(1)} %all-to-all-done.mixed_ref, bf16[128,1024]{1,0:T(8,128)(2,1)S(1)} %copy-done.8, bf16[128,1024]{1,0:T(8,128)(2,1)S(1)} %bitcast.7, f32[1,1024]{1,0:T(1,128)S(1)} %bitcast.9, bf16[1024,1024]{1,0:T(8,128)(2,1)S(1)} %copy-done.2), custom_call_target="tpu_custom_call" | custom-call | flops 268435456 | bytes 3145728 | tf_op jit(solution)/shard_map/layer/pallas_call | solution.py:448
  86.2 6.1 %all-to-all-done.1.score_ref = f32[16,16,128]{2,1,0:T(8,128)S(1)} async-done(((f32[16,16,128]{2,1,0:T(8,128)}), f32[16,16,128]{2,1,0:T(8,128)S(1)}, u32[]{:S(2)}, u32[]{:S(2)}) %all-to-all-start.1) | async-done | bytes 131104 | tf_op jit(solution)/shard_map/all_to_all | solution.py:446
  92.3 1.1 %pick.1 = f32[3,64]{1,0:T(4,128)} custom-call(f32[16,16,128]{2,1,0:T(8,128)S(1)} %all-to-all-done.1.score_ref, s32[8,64]{1,0:T(8,128)S(1)} %get-tuple-element.41.place_ref), custom_call_target="tpu_custom_call" | custom-call | flops 1048576 | bytes 131072 | tf_op jit(solution)/shard_map/pick/pallas_call | solution.py:458
  (47 shorter events, 0.2 us)
Async XLA Ops:
  0.6 24.6 %copy-start = (bf16[256,1024]{1,0:T(8,128)(2,1)S(1)}, bf16[256,1024]{1,0:T(8,128)(2,1)}, u32[]{:S(2)}) copy-start(bf16[256,1024]{1,0:T(8,128)(2,1)} %param.19) | copy-start | bytes 1572868
  0.6 4.8 %copy-start.3 = (bf16[1,128,1024]{2,1,0:T(8,128)(2,1)S(1)}, bf16[1,128,1024]{2,1,0:T(8,128)(2,1)}, u32[]{:S(2)}) copy-start(bf16[1,128,1024]{2,1,0:T(8,128)(2,1)} %param.11) | copy-start | bytes 786436
  0.7 4.8 %copy-start.1 = (bf16[1024,4096]{1,0:T(8,128)(2,1)S(1)}, bf16[1024,4096]{1,0:T(8,128)(2,1)}, u32[]{:S(2)}) copy-start(bf16[1024,4096]{1,0:T(8,128)(2,1)} %w_ref.5) | copy-start | bytes 25165828
  0.7 4.8 %copy-start.14 = (s32[1,3]{1,0:T(1,128)S(1)}, s32[1,3]{1,0:T(1,128)}, u32[]{:S(2)}) copy-start(s32[1,3]{1,0:T(1,128)} %blocks_ref.7) | copy-start | bytes 40
  0.7 4.8 %copy-start.15 = (s32[1,3]{1,0:T(1,128)S(1)}, s32[1,3]{1,0:T(1,128)}, u32[]{:S(2)}) copy-start(s32[1,3]{1,0:T(1,128)} %tail_ref.3) | copy-start | bytes 40
  0.7 34.1 %copy-start.18 = (s32[3,64]{1,0:T(4,128)S(1)}, s32[3,64]{1,0:T(4,128)}, u32[]{:S(2)}) copy-start(s32[3,64]{1,0:T(4,128)} %ids_ref.1) | copy-start | bytes 2308
  0.7 34.1 %copy-start.19 = (f32[8]{0:T(128)S(1)}, f32[8]{0:T(128)}, u32[]{:S(2)}) copy-start(f32[8]{0:T(128)} %slope_ref.1) | copy-start | bytes 100
  0.7 34.1 %copy-start.20 = (s32[64]{0:T(128)S(1)}, s32[64]{0:T(128)}, u32[]{:S(2)}) copy-start(s32[64]{0:T(128)} %param.20) | copy-start | bytes 772
  5.4 11.4 %copy-start.16 = (bf16[384,128]{1,0:T(8,128)(2,1)}, bf16[384,128]{1,0:T(8,128)(2,1)S(1)}, u32[]{:S(2)}) copy-start(bf16[384,128]{1,0:T(8,128)(2,1)S(1)} %get-tuple-element.33) | copy-start | bytes 294916
  5.4 11.4 %copy-start.17 = (bf16[384,128]{1,0:T(8,128)(2,1)}, bf16[384,128]{1,0:T(8,128)(2,1)S(1)}, u32[]{:S(2)}) copy-start(bf16[384,128]{1,0:T(8,128)(2,1)S(1)} %get-tuple-element.32) | copy-start | bytes 294916
  8.4 62.3 %copy-start.2 = (bf16[1024,1024]{1,0:T(8,128)(2,1)S(1)}, bf16[1024,1024]{1,0:T(8,128)(2,1)}, u32[]{:S(2)}) copy-start(bf16[1024,1024]{1,0:T(8,128)(2,1)} %w_ref.7) | copy-start | bytes 6291460
  8.4 62.3 %copy-start.13 = (f32[1024]{0:T(1024)S(1)}, f32[1024]{0:T(1024)}, u32[]{:S(2)}) copy-start(f32[1024]{0:T(1024)} %param.14) | copy-start | bytes 12292
  8.4 9.7 %collective-permute-start = (bf16[384,128]{1,0:T(8,128)(2,1)}, bf16[384,128]{1,0:T(8,128)(2,1)S(1)}, u32[]{:S(2)}, u32[]{:S(2)}) collective-permute-start(bf16[384,128]{1,0:T(8,128)(2,1)} %get-tuple-element.26), channel_id=1, source_target_pairs={{0,1},{1,0},{2,3},{3,2},{4,5},{5,4},{6,7},{7,6},{8,9},{9,8},{10,11... | collective-permute-start | bytes 294920 | tf_op jit(solution)/shard_map/ppermute | solution.py:321
  10.4 12.3 %collective-permute-start.1 = (bf16[384,128]{1,0:T(8,128)(2,1)}, bf16[384,128]{1,0:T(8,128)(2,1)S(1)}, u32[]{:S(2)}, u32[]{:S(2)}) collective-permute-start(bf16[384,128]{1,0:T(8,128)(2,1)} %get-tuple-element.27), channel_id=1, source_target_pairs={{0,8},{1,9},{2,10},{3,11},{4,12},{5,13},{6,14},{7,15},{8,0},{9,1},... | collective-permute-start | bytes 294920 | tf_op jit(solution)/shard_map/ppermute | solution.py:321
  13.6 10.6 %collective-permute-start.2 = (bf16[384,128]{1,0:T(8,128)(2,1)}, bf16[384,128]{1,0:T(8,128)(2,1)S(1)}, u32[]{:S(2)}, u32[]{:S(2)}) collective-permute-start(bf16[384,128]{1,0:T(8,128)(2,1)} %get-tuple-element.28), channel_id=1, source_target_pairs={{0,9},{1,8},{2,11},{3,10},{4,13},{5,12},{6,15},{7,14},{8,1},{9,0},... | collective-permute-start | bytes 294920 | tf_op jit(solution)/shard_map/ppermute | solution.py:321
  13.6 11.7 %collective-permute-start.3 = (bf16[384,128]{1,0:T(8,128)(2,1)}, bf16[384,128]{1,0:T(8,128)(2,1)S(1)}, u32[]{:S(2)}, u32[]{:S(2)}) collective-permute-start(bf16[384,128]{1,0:T(8,128)(2,1)} %get-tuple-element.30), channel_id=1, source_target_pairs={{0,2},{1,3},{2,0},{3,1},{4,6},{5,7},{6,4},{7,5},{8,10},{9,11},{10,... | collective-permute-start | bytes 294920 | tf_op jit(solution)/shard_map/ppermute | solution.py:321
  16.8 21.2 %collective-permute-start.4 = (bf16[384,128]{1,0:T(8,128)(2,1)}, bf16[384,128]{1,0:T(8,128)(2,1)S(1)}, u32[]{:S(2)}, u32[]{:S(2)}) collective-permute-start(bf16[384,128]{1,0:T(8,128)(2,1)} %get-tuple-element.31), channel_id=1, source_target_pairs={{0,3},{1,2},{2,1},{3,0},{4,7},{5,6},{6,5},{7,4},{8,11},{9,10},{10,... | collective-permute-start | bytes 294920 | tf_op jit(solution)/shard_map/ppermute | solution.py:321
  18.1 19.8 %collective-permute-start.5 = (bf16[384,128]{1,0:T(8,128)(2,1)}, bf16[384,128]{1,0:T(8,128)(2,1)S(1)}, u32[]{:S(2)}, u32[]{:S(2)}) collective-permute-start(bf16[384,128]{1,0:T(8,128)(2,1)} %copy-done.17), channel_id=1, source_target_pairs={{0,10},{1,11},{2,8},{3,9},{4,14},{5,15},{6,12},{7,13},{8,2},{9,3},... | collective-permute-start | bytes 294920 | tf_op jit(solution)/shard_map/ppermute | solution.py:321
  22.7 15.3 %collective-permute-start.6 = (bf16[384,128]{1,0:T(8,128)(2,1)}, bf16[384,128]{1,0:T(8,128)(2,1)S(1)}, u32[]{:S(2)}, u32[]{:S(2)}) collective-permute-start(bf16[384,128]{1,0:T(8,128)(2,1)} %copy-done.16), channel_id=1, source_target_pairs={{0,11},{1,10},{2,9},{3,8},{4,15},{5,14},{6,13},{7,12},{8,3},{9,2},... | collective-permute-start | bytes 294920 | tf_op jit(solution)/shard_map/ppermute | solution.py:321
  24.2 17.0 %collective-permute-start.7 = (bf16[4,256,128]{2,1,0:T(8,128)(2,1)S(1)}, bf16[4,256,128]{2,1,0:T(8,128)(2,1)S(1)}, u32[]{:S(2)}, u32[]{:S(2)}) collective-permute-start(bf16[4,256,128]{2,1,0:T(8,128)(2,1)S(1)} %get-tuple-element.29.near_ref), channel_id=1, source_target_pairs={{0,4},{1,5},{2,6},{3,7},{4,0},{5,1},{6,2},{7,3},{8,12},{9,13},{10,... | collective-permute-start | bytes 786440 | tf_op jit(solution)/shard_map/ppermute | solution.py:321
  25.2 19.6 %copy-start.21 = (bf16[32,1024]{1,0:T(8,128)(2,1)}, bf16[32,1024]{1,0:T(8,128)(2,1)S(1)}, u32[]{:S(2)}) copy-start(bf16[32,1024]{1,0:T(8,128)(2,1)S(1)} %constant_dynamic-slice_fusion) | copy-start | bytes 196612
  25.2 15.2 %collective-permute-start.9 = (bf16[32,1024]{1,0:T(8,128)(2,1)S(1)}, bf16[32,1024]{1,0:T(8,128)(2,1)S(1)}, u32[]{:S(2)}, u32[]{:S(2)}) collective-permute-start(bf16[32,1024]{1,0:T(8,128)(2,1)S(1)} %constant_dynamic-slice_fusion), channel_id=1, source_target_pairs={{0,32},{16,48},{32,0},{48,16},{64,96},{80,112},{96,64},{112,80},{1... | collective-permute-start | bytes 196616 | tf_op jit(solution)/shard_map/ppermute | solution.py:317
  38.0 6.8 %collective-permute-start.8 = (bf16[4,256,128]{2,1,0:T(8,128)(2,1)S(1)}, bf16[4,256,128]{2,1,0:T(8,128)(2,1)S(1)}, u32[]{:S(2)}, u32[]{:S(2)}) collective-permute-start(bf16[4,256,128]{2,1,0:T(8,128)(2,1)S(1)} %get-tuple-element.34.far_ref), channel_id=1, source_target_pairs={{0,4},{1,5},{2,6},{3,7},{4,0},{5,1},{6,2},{7,3},{8,12},{9,13},{10,... | collective-permute-start | bytes 786440 | tf_op jit(solution)/shard_map/ppermute | solution.py:321
  40.5 4.4 %copy-start.22 = (bf16[32,1024]{1,0:T(8,128)(2,1)}, bf16[32,1024]{1,0:T(8,128)(2,1)S(1)}, u32[]{:S(2)}) copy-start(bf16[32,1024]{1,0:T(8,128)(2,1)S(1)} %collective-permute-done.9) | copy-start | bytes 196612
  41.2 12.4 %collective-permute-start.10 = (bf16[64,1024]{1,0:T(8,128)(2,1)}, bf16[64,1024]{1,0:T(8,128)(2,1)}, u32[]{:S(2)}, u32[]{:S(2)}) collective-permute-start(bf16[64,1024]{1,0:T(8,128)(2,1)} %pad_maximum_fusion.1), channel_id=1, source_target_pairs={{0,16},{16,0},{32,48},{48,32},{64,80},{80,64},{96,112},{112,96},{1... | collective-permute-start | bytes 393224 | tf_op jit(solution)/shard_map/ppermute | solution.py:317
  46.7 24.0 %all-to-all-start = ((bf16[8,160,128]{2,1,0:T(8,128)(2,1)}), bf16[8,160,128]{2,1,0:T(8,128)(2,1)S(1)}, u32[]{:S(2)}, u32[]{:S(2)}) async-start(bf16[8,160,128]{2,1,0:T(8,128)(2,1)} %attend_last.1), calls=%async_computation | async-start | bytes 655360 | tf_op jit(solution)/shard_map/all_to_all | solution.py:435
  54.5 7.5 %collective-permute-start.11 = (bf16[128,1024]{1,0:T(8,128)(2,1)S(1)}, bf16[128,1024]{1,0:T(8,128)(2,1)S(1)}, u32[]{:S(2)}, u32[]{:S(2)}) collective-permute-start(bf16[128,1024]{1,0:T(8,128)(2,1)S(1)} %pad_maximum_fusion.ta_ref), channel_id=1, source_target_pairs={{0,64},{16,80},{32,96},{48,112},{64,128},{80,144},{96,160},{112,17... | collective-permute-start | bytes 786440 | tf_op jit(solution)/shard_map/ppermute | solution.py:317
  55.1 8.7 %collective-permute-start.13 = (bf16[128,1024]{1,0:T(8,128)(2,1)S(1)}, bf16[128,1024]{1,0:T(8,128)(2,1)S(1)}, u32[]{:S(2)}, u32[]{:S(2)}) collective-permute-start(bf16[128,1024]{1,0:T(8,128)(2,1)S(1)} %pad_maximum_fusion.ta_ref), channel_id=1, source_target_pairs={{0,192},{16,208},{32,224},{48,240},{64,0},{80,16},{96,32},{112,48}... | collective-permute-start | bytes 786440 | tf_op jit(solution)/shard_map/ppermute | solution.py:317
  62.0 5.4 %copy-start.4 = (bf16[128,1024]{1,0:T(8,128)(2,1)}, bf16[128,1024]{1,0:T(8,128)(2,1)S(1)}, u32[]{:S(2)}) copy-start(bf16[128,1024]{1,0:T(8,128)(2,1)S(1)} %collective-permute-done.11.tb_ref) | copy-start | bytes 786436
  62.1 5.3 %collective-permute-start.12 = (bf16[64,1024]{1,0:T(8,128)(2,1)S(1)}, bf16[64,1024]{1,0:T(8,128)(2,1)S(1)}, u32[]{:S(2)}, u32[]{:S(2)}) collective-permute-start(bf16[64,1024]{1,0:T(8,128)(2,1)S(1)} %slice.8), channel_id=1, source_target_pairs={{0,64},{16,80},{32,96},{48,112},{64,128},{80,144},{96,160},{112,17... | collective-permute-start | bytes 393224 | tf_op jit(solution)/shard_map/ppermute | solution.py:317
  63.8 3.6 %copy-start.6 = (bf16[128,1024]{1,0:T(8,128)(2,1)}, bf16[128,1024]{1,0:T(8,128)(2,1)S(1)}, u32[]{:S(2)}) copy-start(bf16[128,1024]{1,0:T(8,128)(2,1)S(1)} %collective-permute-done.13.te_ref) | copy-start | bytes 786436
  63.8 6.3 %collective-permute-start.14 = (bf16[64,1024]{1,0:T(8,128)(2,1)S(1)}, bf16[64,1024]{1,0:T(8,128)(2,1)S(1)}, u32[]{:S(2)}, u32[]{:S(2)}) collective-permute-start(bf16[64,1024]{1,0:T(8,128)(2,1)S(1)} %slice.9), channel_id=1, source_target_pairs={{0,192},{16,208},{32,224},{48,240},{64,0},{80,16},{96,32},{112,48}... | collective-permute-start | bytes 393224 | tf_op jit(solution)/shard_map/ppermute | solution.py:317
  67.4 0.6 copy-start.9
  70.1 0.7 copy-start.11
  70.7 1.0 %copy-start.5 = (bf16[128,1024]{1,0:T(8,128)(2,1)S(1)}, bf16[128,1024]{1,0:T(8,128)(2,1)}, u32[]{:S(2)}) copy-start(bf16[128,1024]{1,0:T(8,128)(2,1)} %copy-done.4) | copy-start | bytes 786436
  71.7 0.9 %copy-start.7 = (bf16[128,1024]{1,0:T(8,128)(2,1)S(1)}, bf16[128,1024]{1,0:T(8,128)(2,1)}, u32[]{:S(2)}) copy-start(bf16[128,1024]{1,0:T(8,128)(2,1)} %copy-done.6) | copy-start | bytes 786436
  72.6 0.9 copy-start.10
  73.5 0.9 copy-start.12
  76.6 15.7 %all-to-all-start.1 = ((f32[16,16,128]{2,1,0:T(8,128)}), f32[16,16,128]{2,1,0:T(8,128)S(1)}, u32[]{:S(2)}, u32[]{:S(2)}) async-start(f32[16,16,128]{2,1,0:T(8,128)} %state.1), calls=%async_computation.1 | async-start | bytes 262144 | tf_op jit(solution)/shard_map/all_to_all | solution.py:446
  83.9 1.0 %copy-start.8 = (bf16[128,1024]{1,0:T(8,128)(2,1)S(1)}, bf16[128,1024]{1,0:T(8,128)(2,1)}, u32[]{:S(2)}) copy-start(bf16[128,1024]{1,0:T(8,128)(2,1)} %get-tuple-element.40.gate_ref) | copy-start | bytes 786436

commit v3 on v1

--- a/solution.py
+++ b/solution.py
@@ -57,57 +57,14 @@
     return (0, one, one + blocks_ref[0, 1])
 
 
-def project_kernel(blocks_ref, tail_ref, x_ref, gain_ref, w_ref, gate_ref, extra_ref, *refs):
-    out_refs, weights, sems = refs[:HEADS], refs[HEADS], refs[HEADS + 1]
-    me = lax.axis_index("seq")
-    order = FAR + NEAR
-
-    def copies(at):
-        head = head_of(me) ^ order[at]
-        return [
-            pltpu.make_async_copy(
-                w_ref.at[:, pl.ds(pl.multiple_of((group * HEADS + head) * HD, HD), HD)],
-                weights.at[at, :, group * HD : (group + 1) * HD],
-                sems.at[at, group],
-            )
-            for group in range(4)
-        ]
-
-    for at in range(HEADS):
-        for copy in copies(at):
-            copy.start()
-    normed = (layer_norm(x_ref[...].astype(jnp.float32)) * gain_ref[...]).astype(jnp.bfloat16)
-    for at, out_ref in enumerate(out_refs):
-        for copy in copies(at):
-            copy.wait()
-        parts = silu(jnp.dot(normed, weights[at], preferred_element_type=jnp.float32))
-        head = head_of(me) ^ order[at]
-        gate_ref[:, pl.ds(pl.multiple_of(head * HD, HD), HD)] = parts[:, :HD].astype(jnp.bfloat16)
-        out_ref[ROW_K:ROW_V, :] = parts[:, 2 * HD : 3 * HD].T.astype(jnp.bfloat16)
-        out_ref[ROW_V:ROW_Q, :] = parts[:, 3 * HD :].astype(jnp.bfloat16)
-        out_ref[ROW_Q:ROWS_A, :] = parts[:, HD : 2 * HD].astype(jnp.bfloat16)
-
-    starts = user_starts(blocks_ref)
-    last = jnp.int32(-1)
-    for user in range(USERS):
-        last = jnp.where(starts[user] + blocks_ref[0, user] - 1 == me, tail_ref[0, user] - 1, last)
-    pick = (lax.broadcasted_iota(jnp.int32, (16, BLK), 1) == last).astype(jnp.bfloat16)
-    gate_row = jnp.dot(pick, gate_ref[...], preferred_element_type=jnp.float32)[0:1]
-    token_row = jnp.dot(pick, x_ref[...], preferred_element_type=jnp.float32)[0:1]
-    pieces = [row[:, h * HD : (h + 1) * HD] for row in (gate_row, token_row) for h in range(HEADS)]
-    extra_ref[...] = jnp.concatenate(pieces, axis=0).astype(jnp.bfloat16)
-
-
-def prepare_kernel(
-    blocks_ref, slope_ref, ids_ref, map_ref, bias_ref, list_ref, place_ref
-):
+def prepare(blocks_ref, slope_ref, ids_ref, map_ref, bias_ref, list_ref, place_ref):
     me, dp = lax.axis_index("seq"), lax.axis_index("dp")
     starts = user_starts(blocks_ref)
     slope = slope_ref[head_of(me)]
     offset = lax.broadcasted_iota(jnp.int32, (BLK, BLK), 0) - lax.broadcasted_iota(jnp.int32, (BLK, BLK), 1)
     for d in range(MAXD):
         gap = offset + d * BLK
-        table = slope * jnp.log1p(jnp.maximum(gap, 0).astype(jnp.float32))
+        table = slope * jnp.log(jnp.maximum(gap + 1, 1).astype(jnp.float32))
         bias_ref[d] = jnp.where(gap >= 0, table, MASKED) if d == 0 else table
 
     def fill(t, counts):
@@ -150,6 +107,63 @@
         source = (shard // 4) * 8 + set_of(end) * 4 + shard % 4
         place_ref[2 * user : 2 * user + 1, :] = source * 16 + user * 4 + x_rel
         place_ref[2 * user + 1 : 2 * user + 2, :] = lane
+
+
+def project_kernel(
+    blocks_ref,
+    tail_ref,
+    slope_ref,
+    ids_ref,
+    map_ref,
+    x_ref,
+    gain_ref,
+    w_ref,
+    gate_ref,
+    extra_ref,
+    bias_ref,
+    list_ref,
+    place_ref,
+    *refs,
+):
+    out_refs, weights, sems = refs[:HEADS], refs[HEADS], refs[HEADS + 1]
+    me = lax.axis_index("seq")
+    order = FAR + NEAR
+
+    def copies(at):
+        head = head_of(me) ^ order[at]
+        return [
+            pltpu.make_async_copy(
+                w_ref.at[:, pl.ds(pl.multiple_of((group * HEADS + head) * HD, HD), HD)],
+                weights.at[at, :, group * HD : (group + 1) * HD],
+                sems.at[at, group],
+            )
+            for group in range(4)
+        ]
+
+    for at in range(HEADS):
+        for copy in copies(at):
+            copy.start()
+    normed = (layer_norm(x_ref[...].astype(jnp.float32)) * gain_ref[...]).astype(jnp.bfloat16)
+    prepare(blocks_ref, slope_ref, ids_ref, map_ref, bias_ref, list_ref, place_ref)
+    for at, out_ref in enumerate(out_refs):
+        for copy in copies(at):
+            copy.wait()
+        parts = silu(jnp.dot(normed, weights[at], preferred_element_type=jnp.float32))
+        head = head_of(me) ^ order[at]
+        gate_ref[:, pl.ds(pl.multiple_of(head * HD, HD), HD)] = parts[:, :HD].astype(jnp.bfloat16)
+        out_ref[ROW_K:ROW_V, :] = parts[:, 2 * HD : 3 * HD].T.astype(jnp.bfloat16)
+        out_ref[ROW_V:ROW_Q, :] = parts[:, 3 * HD :].astype(jnp.bfloat16)
+        out_ref[ROW_Q:ROWS_A, :] = parts[:, HD : 2 * HD].astype(jnp.bfloat16)
+
+    starts = user_starts(blocks_ref)
+    last = jnp.int32(-1)
+    for user in range(USERS):
+        last = jnp.where(starts[user] + blocks_ref[0, user] - 1 == me, tail_ref[0, user] - 1, last)
+    pick = (lax.broadcasted_iota(jnp.int32, (16, BLK), 1) == last).astype(jnp.bfloat16)
+    gate_row = jnp.dot(pick, gate_ref[...], preferred_element_type=jnp.float32)[0:1]
+    token_row = jnp.dot(pick, x_ref[...], preferred_element_type=jnp.float32)[0:1]
+    pieces = [row[:, h * HD : (h + 1) * HD] for row in (gate_row, token_row) for h in range(HEADS)]
+    extra_ref[...] = jnp.concatenate(pieces, axis=0).astype(jnp.bfloat16)
 
 
 def run_pairs(list_ref, which, query, keys, values, bias_ref, acc):
@@ -237,7 +251,7 @@
         out_ref[t, ROW_X:ROWS_B, :] = extra_ref[...]
 
 
-def state_kernel(blocks_ref, mixed_ref, gain_ref, w_ref, ta_ref, tb_ref, tc_ref, td_ref, score_ref):
+def state_kernel(blocks_ref, mixed_ref, gain_ref, w_ref, ta_ref, tb_ref, tc_ref, td_ref, te_ref, score_ref):
     starts = user_starts(blocks_ref)
     tail = jnp.concatenate([mixed_ref[h, ROW_E:ROW_X, :].astype(jnp.float32) for h in range(HEADS)], axis=1)
     gates, tokens = [], []
@@ -253,8 +267,9 @@
     states = (token_tail + jnp.dot(gated, w_ref[...], preferred_element_type=jnp.float32)).astype(jnp.bfloat16)
     parts = [
         lax.dot_general(states, t_ref[...], (((1,), (1,)), ((), ())), preferred_element_type=jnp.float32)
-        for t_ref in (ta_ref, tb_ref, tc_ref, td_ref)
+        for t_ref in (ta_ref, tb_ref, tc_ref, td_ref, te_ref)
     ]
+    parts[2:4] = [jnp.concatenate(parts[2:4], axis=1)]
     rows = [part[user : user + 1] for user in range(USERS) for part in parts]
     block = jnp.concatenate(rows + [jnp.zeros((4, 128), jnp.float32)], axis=0)
     for to in range(NSEQ):
@@ -329,35 +344,42 @@
     seq = lax.axis_index("seq")
     mine = head_of(seq)
 
-    gate, extra, *sent = pl.pallas_call(
+    gate, extra, bias, pairs, places, *sent = pl.pallas_call(
         project_kernel,
-        in_specs=[smem(), smem(), vmem(), vmem(), pl.BlockSpec(memory_space=pltpu.HBM)],
-        out_specs=[vmem()] * (2 + HEADS),
-        out_shape=[pltpu.HBM((BLK, D), jnp.bfloat16), sds((16, HD))] + [sds((ROWS_A, HD))] * HEADS,
+        in_specs=[smem(), smem(), smem()] + [vmem()] * 4 + [pl.BlockSpec(memory_space=pltpu.HBM)],
+        out_specs=[vmem()] * 3 + [smem()] + [vmem()] * (1 + HEADS),
+        out_shape=[
+            pltpu.HBM((BLK, D), jnp.bfloat16),
+            sds((16, HD)),
+            pltpu.HBM((MAXD, BLK, BLK), jnp.float32),
+            sds((2 * LIST,), jnp.int32),
+            sds((8, 64), jnp.int32),
+        ]
+        + [sds((ROWS_A, HD))] * HEADS,
         scratch_shapes=[pltpu.VMEM((HEADS, D, 4 * HD), jnp.bfloat16), pltpu.SemaphoreType.DMA((HEADS, 4))],
         name="project",
         cost_estimate=cost(2 * BLK * D * 4 * D, 10 << 20),
         compiler_params=GRANT,
-    )(*(in_hbm(value) for value in (hist_blocks, hist_tail, x_rows, in_gain[None, :], w_proj)))
+    )(
+        *(
+            in_hbm(value)
+            for value in (
+                hist_blocks,
+                hist_tail,
+                rab_slope,
+                beam_nodes,
+                subtree_map[None, :],
+                x_rows,
+                in_gain[None, :],
+                w_proj,
+            )
+        )
+    )
     far_got, near_got = [], [sent[4]]
     for q, value in zip(FAR, sent[:4]):
         far_got.append(seq_xor(value, spread(q)))
     for q, value in zip(NEAR[1:], sent[5:]):
         near_got.append(seq_xor(value, spread(q)))
-
-    bias, pairs, places = pl.pallas_call(
-        prepare_kernel,
-        in_specs=[smem(), smem(), vmem(), vmem()],
-        out_specs=[vmem(), smem(), vmem()],
-        out_shape=[
-            sds((MAXD, BLK, BLK), jnp.float32),
-            sds((2 * LIST,), jnp.int32),
-            sds((8, 64), jnp.int32),
-        ],
-        name="prepare",
-        cost_estimate=cost(1 << 28, 4 << 20),
-        compiler_params=GRANT,
-    )(hist_blocks, rab_slope, beam_nodes, subtree_map[None, :])
 
     def sort(got):
         return pl.pallas_call(
@@ -377,9 +399,11 @@
     own = lax.dynamic_slice_in_dim(node_table, mine * 32, 32, 0)
     pair = jnp.concatenate([own, dp_shift(own, lambda i: i ^ 2)], axis=0)
     quad = jnp.concatenate([pair, dp_shift(pair, lambda i: i ^ 1)], axis=0)
-    table = [quad]
-    for n in (1, 2, 3):
-        table.append(dp_shift(quad, lambda i, n=n: (i + 4 * n) % 16))
+    below = dp_shift(quad, lambda i: (i + 4) % 16)
+    above = dp_shift(quad, lambda i: (i + 12) % 16)
+    opposite_first = dp_shift(below[:64], lambda i: (i + 4) % 16)
+    opposite_last = dp_shift(above[64:], lambda i: (i + 12) % 16)
+    table = [quad, below, opposite_first, opposite_last, above]
 
     part, queries = pl.pallas_call(
         attend_first_kernel,
@@ -407,7 +431,7 @@
 
     sent = pl.pallas_call(
         state_kernel,
-        in_specs=[smem()] + [vmem()] * 7,
+        in_specs=[smem()] + [vmem()] * 8,
         out_specs=vmem(),
         out_shape=pltpu.HBM((NSEQ, 16, 128), jnp.float32),
         name="state",

time: 103 us -> 95 us (0.922)
  the two profiles are of different devices: /device:TPU:0 before, /device:TPU:6 now
where the time goes in v3:
time: 95 us; the launch traced here: 94.5 us
  starting transfers between devices  46.6 us (49%)
  waiting for transfers between devices  20.3 us (21%)
  Pallas kernels  17 us (18%)
  local copies, waits for them, and re-layouts  8.19 us (9%)
  other arithmetic  1.61 us (2%)
    ppermute x9, starting transfers between devices, seq_xor(): return lax.ppermute(value, 'seq', [(i, i ^ apart) for i in range(NSEQ)])  18.1 us
    ppermute x6, starting transfers between devices, dp_shift(): return lax.ppermute(value, 'dp', [(i, move(i)) for i in range(16)])  11.8 us
    ppermute x6, waiting for transfers between devices, dp_shift(): return lax.ppermute(value, 'dp', [(i, move(i)) for i in range(16)])  10.5 us
    all_to_all x1, starting transfers between devices, layer(): lax.all_to_all(back, 'seq', 0, 0, tiled=True, axis_index_groups=SETS)  8.88 us
    unnamed x36, local copies, waits for them, and re-layouts  8.16 us
    all_to_all x1, starting transfers between devices, layer(): scores = lax.all_to_all(sent, 'seq', 0, 0, tiled=True)  7.74 us
    pallas_call x1, Pallas kernels, layer(): pl.pallas_call(project_kernel, in_specs=[smem(), smem(), smem()] + [vmem(...  7.53 us
    all_to_all x1, waiting for transfers between devices, layer(): scores = lax.all_to_all(sent, 'seq', 0, 0, tiled=True)  6.1 us
  transfers between devices with their start and end apart: 17, of which 8 were waited for; matrix products, arithmetic and copies ran while one was open for 2% of the time, Pallas kernels for 7%

profile of v3, /device:TPU:6, one launch (start us, length us, event | category | flops | bytes accessed | tf_op | source)
XLA Modules:
  0.0 94.5 jit_solution(9793986738796909863)
XLA Ops:
  0.6 0.0 copy-start
  0.7 7.5 %project.1 = (bf16[128,1024]{1,0:T(8,128)(2,1)}, bf16[16,128]{1,0:T(8,128)(2,1)S(1)}, f32[10,128,128]{2,1,0:T(8,128)}, s32[256]{0:T(256)S(1)}, s32[8,64]{1,0:T(8...) custom-call(s32[1,3]{1,0:T(1,128)} %blocks_ref.5, ...), custom_call_target="tpu_custom_call" | custom-call | flops 1073741824 | bytes 10485760 | tf_op jit(solution)/shard_map/project/pallas_call | solution.py:347
  8.2 0.0 copy-start.1
  8.2 0.0 copy-start.12
  8.2 2.0 %collective-permute-start = (bf16[384,128]{1,0:T(8,128)(2,1)}, bf16[384,128]{1,0:T(8,128)(2,1)S(1)}, u32[]{:S(2)}, u32[]{:S(2)}) collective-permute-start(bf16[384,128]{1,0:T(8,128)(2,1)} %get-tuple-element.24), channel_id=1, source_target_pairs={{0,1},{1,0},{2,3},{3,2},{4,5},{5,4},{6,7},{7,6},{8,9},{9,8},{10,11... | collective-permute-start | bytes 294920 | tf_op jit(solution)/shard_map/ppermute | solution.py:319
  10.2 3.2 %collective-permute-start.1 = (bf16[384,128]{1,0:T(8,128)(2,1)}, bf16[384,128]{1,0:T(8,128)(2,1)S(1)}, u32[]{:S(2)}, u32[]{:S(2)}) collective-permute-start(bf16[384,128]{1,0:T(8,128)(2,1)} %get-tuple-element.25), channel_id=1, source_target_pairs={{0,8},{1,9},{2,10},{3,11},{4,12},{5,13},{6,14},{7,15},{8,0},{9,1},... | collective-permute-start | bytes 294920 | tf_op jit(solution)/shard_map/ppermute | solution.py:319
  13.4 0.0 collective-permute-start.2
  13.4 3.3 %collective-permute-start.3 = (bf16[384,128]{1,0:T(8,128)(2,1)}, bf16[384,128]{1,0:T(8,128)(2,1)S(1)}, u32[]{:S(2)}, u32[]{:S(2)}) collective-permute-start(bf16[384,128]{1,0:T(8,128)(2,1)} %get-tuple-element.28), channel_id=1, source_target_pairs={{0,2},{1,3},{2,0},{3,1},{4,6},{5,7},{6,4},{7,5},{8,10},{9,11},{10,... | collective-permute-start | bytes 294920 | tf_op jit(solution)/shard_map/ppermute | solution.py:319
  16.7 1.2 %collective-permute-start.4 = (bf16[384,128]{1,0:T(8,128)(2,1)}, bf16[384,128]{1,0:T(8,128)(2,1)S(1)}, u32[]{:S(2)}, u32[]{:S(2)}) collective-permute-start(bf16[384,128]{1,0:T(8,128)(2,1)} %get-tuple-element.29), channel_id=1, source_target_pairs={{0,3},{1,2},{2,1},{3,0},{4,7},{5,6},{6,5},{7,4},{8,11},{9,10},{10,... | collective-permute-start | bytes 294920 | tf_op jit(solution)/shard_map/ppermute | solution.py:319
  17.9 4.7 %collective-permute-start.5 = (bf16[384,128]{1,0:T(8,128)(2,1)}, bf16[384,128]{1,0:T(8,128)(2,1)S(1)}, u32[]{:S(2)}, u32[]{:S(2)}) collective-permute-start(bf16[384,128]{1,0:T(8,128)(2,1)} %get-tuple-element.30), channel_id=1, source_target_pairs={{0,10},{1,11},{2,8},{3,9},{4,14},{5,15},{6,12},{7,13},{8,2},{9,3},... | collective-permute-start | bytes 294920 | tf_op jit(solution)/shard_map/ppermute | solution.py:319
  22.6 0.0 collective-permute-done.1.refs_2_
  22.6 1.2 %collective-permute-start.6 = (bf16[384,128]{1,0:T(8,128)(2,1)S(1)}, bf16[384,128]{1,0:T(8,128)(2,1)S(1)}, u32[]{:S(2)}, u32[]{:S(2)}) collective-permute-start(bf16[384,128]{1,0:T(8,128)(2,1)S(1)} %get-tuple-element.31), channel_id=1, source_target_pairs={{0,11},{1,10},{2,9},{3,8},{4,15},{5,14},{6,13},{7,12},{8,3},{9,2},... | collective-permute-start | bytes 294920 | tf_op jit(solution)/shard_map/ppermute | solution.py:319
  23.8 0.0 collective-permute-done.2.refs_3_
  23.8 1.6 %collective-permute-start.7 = (bf16[4,256,128]{2,1,0:T(8,128)(2,1)S(1)}, bf16[4,256,128]{2,1,0:T(8,128)(2,1)S(1)}, u32[]{:S(2)}, u32[]{:S(2)}) collective-permute-start(bf16[4,256,128]{2,1,0:T(8,128)(2,1)S(1)} %get-tuple-element.27.near_ref), channel_id=1, source_target_pairs={{0,4},{1,5},{2,6},{3,7},{4,0},{5,1},{6,2},{7,3},{8,12},{9,13},{10,... | collective-permute-start | bytes 786440 | tf_op jit(solution)/shard_map/ppermute | solution.py:319
  25.4 2.3 %collective-permute-done.3.refs_0_ = bf16[384,128]{1,0:T(8,128)(2,1)S(1)} collective-permute-done((bf16[384,128]{1,0:T(8,128)(2,1)}, bf16[384,128]{1,0:T(8,128)(2,1)S(1)}, u32[]{:S(2)}, u32[]{:S(2)}) %collective-permute-start.3) | collective-permute-done | bytes 98336 | tf_op jit(solution)/shard_map/ppermute | solution.py:319
  27.7 7.4 %collective-permute-start.9 = (bf16[32,1024]{1,0:T(8,128)(2,1)S(1)}, bf16[32,1024]{1,0:T(8,128)(2,1)S(1)}, u32[]{:S(2)}, u32[]{:S(2)}) collective-permute-start(bf16[32,1024]{1,0:T(8,128)(2,1)S(1)} %constant_dynamic-slice_fusion), channel_id=1, source_target_pairs={{0,32},{16,48},{32,0},{48,16},{64,96},{80,112},{96,64},{112,80},{1... | collective-permute-start | bytes 196616 | tf_op jit(solution)/shard_map/ppermute | solution.py:315
  35.1 0.0 collective-permute-done.4.refs_1_
  35.1 1.0 %collective-permute-done.5.refs_2_ = bf16[384,128]{1,0:T(8,128)(2,1)S(1)} collective-permute-done((bf16[384,128]{1,0:T(8,128)(2,1)}, bf16[384,128]{1,0:T(8,128)(2,1)S(1)}, u32[]{:S(2)}, u32[]{:S(2)}) %collective-permute-start.5) | collective-permute-done | bytes 98336 | tf_op jit(solution)/shard_map/ppermute | solution.py:319
  36.1 1.0 %collective-permute-start.8 = (bf16[4,256,128]{2,1,0:T(8,128)(2,1)S(1)}, bf16[4,256,128]{2,1,0:T(8,128)(2,1)S(1)}, u32[]{:S(2)}, u32[]{:S(2)}) collective-permute-start(bf16[4,256,128]{2,1,0:T(8,128)(2,1)S(1)} %get-tuple-element.32.far_ref), channel_id=1, source_target_pairs={{0,4},{1,5},{2,6},{3,7},{4,0},{5,1},{6,2},{7,3},{8,12},{9,13},{10,... | collective-permute-start | bytes 786440 | tf_op jit(solution)/shard_map/ppermute | solution.py:319
  37.2 0.2 collective-permute-done.9
  37.4 0.7 pad_maximum_fusion.1
  38.1 1.1 %copy-done.15 = f32[10,128,128]{2,1,0:T(8,128)S(1)} copy-done((f32[10,128,128]{2,1,0:T(8,128)S(1)}, f32[10,128,128]{2,1,0:T(8,128)}, u32[]{:S(2)}) %copy-start.15) | copy-done | bytes 655384
  39.2 3.1 %attend_first.1 = (f32[8,128,128]{2,1,0:T(8,128)S(1)}, bf16[8,128,128]{2,1,0:T(8,128)(2,1)S(1)}) custom-call(s32[256]{0:T(256)S(1)} %get-tuple-element.21.list_ref, f32[10,128,128]{2,1,0:T(8,128)S(1)} %copy-done.15, bf16[4,256,128]{2,1,0:T(8,128)(2,1)S(1)} %get-tuple-element.27.near_ref, bf16[4,256,128]{2,1,0:T(8,128)(2,1)S(1)} %get-tuple-element.32.far_ref, ...), custom_call_target="tpu_custom_call" | custom-call | flops 2147483648 | bytes 4194304 | tf_op jit(solution)/shard_map/attend_first/pallas_call | solution.py:408
  42.3 0.3 collective-permute-done.8.cross_ref
  42.6 1.1 %copy-done.16 = f32[10,128,128]{2,1,0:T(8,128)S(1)} copy-done((f32[10,128,128]{2,1,0:T(8,128)S(1)}, f32[10,128,128]{2,1,0:T(8,128)}, u32[]{:S(2)}) %copy-start.16) | copy-done | bytes 655384
  43.7 1.9 %attend_last.1 = bf16[8,160,128]{2,1,0:T(8,128)(2,1)} custom-call(s32[1,3]{1,0:T(1,128)S(1)} %copy-done.13, s32[1,3]{1,0:T(1,128)S(1)} %copy-done.14, s32[256]{0:T(256)S(1)} %get-tuple-element.21.list_ref, f32[10,128,128]{2,1,0:T(8,128)S(1)} %copy-done.16, bf16[8,128,128]{2,1,0:T(8,128)(2,1)S(1)} %get-tuple-element.35.queries_ref, ...), custom_call_target="tpu_custom_call" | custom-call | flops 1073741824 | bytes 2097152 | tf_op jit(solution)/shard_map/attend_last/pallas_call | solution.py:419
  45.6 8.9 %all-to-all-start = ((bf16[8,160,128]{2,1,0:T(8,128)(2,1)}), bf16[8,160,128]{2,1,0:T(8,128)(2,1)S(1)}, u32[]{:S(2)}, u32[]{:S(2)}) async-start(bf16[8,160,128]{2,1,0:T(8,128)(2,1)} %attend_last.1), calls=%async_computation | async-start | bytes 655360 | tf_op jit(solution)/shard_map/all_to_all | solution.py:430
  54.5 0.9 pad_maximum_fusion.ta_ref
  55.4 0.3 collective-permute-start.11
  55.7 1.8 %collective-permute-start.13 = (bf16[128,1024]{1,0:T(8,128)(2,1)S(1)}, bf16[128,1024]{1,0:T(8,128)(2,1)S(1)}, u32[]{:S(2)}, u32[]{:S(2)}) collective-permute-start(bf16[128,1024]{1,0:T(8,128)(2,1)S(1)} %pad_maximum_fusion.ta_ref), channel_id=1, source_target_pairs={{0,192},{16,208},{32,224},{48,240},{64,0},{80,16},{96,32},{112,48}... | collective-permute-start | bytes 786440 | tf_op jit(solution)/shard_map/ppermute | solution.py:315
  57.5 5.0 %collective-permute-done.11.tb_ref = bf16[128,1024]{1,0:T(8,128)(2,1)S(1)} collective-permute-done((bf16[128,1024]{1,0:T(8,128)(2,1)S(1)}, bf16[128,1024]{1,0:T(8,128)(2,1)S(1)}, u32[]{:S(2)}, u32[]{:S(2)}) %collective-permute-start.11) | collective-permute-done | bytes 262176 | tf_op jit(solution)/shard_map/ppermute | solution.py:315
  62.5 2.0 %collective-permute-start.12 = (bf16[64,1024]{1,0:T(8,128)(2,1)S(1)}, bf16[64,1024]{1,0:T(8,128)(2,1)S(1)}, u32[]{:S(2)}, u32[]{:S(2)}) collective-permute-start(bf16[64,1024]{1,0:T(8,128)(2,1)S(1)} %slice.8), channel_id=1, source_target_pairs={{0,64},{16,80},{32,96},{48,112},{64,128},{80,144},{96,160},{112,17... | collective-permute-start | bytes 393224 | tf_op jit(solution)/shard_map/ppermute | solution.py:315
  64.6 0.3 collective-permute-start.14
  64.9 2.8 %collective-permute-done.12.tc_ref = bf16[64,1024]{1,0:T(8,128)(2,1)S(1)} collective-permute-done((bf16[64,1024]{1,0:T(8,128)(2,1)S(1)}, bf16[64,1024]{1,0:T(8,128)(2,1)S(1)}, u32[]{:S(2)}, u32[]{:S(2)}) %collective-permute-start.12) | collective-permute-done | bytes 131104 | tf_op jit(solution)/shard_map/ppermute | solution.py:315
  67.8 0.6 copy-done.8
  68.4 2.4 %collective-permute-done.14.td_ref = bf16[64,1024]{1,0:T(8,128)(2,1)S(1)} collective-permute-done((bf16[64,1024]{1,0:T(8,128)(2,1)S(1)}, bf16[64,1024]{1,0:T(8,128)(2,1)S(1)}, u32[]{:S(2)}, u32[]{:S(2)}) %collective-permute-start.14) | collective-permute-done | bytes 131104 | tf_op jit(solution)/shard_map/ppermute | solution.py:315
  70.8 0.7 copy-done.10
  71.5 0.9 copy-done.4
  72.4 0.9 %copy-done.6 = bf16[128,1024]{1,0:T(8,128)(2,1)S(1)} copy-done((bf16[128,1024]{1,0:T(8,128)(2,1)S(1)}, bf16[128,1024]{1,0:T(8,128)(2,1)}, u32[]{:S(2)}) %copy-start.6) | copy-done | bytes 262168
  73.4 0.9 copy-done.9
  74.3 0.9 copy-done.11
  75.2 2.1 %state.1 = f32[16,16,128]{2,1,0:T(8,128)} custom-call(s32[1,3]{1,0:T(1,128)S(1)} %copy-done.13, bf16[8,160,128]{2,1,0:T(8,128)(2,1)S(1)} %all-to-all-done.mixed_ref, f32[1,1024]{1,0:T(1,128)S(1)} %bitcast.7, bf16[1024,1024]{1,0:T(8,128)(2,1)S(1)} %copy-done.1, bf16[128,1024]{1,0:T(8,128)(2,1)S(1)} %pad_maximum_fusion.ta_ref, ...), custom_call_target="tpu_custom_call" | custom-call | flops 33554432 | bytes 3145728 | tf_op jit(solution)/shard_map/state/pallas_call | solution.py:432
  77.3 7.7 %all-to-all-start.1 = ((f32[16,16,128]{2,1,0:T(8,128)}), f32[16,16,128]{2,1,0:T(8,128)S(1)}, u32[]{:S(2)}, u32[]{:S(2)}) async-start(f32[16,16,128]{2,1,0:T(8,128)} %state.1), calls=%async_computation.1 | async-start | bytes 262144 | tf_op jit(solution)/shard_map/all_to_all | solution.py:441
  85.1 0.0 copy-start.7
  85.1 0.9 copy-done.7
  86.0 1.3 %layer.1 = bf16[128,1024]{1,0:T(8,128)(2,1)} custom-call(bf16[8,160,128]{2,1,0:T(8,128)(2,1)S(1)} %all-to-all-done.mixed_ref, bf16[128,1024]{1,0:T(8,128)(2,1)S(1)} %copy-done.7, bf16[128,1024]{1,0:T(8,128)(2,1)S(1)} %bitcast.6, f32[1,1024]{1,0:T(1,128)S(1)} %bitcast.8, bf16[1024,1024]{1,0:T(8,128)(2,1)S(1)} %copy-done.1), custom_call_target="tpu_custom_call" | custom-call | flops 268435456 | bytes 3145728 | tf_op jit(solution)/shard_map/layer/pallas_call | solution.py:443
  87.4 6.1 %all-to-all-done.1.score_ref = f32[16,16,128]{2,1,0:T(8,128)S(1)} async-done(((f32[16,16,128]{2,1,0:T(8,128)}), f32[16,16,128]{2,1,0:T(8,128)S(1)}, u32[]{:S(2)}, u32[]{:S(2)}) %all-to-all-start.1) | async-done | bytes 131104 | tf_op jit(solution)/shard_map/all_to_all | solution.py:441
  93.5 1.1 %pick.1 = f32[3,64]{1,0:T(4,128)} custom-call(f32[16,16,128]{2,1,0:T(8,128)S(1)} %all-to-all-done.1.score_ref, s32[8,64]{1,0:T(8,128)S(1)} %get-tuple-element.39.place_ref), custom_call_target="tpu_custom_call" | custom-call | flops 1048576 | bytes 131072 | tf_op jit(solution)/shard_map/pick/pallas_call | solution.py:453
  (35 shorter events, 0.1 us)
Async XLA Ops:
  0.6 24.8 %copy-start = (bf16[256,1024]{1,0:T(8,128)(2,1)S(1)}, bf16[256,1024]{1,0:T(8,128)(2,1)}, u32[]{:S(2)}) copy-start(bf16[256,1024]{1,0:T(8,128)(2,1)} %param.19) | copy-start | bytes 1572868
  0.6 42.0 %copy-start.13 = (s32[1,3]{1,0:T(1,128)S(1)}, s32[1,3]{1,0:T(1,128)}, u32[]{:S(2)}) copy-start(s32[1,3]{1,0:T(1,128)} %blocks_ref.5) | copy-start | bytes 40
  0.7 41.9 %copy-start.14 = (s32[1,3]{1,0:T(1,128)S(1)}, s32[1,3]{1,0:T(1,128)}, u32[]{:S(2)}) copy-start(s32[1,3]{1,0:T(1,128)} %tail_ref.3) | copy-start | bytes 40
  8.2 63.3 %copy-start.1 = (bf16[1024,1024]{1,0:T(8,128)(2,1)S(1)}, bf16[1024,1024]{1,0:T(8,128)(2,1)}, u32[]{:S(2)}) copy-start(bf16[1024,1024]{1,0:T(8,128)(2,1)} %w_ref.5) | copy-start | bytes 6291460
  8.2 63.3 %copy-start.12 = (f32[1024]{0:T(1024)S(1)}, f32[1024]{0:T(1024)}, u32[]{:S(2)}) copy-start(f32[1024]{0:T(1024)} %param.14) | copy-start | bytes 12292
  8.2 9.7 %collective-permute-start = (bf16[384,128]{1,0:T(8,128)(2,1)}, bf16[384,128]{1,0:T(8,128)(2,1)S(1)}, u32[]{:S(2)}, u32[]{:S(2)}) collective-permute-start(bf16[384,128]{1,0:T(8,128)(2,1)} %get-tuple-element.24), channel_id=1, source_target_pairs={{0,1},{1,0},{2,3},{3,2},{4,5},{5,4},{6,7},{7,6},{8,9},{9,8},{10,11... | collective-permute-start | bytes 294920 | tf_op jit(solution)/shard_map/ppermute | solution.py:319
  10.2 12.4 %collective-permute-start.1 = (bf16[384,128]{1,0:T(8,128)(2,1)}, bf16[384,128]{1,0:T(8,128)(2,1)S(1)}, u32[]{:S(2)}, u32[]{:S(2)}) collective-permute-start(bf16[384,128]{1,0:T(8,128)(2,1)} %get-tuple-element.25), channel_id=1, source_target_pairs={{0,8},{1,9},{2,10},{3,11},{4,12},{5,13},{6,14},{7,15},{8,0},{9,1},... | collective-permute-start | bytes 294920 | tf_op jit(solution)/shard_map/ppermute | solution.py:319
  13.4 10.3 %collective-permute-start.2 = (bf16[384,128]{1,0:T(8,128)(2,1)S(1)}, bf16[384,128]{1,0:T(8,128)(2,1)S(1)}, u32[]{:S(2)}, u32[]{:S(2)}) collective-permute-start(bf16[384,128]{1,0:T(8,128)(2,1)S(1)} %get-tuple-element.26), channel_id=1, source_target_pairs={{0,9},{1,8},{2,11},{3,10},{4,13},{5,12},{6,15},{7,14},{8,1},{9,0},... | collective-permute-start | bytes 294920 | tf_op jit(solution)/shard_map/ppermute | solution.py:319
  13.4 14.3 %collective-permute-start.3 = (bf16[384,128]{1,0:T(8,128)(2,1)}, bf16[384,128]{1,0:T(8,128)(2,1)S(1)}, u32[]{:S(2)}, u32[]{:S(2)}) collective-permute-start(bf16[384,128]{1,0:T(8,128)(2,1)} %get-tuple-element.28), channel_id=1, source_target_pairs={{0,2},{1,3},{2,0},{3,1},{4,6},{5,7},{6,4},{7,5},{8,10},{9,11},{10,... | collective-permute-start | bytes 294920 | tf_op jit(solution)/shard_map/ppermute | solution.py:319
  16.7 18.4 %collective-permute-start.4 = (bf16[384,128]{1,0:T(8,128)(2,1)}, bf16[384,128]{1,0:T(8,128)(2,1)S(1)}, u32[]{:S(2)}, u32[]{:S(2)}) collective-permute-start(bf16[384,128]{1,0:T(8,128)(2,1)} %get-tuple-element.29), channel_id=1, source_target_pairs={{0,3},{1,2},{2,1},{3,0},{4,7},{5,6},{6,5},{7,4},{8,11},{9,10},{10,... | collective-permute-start | bytes 294920 | tf_op jit(solution)/shard_map/ppermute | solution.py:319
  17.9 18.2 %collective-permute-start.5 = (bf16[384,128]{1,0:T(8,128)(2,1)}, bf16[384,128]{1,0:T(8,128)(2,1)S(1)}, u32[]{:S(2)}, u32[]{:S(2)}) collective-permute-start(bf16[384,128]{1,0:T(8,128)(2,1)} %get-tuple-element.30), channel_id=1, source_target_pairs={{0,10},{1,11},{2,8},{3,9},{4,14},{5,15},{6,12},{7,13},{8,2},{9,3},... | collective-permute-start | bytes 294920 | tf_op jit(solution)/shard_map/ppermute | solution.py:319
  22.6 13.5 %collective-permute-start.6 = (bf16[384,128]{1,0:T(8,128)(2,1)S(1)}, bf16[384,128]{1,0:T(8,128)(2,1)S(1)}, u32[]{:S(2)}, u32[]{:S(2)}) collective-permute-start(bf16[384,128]{1,0:T(8,128)(2,1)S(1)} %get-tuple-element.31), channel_id=1, source_target_pairs={{0,11},{1,10},{2,9},{3,8},{4,15},{5,14},{6,13},{7,12},{8,3},{9,2},... | collective-permute-start | bytes 294920 | tf_op jit(solution)/shard_map/ppermute | solution.py:319
  23.8 14.3 %collective-permute-start.7 = (bf16[4,256,128]{2,1,0:T(8,128)(2,1)S(1)}, bf16[4,256,128]{2,1,0:T(8,128)(2,1)S(1)}, u32[]{:S(2)}, u32[]{:S(2)}) collective-permute-start(bf16[4,256,128]{2,1,0:T(8,128)(2,1)S(1)} %get-tuple-element.27.near_ref), channel_id=1, source_target_pairs={{0,4},{1,5},{2,6},{3,7},{4,0},{5,1},{6,2},{7,3},{8,12},{9,13},{10,... | collective-permute-start | bytes 786440 | tf_op jit(solution)/shard_map/ppermute | solution.py:319
  27.7 9.7 %collective-permute-start.9 = (bf16[32,1024]{1,0:T(8,128)(2,1)S(1)}, bf16[32,1024]{1,0:T(8,128)(2,1)S(1)}, u32[]{:S(2)}, u32[]{:S(2)}) collective-permute-start(bf16[32,1024]{1,0:T(8,128)(2,1)S(1)} %constant_dynamic-slice_fusion), channel_id=1, source_target_pairs={{0,32},{16,48},{32,0},{48,16},{64,96},{80,112},{96,64},{112,80},{1... | collective-permute-start | bytes 196616 | tf_op jit(solution)/shard_map/ppermute | solution.py:315
  36.1 6.5 %collective-permute-start.8 = (bf16[4,256,128]{2,1,0:T(8,128)(2,1)S(1)}, bf16[4,256,128]{2,1,0:T(8,128)(2,1)S(1)}, u32[]{:S(2)}, u32[]{:S(2)}) collective-permute-start(bf16[4,256,128]{2,1,0:T(8,128)(2,1)S(1)} %get-tuple-element.32.far_ref), channel_id=1, source_target_pairs={{0,4},{1,5},{2,6},{3,7},{4,0},{5,1},{6,2},{7,3},{8,12},{9,13},{10,... | collective-permute-start | bytes 786440 | tf_op jit(solution)/shard_map/ppermute | solution.py:319
  37.4 8.2 %copy-start.17 = (bf16[32,1024]{1,0:T(8,128)(2,1)}, bf16[32,1024]{1,0:T(8,128)(2,1)S(1)}, u32[]{:S(2)}) copy-start(bf16[32,1024]{1,0:T(8,128)(2,1)S(1)} %collective-permute-done.9) | copy-start | bytes 196612
  38.1 16.4 %collective-permute-start.10 = (bf16[64,1024]{1,0:T(8,128)(2,1)}, bf16[64,1024]{1,0:T(8,128)(2,1)}, u32[]{:S(2)}, u32[]{:S(2)}) collective-permute-start(bf16[64,1024]{1,0:T(8,128)(2,1)} %pad_maximum_fusion.1), channel_id=1, source_target_pairs={{0,16},{16,0},{32,48},{48,32},{64,80},{80,64},{96,112},{112,96},{1... | collective-permute-start | bytes 393224 | tf_op jit(solution)/shard_map/ppermute | solution.py:315
  38.1 1.1 %copy-start.15 = (f32[10,128,128]{2,1,0:T(8,128)S(1)}, f32[10,128,128]{2,1,0:T(8,128)}, u32[]{:S(2)}) copy-start(f32[10,128,128]{2,1,0:T(8,128)} %get-tuple-element.22.bias_ref) | copy-start | bytes 1966084
  39.2 45.9 %copy-start.2 = (bf16[1,128,1024]{2,1,0:T(8,128)(2,1)S(1)}, bf16[1,128,1024]{2,1,0:T(8,128)(2,1)}, u32[]{:S(2)}) copy-start(bf16[1,128,1024]{2,1,0:T(8,128)(2,1)} %param.11) | copy-start | bytes 786436
  42.6 1.1 %copy-start.16 = (f32[10,128,128]{2,1,0:T(8,128)S(1)}, f32[10,128,128]{2,1,0:T(8,128)}, u32[]{:S(2)}) copy-start(f32[10,128,128]{2,1,0:T(8,128)} %get-tuple-element.22.bias_ref) | copy-start | bytes 1966084
  45.6 25.9 %all-to-all-start = ((bf16[8,160,128]{2,1,0:T(8,128)(2,1)}), bf16[8,160,128]{2,1,0:T(8,128)(2,1)S(1)}, u32[]{:S(2)}, u32[]{:S(2)}) async-start(bf16[8,160,128]{2,1,0:T(8,128)(2,1)} %attend_last.1), calls=%async_computation | async-start | bytes 655360 | tf_op jit(solution)/shard_map/all_to_all | solution.py:430
  55.4 7.1 %collective-permute-start.11 = (bf16[128,1024]{1,0:T(8,128)(2,1)S(1)}, bf16[128,1024]{1,0:T(8,128)(2,1)S(1)}, u32[]{:S(2)}, u32[]{:S(2)}) collective-permute-start(bf16[128,1024]{1,0:T(8,128)(2,1)S(1)} %pad_maximum_fusion.ta_ref), channel_id=1, source_target_pairs={{0,64},{16,80},{32,96},{48,112},{64,128},{80,144},{96,160},{112,17... | collective-permute-start | bytes 786440 | tf_op jit(solution)/shard_map/ppermute | solution.py:315
  55.7 8.9 %collective-permute-start.13 = (bf16[128,1024]{1,0:T(8,128)(2,1)S(1)}, bf16[128,1024]{1,0:T(8,128)(2,1)S(1)}, u32[]{:S(2)}, u32[]{:S(2)}) collective-permute-start(bf16[128,1024]{1,0:T(8,128)(2,1)S(1)} %pad_maximum_fusion.ta_ref), channel_id=1, source_target_pairs={{0,192},{16,208},{32,224},{48,240},{64,0},{80,16},{96,32},{112,48}... | collective-permute-start | bytes 786440 | tf_op jit(solution)/shard_map/ppermute | solution.py:315
  62.5 5.2 %copy-start.3 = (bf16[128,1024]{1,0:T(8,128)(2,1)}, bf16[128,1024]{1,0:T(8,128)(2,1)S(1)}, u32[]{:S(2)}) copy-start(bf16[128,1024]{1,0:T(8,128)(2,1)S(1)} %collective-permute-done.11.tb_ref) | copy-start | bytes 786436
  62.5 5.2 %collective-permute-start.12 = (bf16[64,1024]{1,0:T(8,128)(2,1)S(1)}, bf16[64,1024]{1,0:T(8,128)(2,1)S(1)}, u32[]{:S(2)}, u32[]{:S(2)}) collective-permute-start(bf16[64,1024]{1,0:T(8,128)(2,1)S(1)} %slice.8), channel_id=1, source_target_pairs={{0,64},{16,80},{32,96},{48,112},{64,128},{80,144},{96,160},{112,17... | collective-permute-start | bytes 393224 | tf_op jit(solution)/shard_map/ppermute | solution.py:315
  64.5 3.2 %copy-start.5 = (bf16[128,1024]{1,0:T(8,128)(2,1)}, bf16[128,1024]{1,0:T(8,128)(2,1)S(1)}, u32[]{:S(2)}) copy-start(bf16[128,1024]{1,0:T(8,128)(2,1)S(1)} %collective-permute-done.13.te_ref) | copy-start | bytes 786436
  64.6 6.3 %collective-permute-start.14 = (bf16[64,1024]{1,0:T(8,128)(2,1)S(1)}, bf16[64,1024]{1,0:T(8,128)(2,1)S(1)}, u32[]{:S(2)}, u32[]{:S(2)}) collective-permute-start(bf16[64,1024]{1,0:T(8,128)(2,1)S(1)} %slice.9), channel_id=1, source_target_pairs={{0,192},{16,208},{32,224},{48,240},{64,0},{80,16},{96,32},{112,48}... | collective-permute-start | bytes 393224 | tf_op jit(solution)/shard_map/ppermute | solution.py:315
  67.8 0.6 copy-start.8
  70.8 0.7 copy-start.10
  71.5 1.0 %copy-start.4 = (bf16[128,1024]{1,0:T(8,128)(2,1)S(1)}, bf16[128,1024]{1,0:T(8,128)(2,1)}, u32[]{:S(2)}) copy-start(bf16[128,1024]{1,0:T(8,128)(2,1)} %copy-done.3) | copy-start | bytes 786436
  72.4 0.9 %copy-start.6 = (bf16[128,1024]{1,0:T(8,128)(2,1)S(1)}, bf16[128,1024]{1,0:T(8,128)(2,1)}, u32[]{:S(2)}) copy-start(bf16[128,1024]{1,0:T(8,128)(2,1)} %copy-done.5) | copy-start | bytes 786436
  73.4 0.9 copy-start.9
  74.3 0.9 copy-start.11
  77.3 16.1 %all-to-all-start.1 = ((f32[16,16,128]{2,1,0:T(8,128)}), f32[16,16,128]{2,1,0:T(8,128)S(1)}, u32[]{:S(2)}, u32[]{:S(2)}) async-start(f32[16,16,128]{2,1,0:T(8,128)} %state.1), calls=%async_computation.1 | async-start | bytes 262144 | tf_op jit(solution)/shard_map/all_to_all | solution.py:441
  85.1 1.0 %copy-start.7 = (bf16[128,1024]{1,0:T(8,128)(2,1)S(1)}, bf16[128,1024]{1,0:T(8,128)(2,1)}, u32[]{:S(2)}) copy-start(bf16[128,1024]{1,0:T(8,128)(2,1)} %get-tuple-element.38.gate_ref) | copy-start | bytes 786436

commit v4 on v3

--- a/solution.py
+++ b/solution.py
@@ -57,7 +57,7 @@
     return (0, one, one + blocks_ref[0, 1])
 
 
-def prepare(blocks_ref, slope_ref, ids_ref, map_ref, bias_ref, list_ref, place_ref):
+def prepare_kernel(blocks_ref, slope_ref, ids_ref, map_ref, bias_ref, list_ref, place_ref):
     me, dp = lax.axis_index("seq"), lax.axis_index("dp")
     starts = user_starts(blocks_ref)
     slope = slope_ref[head_of(me)]
@@ -109,58 +109,28 @@
         place_ref[2 * user + 1 : 2 * user + 2, :] = lane
 
 
-def project_kernel(
-    blocks_ref,
-    tail_ref,
-    slope_ref,
-    ids_ref,
-    map_ref,
-    x_ref,
-    gain_ref,
-    w_ref,
-    gate_ref,
-    extra_ref,
-    bias_ref,
-    list_ref,
-    place_ref,
-    *refs,
-):
-    out_refs, weights, sems = refs[:HEADS], refs[HEADS], refs[HEADS + 1]
+def project_kernel(blocks_ref, tail_ref, x_ref, gain_ref, w_ref, gate_ref, extra_ref, *out_refs):
     me = lax.axis_index("seq")
-    order = FAR + NEAR
-
-    def copies(at):
-        head = head_of(me) ^ order[at]
-        return [
-            pltpu.make_async_copy(
-                w_ref.at[:, pl.ds(pl.multiple_of((group * HEADS + head) * HD, HD), HD)],
-                weights.at[at, :, group * HD : (group + 1) * HD],
-                sems.at[at, group],
-            )
-            for group in range(4)
-        ]
-
-    for at in range(HEADS):
-        for copy in copies(at):
-            copy.start()
     normed = (layer_norm(x_ref[...].astype(jnp.float32)) * gain_ref[...]).astype(jnp.bfloat16)
-    prepare(blocks_ref, slope_ref, ids_ref, map_ref, bias_ref, list_ref, place_ref)
-    for at, out_ref in enumerate(out_refs):
-        for copy in copies(at):
-            copy.wait()
-        parts = silu(jnp.dot(normed, weights[at], preferred_element_type=jnp.float32))
-        head = head_of(me) ^ order[at]
-        gate_ref[:, pl.ds(pl.multiple_of(head * HD, HD), HD)] = parts[:, :HD].astype(jnp.bfloat16)
-        out_ref[ROW_K:ROW_V, :] = parts[:, 2 * HD : 3 * HD].T.astype(jnp.bfloat16)
-        out_ref[ROW_V:ROW_Q, :] = parts[:, 3 * HD :].astype(jnp.bfloat16)
-        out_ref[ROW_Q:ROWS_A, :] = parts[:, HD : 2 * HD].astype(jnp.bfloat16)
+    for q, out_ref in zip(FAR + NEAR, out_refs):
+        head = head_of(me) ^ q
+
+        def part(group, head=head):
+            columns = pl.ds(pl.multiple_of((group * HEADS + head) * HD, HD), HD)
+            return silu(jnp.dot(normed, w_ref[:, columns], preferred_element_type=jnp.float32))
+
+        out_ref[ROW_K:ROW_V, :] = part(2).T.astype(jnp.bfloat16)
+        out_ref[ROW_V:ROW_Q, :] = part(3).astype(jnp.bfloat16)
+        out_ref[ROW_Q:ROWS_A, :] = part(1).astype(jnp.bfloat16)
+    gate = silu(jnp.dot(normed, w_ref[:, :D], preferred_element_type=jnp.float32)).astype(jnp.bfloat16)
+    gate_ref[...] = gate
 
     starts = user_starts(blocks_ref)
     last = jnp.int32(-1)
     for user in range(USERS):
         last = jnp.where(starts[user] + blocks_ref[0, user] - 1 == me, tail_ref[0, user] - 1, last)
     pick = (lax.broadcasted_iota(jnp.int32, (16, BLK), 1) == last).astype(jnp.bfloat16)
-    gate_row = jnp.dot(pick, gate_ref[...], preferred_element_type=jnp.float32)[0:1]
+    gate_row = jnp.dot(pick, gate, preferred_element_type=jnp.float32)[0:1]
     token_row = jnp.dot(pick, x_ref[...], preferred_element_type=jnp.float32)[0:1]
     pieces = [row[:, h * HD : (h + 1) * HD] for row in (gate_row, token_row) for h in range(HEADS)]
     extra_ref[...] = jnp.concatenate(pieces, axis=0).astype(jnp.bfloat16)
@@ -344,37 +314,39 @@
     seq = lax.axis_index("seq")
     mine = head_of(seq)
 
-    gate, extra, bias, pairs, places, *sent = pl.pallas_call(
-        project_kernel,
-        in_specs=[smem(), smem(), smem()] + [vmem()] * 4 + [pl.BlockSpec(memory_space=pltpu.HBM)],
-        out_specs=[vmem()] * 3 + [smem()] + [vmem()] * (1 + HEADS),
+    own = lax.dynamic_slice_in_dim(node_table, mine * 32, 32, 0)
+    pair = jnp.concatenate([own, dp_shift(own, lambda i: i ^ 2)], axis=0)
+    quad = jnp.concatenate([pair, dp_shift(pair, lambda i: i ^ 1)], axis=0)
+    below = dp_shift(quad, lambda i: (i + 4) % 16)
+    above = dp_shift(quad, lambda i: (i + 12) % 16)
+    opposite_first = dp_shift(below[:64], lambda i: (i + 4) % 16)
+    opposite_last = dp_shift(above[64:], lambda i: (i + 12) % 16)
+    table = [quad, below, opposite_first, opposite_last, above]
+
+    bias, pairs, places = pl.pallas_call(
+        prepare_kernel,
+        in_specs=[smem(), smem(), vmem(), vmem()],
+        out_specs=[vmem(), smem(), vmem()],
         out_shape=[
-            pltpu.HBM((BLK, D), jnp.bfloat16),
-            sds((16, HD)),
-            pltpu.HBM((MAXD, BLK, BLK), jnp.float32),
+            sds((MAXD, BLK, BLK), jnp.float32),
             sds((2 * LIST,), jnp.int32),
             sds((8, 64), jnp.int32),
-        ]
-        + [sds((ROWS_A, HD))] * HEADS,
-        scratch_shapes=[pltpu.VMEM((HEADS, D, 4 * HD), jnp.bfloat16), pltpu.SemaphoreType.DMA((HEADS, 4))],
+        ],
+        name="prepare",
+        cost_estimate=cost(1 << 32, 1 << 24),
+        compiler_params=GRANT,
+    )(*(in_hbm(value) for value in (hist_blocks, rab_slope, beam_nodes, subtree_map[None, :])))
+    x_here, _ = lax.optimization_barrier((x_rows, pairs))
+
+    gate, extra, *sent = pl.pallas_call(
+        project_kernel,
+        in_specs=[smem(), smem()] + [vmem()] * 3,
+        out_specs=[vmem()] * (2 + HEADS),
+        out_shape=[pltpu.HBM((BLK, D), jnp.bfloat16), sds((16, HD))] + [sds((ROWS_A, HD))] * HEADS,
         name="project",
         cost_estimate=cost(2 * BLK * D * 4 * D, 10 << 20),
         compiler_params=GRANT,
-    )(
-        *(
-            in_hbm(value)
-            for value in (
-                hist_blocks,
-                hist_tail,
-                rab_slope,
-                beam_nodes,
-                subtree_map[None, :],
-                x_rows,
-                in_gain[None, :],
-                w_proj,
-            )
-        )
-    )
+    )(hist_blocks, hist_tail, x_here, in_gain[None, :], w_proj)
     far_got, near_got = [], [sent[4]]
     for q, value in zip(FAR, sent[:4]):
         far_got.append(seq_xor(value, spread(q)))
@@ -396,15 +368,6 @@
     far_kv, far_q = sort(far_got)
     far_cross = seq_xor(far_kv, 4)
 
-    own = lax.dynamic_slice_in_dim(node_table, mine * 32, 32, 0)
-    pair = jnp.concatenate([own, dp_shift(own, lambda i: i ^ 2)], axis=0)
-    quad = jnp.concatenate([pair, dp_shift(pair, lambda i: i ^ 1)], axis=0)
-    below = dp_shift(quad, lambda i: (i + 4) % 16)
-    above = dp_shift(quad, lambda i: (i + 12) % 16)
-    opposite_first = dp_shift(below[:64], lambda i: (i + 4) % 16)
-    opposite_last = dp_shift(above[64:], lambda i: (i + 12) % 16)
-    table = [quad, below, opposite_first, opposite_last, above]
-
     part, queries = pl.pallas_call(
         attend_first_kernel,
         in_specs=[smem()] + [vmem()] * 6,

time: 95 us -> 96.9 us (1.020)
  local copies, waits for them, and re-layouts: 8.19 us -> 10.8 us
    unnamed x36 -> x50, local copies, waits for them, and re-layouts: 8.16 us -> 10.8 us
    pallas_call x1 -> x2, Pallas kernels: 7.53 us -> 7.56 us  [the longest x1 4.23 us: layer(): pl.pallas_call(project_kernel, in_specs=[smem(), smem()] + [vmem()] * 3,...]
  transfers between devices with their start and end apart: 17 -> 17, of which waited for: 8 -> 7; matrix products, arithmetic and copies ran while one was open for 2% -> 1% of each run, Pallas kernels for 7% -> 7%
where the time goes in v4:
time: 96.9 us; the launch traced here: 96.4 us
  starting transfers between devices  46.7 us (48%)
  waiting for transfers between devices  19.9 us (21%)
  Pallas kernels  17.1 us (18%)
  local copies, waits for them, and re-layouts  10.8 us (11%)
    ppermute x9, starting transfers between devices, seq_xor(): return lax.ppermute(value, 'seq', [(i, i ^ apart) for i in range(NSEQ)])  18.4 us
    ppermute x6, starting transfers between devices, dp_shift(): return lax.ppermute(value, 'dp', [(i, move(i)) for i in range(16)])  11.8 us
    unnamed x50, local copies, waits for them, and re-layouts  10.8 us
    ppermute x6, waiting for transfers between devices, dp_shift(): return lax.ppermute(value, 'dp', [(i, move(i)) for i in range(16)])  10.2 us
    all_to_all x1, starting transfers between devices, layer(): lax.all_to_all(back, 'seq', 0, 0, tiled=True, axis_index_groups=SETS)  8.74 us
    all_to_all x1, starting transfers between devices, layer(): scores = lax.all_to_all(sent, 'seq', 0, 0, tiled=True)  7.75 us
    all_to_all x1, waiting for transfers between devices, layer(): scores = lax.all_to_all(sent, 'seq', 0, 0, tiled=True)  6.09 us
    pallas_call x1, Pallas kernels, layer(): pl.pallas_call(project_kernel, in_specs=[smem(), smem()] + [vmem()] * 3,...  4.23 us
  transfers between devices with their start and end apart: 17, of which 7 were waited for; matrix products, arithmetic and copies ran while one was open for 1% of the time, Pallas kernels for 7%

profile of v4, /device:TPU:6, one launch (start us, length us, event | category | flops | bytes accessed | tf_op | source)
XLA Modules:
  0.0 96.4 jit_solution(9444884982854522960)
XLA Ops:
  0.6 0.0 copy-start
  0.7 0.0 slice-start
  0.7 0.0 slice-start.1
  0.7 3.3 %prepare.1 = (f32[10,128,128]{2,1,0:T(8,128)S(1)}, s32[256]{0:T(256)S(1)}, s32[8,64]{1,0:T(8,128)S(1)}) custom-call(s32[1,3]{1,0:T(1,128)} %blocks_ref.7, f32[8]{0:T(128)} %slope_ref.1, s32[3,64]{1,0:T(4,128)} %ids_ref.1, s32[1,64]{1,0:T(1,128)} %bitcast.13), custom_call_target="tpu_custom_call" | custom-call | flops 4294967296 | bytes 16777216 | tf_op jit(solution)/shard_map/prepare/pallas_call | solution.py:326
  4.1 0.9 copy-done.18
  5.0 4.2 %project.1 = (bf16[128,1024]{1,0:T(8,128)(2,1)}, bf16[16,128]{1,0:T(8,128)(2,1)S(1)}, bf16[384,128]{1,0:T(8,128)(2,1)}, bf16[384,128]{1,0:T(8,128)(2,1)}, bf16[3...) custom-call(s32[1,3]{1,0:T(1,128)S(1)} %copy-done.14, ...), custom_call_target="tpu_custom_call" | custom-call | flops 1073741824 | bytes 10485760 | tf_op jit(solution)/shard_map/project/pallas_call | solution.py:341
  9.2 0.6 copy-done.16
  9.8 0.6 copy-done.17
  10.5 1.9 %collective-permute-start = (bf16[384,128]{1,0:T(8,128)(2,1)}, bf16[384,128]{1,0:T(8,128)(2,1)S(1)}, u32[]{:S(2)}, u32[]{:S(2)}) collective-permute-start(bf16[384,128]{1,0:T(8,128)(2,1)} %get-tuple-element.26), channel_id=1, source_target_pairs={{0,1},{1,0},{2,3},{3,2},{4,5},{5,4},{6,7},{7,6},{8,9},{9,8},{10,11... | collective-permute-start | bytes 294920 | tf_op jit(solution)/shard_map/ppermute | solution.py:289
  12.4 3.2 %collective-permute-start.1 = (bf16[384,128]{1,0:T(8,128)(2,1)}, bf16[384,128]{1,0:T(8,128)(2,1)S(1)}, u32[]{:S(2)}, u32[]{:S(2)}) collective-permute-start(bf16[384,128]{1,0:T(8,128)(2,1)} %get-tuple-element.27), channel_id=1, source_target_pairs={{0,8},{1,9},{2,10},{3,11},{4,12},{5,13},{6,14},{7,15},{8,0},{9,1},... | collective-permute-start | bytes 294920 | tf_op jit(solution)/shard_map/ppermute | solution.py:289
  15.6 3.3 %collective-permute-start.3 = (bf16[384,128]{1,0:T(8,128)(2,1)}, bf16[384,128]{1,0:T(8,128)(2,1)S(1)}, u32[]{:S(2)}, u32[]{:S(2)}) collective-permute-start(bf16[384,128]{1,0:T(8,128)(2,1)} %get-tuple-element.30), channel_id=1, source_target_pairs={{0,2},{1,3},{2,0},{3,1},{4,6},{5,7},{6,4},{7,5},{8,10},{9,11},{10,... | collective-permute-start | bytes 294920 | tf_op jit(solution)/shard_map/ppermute | solution.py:289
  18.9 1.2 %collective-permute-start.4 = (bf16[384,128]{1,0:T(8,128)(2,1)}, bf16[384,128]{1,0:T(8,128)(2,1)S(1)}, u32[]{:S(2)}, u32[]{:S(2)}) collective-permute-start(bf16[384,128]{1,0:T(8,128)(2,1)} %get-tuple-element.31), channel_id=1, source_target_pairs={{0,3},{1,2},{2,1},{3,0},{4,7},{5,6},{6,5},{7,4},{8,11},{9,10},{10,... | collective-permute-start | bytes 294920 | tf_op jit(solution)/shard_map/ppermute | solution.py:289
  20.1 4.6 %collective-permute-start.5 = (bf16[384,128]{1,0:T(8,128)(2,1)}, bf16[384,128]{1,0:T(8,128)(2,1)S(1)}, u32[]{:S(2)}, u32[]{:S(2)}) collective-permute-start(bf16[384,128]{1,0:T(8,128)(2,1)} %copy-done.17), channel_id=1, source_target_pairs={{0,10},{1,11},{2,8},{3,9},{4,14},{5,15},{6,12},{7,13},{8,2},{9,3},... | collective-permute-start | bytes 294920 | tf_op jit(solution)/shard_map/ppermute | solution.py:289
  24.8 1.2 %collective-permute-start.6 = (bf16[384,128]{1,0:T(8,128)(2,1)}, bf16[384,128]{1,0:T(8,128)(2,1)S(1)}, u32[]{:S(2)}, u32[]{:S(2)}) collective-permute-start(bf16[384,128]{1,0:T(8,128)(2,1)} %copy-done.16), channel_id=1, source_target_pairs={{0,11},{1,10},{2,9},{3,8},{4,15},{5,14},{6,13},{7,12},{8,3},{9,2},... | collective-permute-start | bytes 294920 | tf_op jit(solution)/shard_map/ppermute | solution.py:289
  26.0 1.6 %collective-permute-start.7 = (bf16[4,256,128]{2,1,0:T(8,128)(2,1)S(1)}, bf16[4,256,128]{2,1,0:T(8,128)(2,1)S(1)}, u32[]{:S(2)}, u32[]{:S(2)}) collective-permute-start(bf16[4,256,128]{2,1,0:T(8,128)(2,1)S(1)} %get-tuple-element.29.near_ref), channel_id=1, source_target_pairs={{0,4},{1,5},{2,6},{3,7},{4,0},{5,1},{6,2},{7,3},{8,12},{9,13},{10,... | collective-permute-start | bytes 786440 | tf_op jit(solution)/shard_map/ppermute | solution.py:289
  27.6 2.1 %collective-permute-done.3.refs_0_ = bf16[384,128]{1,0:T(8,128)(2,1)S(1)} collective-permute-done((bf16[384,128]{1,0:T(8,128)(2,1)}, bf16[384,128]{1,0:T(8,128)(2,1)S(1)}, u32[]{:S(2)}, u32[]{:S(2)}) %collective-permute-start.3) | collective-permute-done | bytes 98336 | tf_op jit(solution)/shard_map/ppermute | solution.py:289
  29.7 7.4 %collective-permute-start.9 = (bf16[32,1024]{1,0:T(8,128)(2,1)S(1)}, bf16[32,1024]{1,0:T(8,128)(2,1)S(1)}, u32[]{:S(2)}, u32[]{:S(2)}) collective-permute-start(bf16[32,1024]{1,0:T(8,128)(2,1)S(1)} %constant_dynamic-slice_fusion), channel_id=1, source_target_pairs={{0,32},{16,48},{32,0},{48,16},{64,96},{80,112},{96,64},{112,80},{1... | collective-permute-start | bytes 196616 | tf_op jit(solution)/shard_map/ppermute | solution.py:285
  37.1 1.0 %collective-permute-done.5.refs_2_ = bf16[384,128]{1,0:T(8,128)(2,1)S(1)} collective-permute-done((bf16[384,128]{1,0:T(8,128)(2,1)}, bf16[384,128]{1,0:T(8,128)(2,1)S(1)}, u32[]{:S(2)}, u32[]{:S(2)}) %collective-permute-start.5) | collective-permute-done | bytes 98336 | tf_op jit(solution)/shard_map/ppermute | solution.py:289
  38.1 1.4 %collective-permute-start.8 = (bf16[4,256,128]{2,1,0:T(8,128)(2,1)S(1)}, bf16[4,256,128]{2,1,0:T(8,128)(2,1)S(1)}, u32[]{:S(2)}, u32[]{:S(2)}) collective-permute-start(bf16[4,256,128]{2,1,0:T(8,128)(2,1)S(1)} %get-tuple-element.34.far_ref), channel_id=1, source_target_pairs={{0,4},{1,5},{2,6},{3,7},{4,0},{5,1},{6,2},{7,3},{8,12},{9,13},{10,... | collective-permute-start | bytes 786440 | tf_op jit(solution)/shard_map/ppermute | solution.py:289
  39.5 0.1 collective-permute-start.10
  39.6 0.5 copy-done.22
  40.1 1.1 %copy-done.19 = f32[10,128,128]{2,1,0:T(8,128)S(1)} copy-done((f32[10,128,128]{2,1,0:T(8,128)S(1)}, f32[10,128,128]{2,1,0:T(8,128)}, u32[]{:S(2)}) %copy-start.19) | copy-done | bytes 655384
  41.2 3.1 %attend_first.1 = (f32[8,128,128]{2,1,0:T(8,128)S(1)}, bf16[8,128,128]{2,1,0:T(8,128)(2,1)S(1)}) custom-call(s32[256]{0:T(256)S(1)} %get-tuple-element.22.list_ref, f32[10,128,128]{2,1,0:T(8,128)S(1)} %copy-done.19, bf16[4,256,128]{2,1,0:T(8,128)(2,1)S(1)} %get-tuple-element.29.near_ref, bf16[4,256,128]{2,1,0:T(8,128)(2,1)S(1)} %get-tuple-element.34.far_ref, ...), custom_call_target="tpu_custom_call" | custom-call | flops 2147483648 | bytes 4194304 | tf_op jit(solution)/shard_map/attend_first/pallas_call | solution.py:371
  44.3 0.5 collective-permute-done.8.cross_ref
  44.8 1.1 %copy-done.20 = f32[10,128,128]{2,1,0:T(8,128)S(1)} copy-done((f32[10,128,128]{2,1,0:T(8,128)S(1)}, f32[10,128,128]{2,1,0:T(8,128)}, u32[]{:S(2)}) %copy-start.20) | copy-done | bytes 655384
  45.9 1.9 %attend_last.1 = bf16[8,160,128]{2,1,0:T(8,128)(2,1)} custom-call(s32[1,3]{1,0:T(1,128)S(1)} %copy-done.14, s32[1,3]{1,0:T(1,128)S(1)} %copy-done.15, s32[256]{0:T(256)S(1)} %get-tuple-element.22.list_ref, f32[10,128,128]{2,1,0:T(8,128)S(1)} %copy-done.20, bf16[8,128,128]{2,1,0:T(8,128)(2,1)S(1)} %get-tuple-element.37.queries_ref, ...), custom_call_target="tpu_custom_call" | custom-call | flops 1073741824 | bytes 2097152 | tf_op jit(solution)/shard_map/attend_last/pallas_call | solution.py:382
  47.8 8.7 %all-to-all-start = ((bf16[8,160,128]{2,1,0:T(8,128)(2,1)}), bf16[8,160,128]{2,1,0:T(8,128)(2,1)S(1)}, u32[]{:S(2)}, u32[]{:S(2)}) async-start(bf16[8,160,128]{2,1,0:T(8,128)(2,1)} %attend_last.1), calls=%async_computation | async-start | bytes 655360 | tf_op jit(solution)/shard_map/all_to_all | solution.py:393
  56.5 1.0 pad_maximum_fusion.ta_ref
  57.5 0.3 collective-permute-start.11
  57.8 1.8 %collective-permute-start.13 = (bf16[128,1024]{1,0:T(8,128)(2,1)S(1)}, bf16[128,1024]{1,0:T(8,128)(2,1)S(1)}, u32[]{:S(2)}, u32[]{:S(2)}) collective-permute-start(bf16[128,1024]{1,0:T(8,128)(2,1)S(1)} %pad_maximum_fusion.ta_ref), channel_id=1, source_target_pairs={{0,192},{16,208},{32,224},{48,240},{64,0},{80,16},{96,32},{112,48}... | collective-permute-start | bytes 786440 | tf_op jit(solution)/shard_map/ppermute | solution.py:285
  59.6 5.0 %collective-permute-done.11.tb_ref = bf16[128,1024]{1,0:T(8,128)(2,1)S(1)} collective-permute-done((bf16[128,1024]{1,0:T(8,128)(2,1)S(1)}, bf16[128,1024]{1,0:T(8,128)(2,1)S(1)}, u32[]{:S(2)}, u32[]{:S(2)}) %collective-permute-start.11) | collective-permute-done | bytes 262176 | tf_op jit(solution)/shard_map/ppermute | solution.py:285
  64.6 1.8 %collective-permute-start.12 = (bf16[64,1024]{1,0:T(8,128)(2,1)S(1)}, bf16[64,1024]{1,0:T(8,128)(2,1)S(1)}, u32[]{:S(2)}, u32[]{:S(2)}) collective-permute-start(bf16[64,1024]{1,0:T(8,128)(2,1)S(1)} %slice.8), channel_id=1, source_target_pairs={{0,64},{16,80},{32,96},{48,112},{64,128},{80,144},{96,160},{112,17... | collective-permute-start | bytes 393224 | tf_op jit(solution)/shard_map/ppermute | solution.py:285
  66.4 0.3 collective-permute-start.14
  66.8 2.8 %collective-permute-done.12.tc_ref = bf16[64,1024]{1,0:T(8,128)(2,1)S(1)} collective-permute-done((bf16[64,1024]{1,0:T(8,128)(2,1)S(1)}, bf16[64,1024]{1,0:T(8,128)(2,1)S(1)}, u32[]{:S(2)}, u32[]{:S(2)}) %collective-permute-start.12) | collective-permute-done | bytes 131104 | tf_op jit(solution)/shard_map/ppermute | solution.py:285
  69.6 0.7 copy-done.8
  70.3 2.4 %collective-permute-done.14.td_ref = bf16[64,1024]{1,0:T(8,128)(2,1)S(1)} collective-permute-done((bf16[64,1024]{1,0:T(8,128)(2,1)S(1)}, bf16[64,1024]{1,0:T(8,128)(2,1)S(1)}, u32[]{:S(2)}, u32[]{:S(2)}) %collective-permute-start.14) | collective-permute-done | bytes 131104 | tf_op jit(solution)/shard_map/ppermute | solution.py:285
  72.7 0.6 copy-done.10
  73.3 0.9 copy-done.4
  74.3 0.9 copy-done.6
  75.2 0.9 copy-done.9
  76.1 0.9 copy-done.11
  77.0 2.1 %state.1 = f32[16,16,128]{2,1,0:T(8,128)} custom-call(s32[1,3]{1,0:T(1,128)S(1)} %copy-done.14, bf16[8,160,128]{2,1,0:T(8,128)(2,1)S(1)} %all-to-all-done.mixed_ref, f32[1,1024]{1,0:T(1,128)S(1)} %bitcast.9, bf16[1024,1024]{1,0:T(8,128)(2,1)S(1)} %copy-done.1, bf16[128,1024]{1,0:T(8,128)(2,1)S(1)} %pad_maximum_fusion.ta_ref, ...), custom_call_target="tpu_custom_call" | custom-call | flops 33554432 | bytes 3145728 | tf_op jit(solution)/shard_map/state/pallas_call | solution.py:395
  79.2 7.7 %all-to-all-start.1 = ((f32[16,16,128]{2,1,0:T(8,128)}), f32[16,16,128]{2,1,0:T(8,128)S(1)}, u32[]{:S(2)}, u32[]{:S(2)}) async-start(f32[16,16,128]{2,1,0:T(8,128)} %state.1), calls=%async_computation.1 | async-start | bytes 262144 | tf_op jit(solution)/shard_map/all_to_all | solution.py:404
  86.9 0.0 copy-start.7
  86.9 0.9 copy-done.7
  87.9 1.4 %layer.1 = bf16[128,1024]{1,0:T(8,128)(2,1)} custom-call(bf16[8,160,128]{2,1,0:T(8,128)(2,1)S(1)} %all-to-all-done.mixed_ref, bf16[128,1024]{1,0:T(8,128)(2,1)S(1)} %copy-done.7, bf16[128,1024]{1,0:T(8,128)(2,1)S(1)} %bitcast.8, f32[1,1024]{1,0:T(1,128)S(1)} %bitcast.10, bf16[1024,1024]{1,0:T(8,128)(2,1)S(1)} %copy-done.1), custom_call_target="tpu_custom_call" | custom-call | flops 268435456 | bytes 3145728 | tf_op jit(solution)/shard_map/layer/pallas_call | solution.py:406
  89.2 6.1 %all-to-all-done.1.score_ref = f32[16,16,128]{2,1,0:T(8,128)S(1)} async-done(((f32[16,16,128]{2,1,0:T(8,128)}), f32[16,16,128]{2,1,0:T(8,128)S(1)}, u32[]{:S(2)}, u32[]{:S(2)}) %all-to-all-start.1) | async-done | bytes 131104 | tf_op jit(solution)/shard_map/all_to_all | solution.py:404
  95.3 1.1 %pick.1 = f32[3,64]{1,0:T(4,128)} custom-call(f32[16,16,128]{2,1,0:T(8,128)S(1)} %all-to-all-done.1.score_ref, s32[8,64]{1,0:T(8,128)S(1)} %get-tuple-element.41.place_ref), custom_call_target="tpu_custom_call" | custom-call | flops 1048576 | bytes 131072 | tf_op jit(solution)/shard_map/pick/pallas_call | solution.py:416
  (51 shorter events, 0.2 us)
Async XLA Ops:
  0.6 26.9 %copy-start = (bf16[256,1024]{1,0:T(8,128)(2,1)S(1)}, bf16[256,1024]{1,0:T(8,128)(2,1)}, u32[]{:S(2)}) copy-start(bf16[256,1024]{1,0:T(8,128)(2,1)} %param.19) | copy-start | bytes 1572868
  0.6 4.3 %copy-start.14 = (s32[1,3]{1,0:T(1,128)S(1)}, s32[1,3]{1,0:T(1,128)}, u32[]{:S(2)}) copy-start(s32[1,3]{1,0:T(1,128)} %blocks_ref.7) | copy-start | bytes 40
  0.7 4.3 %copy-start.2 = (bf16[1,128,1024]{2,1,0:T(8,128)(2,1)S(1)}, bf16[1,128,1024]{2,1,0:T(8,128)(2,1)}, u32[]{:S(2)}) copy-start(bf16[1,128,1024]{2,1,0:T(8,128)(2,1)} %param.11) | copy-start | bytes 786436
  0.7 4.3 %copy-start.13 = (f32[1024]{0:T(1024)S(1)}, f32[1024]{0:T(1024)}, u32[]{:S(2)}) copy-start(f32[1024]{0:T(1024)} %param.12) | copy-start | bytes 12292
  0.7 4.2 %slice-start = ((s8[8388608]{0:T(1024)(128)(4,1)}), s8[4194304]{0:T(1024)(128)(4,1)S(1)}, s32[]{:S(2)}) async-start(s8[8388608]{0:T(1024)(128)(4,1)} %bitcast.5), calls=%async_computation.2 | async-start | bytes 8388608
  0.7 4.2 %copy-start.15 = (s32[1,3]{1,0:T(1,128)S(1)}, s32[1,3]{1,0:T(1,128)}, u32[]{:S(2)}) copy-start(s32[1,3]{1,0:T(1,128)} %tail_ref.3) | copy-start | bytes 40
  0.7 4.2 %slice-start.1 = ((s8[8388608]{0:T(1024)(128)(4,1)}), s8[4194304]{0:T(1024)(128)(4,1)S(1)}, s32[]{:S(2)}) async-start(s8[8388608]{0:T(1024)(128)(4,1)} %bitcast.5), calls=%async_computation.3 | async-start | bytes 8388608
  4.0 0.9 copy-start.18
  9.2 0.6 copy-start.16
  9.8 0.7 copy-start.17
  10.5 62.9 %copy-start.1 = (bf16[1024,1024]{1,0:T(8,128)(2,1)S(1)}, bf16[1024,1024]{1,0:T(8,128)(2,1)}, u32[]{:S(2)}) copy-start(bf16[1024,1024]{1,0:T(8,128)(2,1)} %w_ref.5) | copy-start | bytes 6291460
  10.5 62.9 %copy-start.12 = (f32[1024]{0:T(1024)S(1)}, f32[1024]{0:T(1024)}, u32[]{:S(2)}) copy-start(f32[1024]{0:T(1024)} %param.14) | copy-start | bytes 12292
  10.5 9.6 %collective-permute-start = (bf16[384,128]{1,0:T(8,128)(2,1)}, bf16[384,128]{1,0:T(8,128)(2,1)S(1)}, u32[]{:S(2)}, u32[]{:S(2)}) collective-permute-start(bf16[384,128]{1,0:T(8,128)(2,1)} %get-tuple-element.26), channel_id=1, source_target_pairs={{0,1},{1,0},{2,3},{3,2},{4,5},{5,4},{6,7},{7,6},{8,9},{9,8},{10,11... | collective-permute-start | bytes 294920 | tf_op jit(solution)/shard_map/ppermute | solution.py:289
  12.4 12.4 %collective-permute-start.1 = (bf16[384,128]{1,0:T(8,128)(2,1)}, bf16[384,128]{1,0:T(8,128)(2,1)S(1)}, u32[]{:S(2)}, u32[]{:S(2)}) collective-permute-start(bf16[384,128]{1,0:T(8,128)(2,1)} %get-tuple-element.27), channel_id=1, source_target_pairs={{0,8},{1,9},{2,10},{3,11},{4,12},{5,13},{6,14},{7,15},{8,0},{9,1},... | collective-permute-start | bytes 294920 | tf_op jit(solution)/shard_map/ppermute | solution.py:289
  15.6 10.4 %collective-permute-start.2 = (bf16[384,128]{1,0:T(8,128)(2,1)}, bf16[384,128]{1,0:T(8,128)(2,1)S(1)}, u32[]{:S(2)}, u32[]{:S(2)}) collective-permute-start(bf16[384,128]{1,0:T(8,128)(2,1)} %get-tuple-element.28), channel_id=1, source_target_pairs={{0,9},{1,8},{2,11},{3,10},{4,13},{5,12},{6,15},{7,14},{8,1},{9,0},... | collective-permute-start | bytes 294920 | tf_op jit(solution)/shard_map/ppermute | solution.py:289
  15.6 14.1 %collective-permute-start.3 = (bf16[384,128]{1,0:T(8,128)(2,1)}, bf16[384,128]{1,0:T(8,128)(2,1)S(1)}, u32[]{:S(2)}, u32[]{:S(2)}) collective-permute-start(bf16[384,128]{1,0:T(8,128)(2,1)} %get-tuple-element.30), channel_id=1, source_target_pairs={{0,2},{1,3},{2,0},{3,1},{4,6},{5,7},{6,4},{7,5},{8,10},{9,11},{10,... | collective-permute-start | bytes 294920 | tf_op jit(solution)/shard_map/ppermute | solution.py:289
  18.9 18.2 %collective-permute-start.4 = (bf16[384,128]{1,0:T(8,128)(2,1)}, bf16[384,128]{1,0:T(8,128)(2,1)S(1)}, u32[]{:S(2)}, u32[]{:S(2)}) collective-permute-start(bf16[384,128]{1,0:T(8,128)(2,1)} %get-tuple-element.31), channel_id=1, source_target_pairs={{0,3},{1,2},{2,1},{3,0},{4,7},{5,6},{6,5},{7,4},{8,11},{9,10},{10,... | collective-permute-start | bytes 294920 | tf_op jit(solution)/shard_map/ppermute | solution.py:289
  20.1 18.0 %collective-permute-start.5 = (bf16[384,128]{1,0:T(8,128)(2,1)}, bf16[384,128]{1,0:T(8,128)(2,1)S(1)}, u32[]{:S(2)}, u32[]{:S(2)}) collective-permute-start(bf16[384,128]{1,0:T(8,128)(2,1)} %copy-done.17), channel_id=1, source_target_pairs={{0,10},{1,11},{2,8},{3,9},{4,14},{5,15},{6,12},{7,13},{8,2},{9,3},... | collective-permute-start | bytes 294920 | tf_op jit(solution)/shard_map/ppermute | solution.py:289
  24.8 13.3 %collective-permute-start.6 = (bf16[384,128]{1,0:T(8,128)(2,1)}, bf16[384,128]{1,0:T(8,128)(2,1)S(1)}, u32[]{:S(2)}, u32[]{:S(2)}) collective-permute-start(bf16[384,128]{1,0:T(8,128)(2,1)} %copy-done.16), channel_id=1, source_target_pairs={{0,11},{1,10},{2,9},{3,8},{4,15},{5,14},{6,13},{7,12},{8,3},{9,2},... | collective-permute-start | bytes 294920 | tf_op jit(solution)/shard_map/ppermute | solution.py:289
  26.0 13.6 %collective-permute-start.7 = (bf16[4,256,128]{2,1,0:T(8,128)(2,1)S(1)}, bf16[4,256,128]{2,1,0:T(8,128)(2,1)S(1)}, u32[]{:S(2)}, u32[]{:S(2)}) collective-permute-start(bf16[4,256,128]{2,1,0:T(8,128)(2,1)S(1)} %get-tuple-element.29.near_ref), channel_id=1, source_target_pairs={{0,4},{1,5},{2,6},{3,7},{4,0},{5,1},{6,2},{7,3},{8,12},{9,13},{10,... | collective-permute-start | bytes 786440 | tf_op jit(solution)/shard_map/ppermute | solution.py:289
  27.6 20.2 %copy-start.21 = (bf16[32,1024]{1,0:T(8,128)(2,1)}, bf16[32,1024]{1,0:T(8,128)(2,1)S(1)}, u32[]{:S(2)}) copy-start(bf16[32,1024]{1,0:T(8,128)(2,1)S(1)} %constant_dynamic-slice_fusion) | copy-start | bytes 196612
  29.7 9.8 %collective-permute-start.9 = (bf16[32,1024]{1,0:T(8,128)(2,1)S(1)}, bf16[32,1024]{1,0:T(8,128)(2,1)S(1)}, u32[]{:S(2)}, u32[]{:S(2)}) collective-permute-start(bf16[32,1024]{1,0:T(8,128)(2,1)S(1)} %constant_dynamic-slice_fusion), channel_id=1, source_target_pairs={{0,32},{16,48},{32,0},{48,16},{64,96},{80,112},{96,64},{112,80},{1... | collective-permute-start | bytes 196616 | tf_op jit(solution)/shard_map/ppermute | solution.py:285
  38.1 6.7 %collective-permute-start.8 = (bf16[4,256,128]{2,1,0:T(8,128)(2,1)S(1)}, bf16[4,256,128]{2,1,0:T(8,128)(2,1)S(1)}, u32[]{:S(2)}, u32[]{:S(2)}) collective-permute-start(bf16[4,256,128]{2,1,0:T(8,128)(2,1)S(1)} %get-tuple-element.34.far_ref), channel_id=1, source_target_pairs={{0,4},{1,5},{2,6},{3,7},{4,0},{5,1},{6,2},{7,3},{8,12},{9,13},{10,... | collective-permute-start | bytes 786440 | tf_op jit(solution)/shard_map/ppermute | solution.py:289
  39.5 0.6 copy-start.22
  39.5 17.0 %collective-permute-start.10 = (bf16[64,1024]{1,0:T(8,128)(2,1)S(1)}, bf16[64,1024]{1,0:T(8,128)(2,1)}, u32[]{:S(2)}, u32[]{:S(2)}) collective-permute-start(bf16[64,1024]{1,0:T(8,128)(2,1)S(1)} %pad_maximum_fusion.1), channel_id=1, source_target_pairs={{0,16},{16,0},{32,48},{48,32},{64,80},{80,64},{96,112},{112,96},{1... | collective-permute-start | bytes 393224 | tf_op jit(solution)/shard_map/ppermute | solution.py:285
  40.1 1.1 %copy-start.19 = (f32[10,128,128]{2,1,0:T(8,128)S(1)}, f32[10,128,128]{2,1,0:T(8,128)}, u32[]{:S(2)}) copy-start(f32[10,128,128]{2,1,0:T(8,128)} %copy-done.18) | copy-start | bytes 1966084
  44.8 1.1 %copy-start.20 = (f32[10,128,128]{2,1,0:T(8,128)S(1)}, f32[10,128,128]{2,1,0:T(8,128)}, u32[]{:S(2)}) copy-start(f32[10,128,128]{2,1,0:T(8,128)} %copy-done.18) | copy-start | bytes 1966084
  47.8 25.5 %all-to-all-start = ((bf16[8,160,128]{2,1,0:T(8,128)(2,1)}), bf16[8,160,128]{2,1,0:T(8,128)(2,1)S(1)}, u32[]{:S(2)}, u32[]{:S(2)}) async-start(bf16[8,160,128]{2,1,0:T(8,128)(2,1)} %attend_last.1), calls=%async_computation | async-start | bytes 655360 | tf_op jit(solution)/shard_map/all_to_all | solution.py:393
  57.5 7.1 %collective-permute-start.11 = (bf16[128,1024]{1,0:T(8,128)(2,1)S(1)}, bf16[128,1024]{1,0:T(8,128)(2,1)S(1)}, u32[]{:S(2)}, u32[]{:S(2)}) collective-permute-start(bf16[128,1024]{1,0:T(8,128)(2,1)S(1)} %pad_maximum_fusion.ta_ref), channel_id=1, source_target_pairs={{0,64},{16,80},{32,96},{48,112},{64,128},{80,144},{96,160},{112,17... | collective-permute-start | bytes 786440 | tf_op jit(solution)/shard_map/ppermute | solution.py:285
  57.8 8.6 %collective-permute-start.13 = (bf16[128,1024]{1,0:T(8,128)(2,1)S(1)}, bf16[128,1024]{1,0:T(8,128)(2,1)S(1)}, u32[]{:S(2)}, u32[]{:S(2)}) collective-permute-start(bf16[128,1024]{1,0:T(8,128)(2,1)S(1)} %pad_maximum_fusion.ta_ref), channel_id=1, source_target_pairs={{0,192},{16,208},{32,224},{48,240},{64,0},{80,16},{96,32},{112,48}... | collective-permute-start | bytes 786440 | tf_op jit(solution)/shard_map/ppermute | solution.py:285
  64.6 5.1 %copy-start.3 = (bf16[128,1024]{1,0:T(8,128)(2,1)}, bf16[128,1024]{1,0:T(8,128)(2,1)S(1)}, u32[]{:S(2)}) copy-start(bf16[128,1024]{1,0:T(8,128)(2,1)S(1)} %collective-permute-done.11.tb_ref) | copy-start | bytes 786436
  64.6 5.0 %collective-permute-start.12 = (bf16[64,1024]{1,0:T(8,128)(2,1)S(1)}, bf16[64,1024]{1,0:T(8,128)(2,1)S(1)}, u32[]{:S(2)}, u32[]{:S(2)}) collective-permute-start(bf16[64,1024]{1,0:T(8,128)(2,1)S(1)} %slice.8), channel_id=1, source_target_pairs={{0,64},{16,80},{32,96},{48,112},{64,128},{80,144},{96,160},{112,17... | collective-permute-start | bytes 393224 | tf_op jit(solution)/shard_map/ppermute | solution.py:285
  66.4 3.2 %copy-start.5 = (bf16[128,1024]{1,0:T(8,128)(2,1)}, bf16[128,1024]{1,0:T(8,128)(2,1)S(1)}, u32[]{:S(2)}) copy-start(bf16[128,1024]{1,0:T(8,128)(2,1)S(1)} %collective-permute-done.13.te_ref) | copy-start | bytes 786436
  66.4 6.3 %collective-permute-start.14 = (bf16[64,1024]{1,0:T(8,128)(2,1)S(1)}, bf16[64,1024]{1,0:T(8,128)(2,1)S(1)}, u32[]{:S(2)}, u32[]{:S(2)}) collective-permute-start(bf16[64,1024]{1,0:T(8,128)(2,1)S(1)} %slice.9), channel_id=1, source_target_pairs={{0,192},{16,208},{32,224},{48,240},{64,0},{80,16},{96,32},{112,48}... | collective-permute-start | bytes 393224 | tf_op jit(solution)/shard_map/ppermute | solution.py:285
  69.6 0.7 copy-start.8
  72.7 0.6 copy-start.10
  73.3 1.0 copy-start.4
  74.3 0.9 copy-start.6
  75.2 0.9 copy-start.9
  76.1 0.9 copy-start.11
  79.2 16.2 %all-to-all-start.1 = ((f32[16,16,128]{2,1,0:T(8,128)}), f32[16,16,128]{2,1,0:T(8,128)S(1)}, u32[]{:S(2)}, u32[]{:S(2)}) async-start(f32[16,16,128]{2,1,0:T(8,128)} %state.1), calls=%async_computation.1 | async-start | bytes 262144 | tf_op jit(solution)/shard_map/all_to_all | solution.py:404
  86.9 1.0 copy-start.7

commit v5 on v4

--- a/solution.py
+++ b/solution.py
@@ -18,8 +18,9 @@
 MASKED = -1e30
 ROW_K, ROW_V, ROW_Q, ROWS_A = 0, 128, 256, 384
 ROW_E, ROW_X, ROWS_B = 128, 144, 160
-FAR = (2, 3, 6, 7)
-NEAR = (0, 1, 4, 5)
+NEAR = (0, 1, 4)
+LATE = (2, 3, 6, 7, 5)
+PLACES = 0x65724310
 SETS = [[0, 1, 2, 3, 8, 9, 10, 11], [4, 5, 6, 7, 12, 13, 14, 15]]
 LIST = 128
 GRANT = pltpu.CompilerParams(vmem_limit_bytes=16 << 20)
@@ -38,7 +39,7 @@
 
 
 def place_of(q):
-    return q % 2 + (q // 4) * 2 + ((q // 2) % 2) * 4
+    return (PLACES >> (4 * q)) & 7
 
 
 def silu(x):
@@ -75,7 +76,7 @@
             apart = j ^ me
             cross = (apart // 4) % 2
             q = (apart // 8) * 4 + apart % 4
-            late = cross * ((q // 2) % 2)
+            late = cross * (place_of(q) >= len(NEAR)).astype(jnp.int32)
             code = (place_of(t ^ head_of(me)) * 16 + cross * 8 + place_of(q)) * 16 + b - j
             first, second = counts
             list_ref[jnp.where(late == 1, LIST + second, first)] = code
@@ -112,16 +113,22 @@
 def project_kernel(blocks_ref, tail_ref, x_ref, gain_ref, w_ref, gate_ref, extra_ref, *out_refs):
     me = lax.axis_index("seq")
     normed = (layer_norm(x_ref[...].astype(jnp.float32)) * gain_ref[...]).astype(jnp.bfloat16)
-    for q, out_ref in zip(FAR + NEAR, out_refs):
-        head = head_of(me) ^ q
-
-        def part(group, head=head):
-            columns = pl.ds(pl.multiple_of((group * HEADS + head) * HD, HD), HD)
-            return silu(jnp.dot(normed, w_ref[:, columns], preferred_element_type=jnp.float32))
-
-        out_ref[ROW_K:ROW_V, :] = part(2).T.astype(jnp.bfloat16)
-        out_ref[ROW_V:ROW_Q, :] = part(3).astype(jnp.bfloat16)
-        out_ref[ROW_Q:ROWS_A, :] = part(1).astype(jnp.bfloat16)
+    mine = head_of(me)
+    outs = dict(zip(NEAR + LATE, out_refs))
+    for q in (2, 6, 0, 4):
+        odd = (mine ^ q) % 2 == 1
+
+        def pair(group, q=q, odd=odd):
+            first = (mine ^ q) // 2 * 2
+            columns = pl.ds(pl.multiple_of((group * HEADS + first) * HD, 2 * HD), 2 * HD)
+            both = silu(jnp.dot(normed, w_ref[:, columns], preferred_element_type=jnp.float32))
+            low, high = both[:, :HD], both[:, HD:]
+            return jnp.where(odd, high, low), jnp.where(odd, low, high)
+
+        for here, key, value, query in zip((q, q + 1), pair(2), pair(3), pair(1)):
+            outs[here][ROW_K:ROW_V, :] = key.T.astype(jnp.bfloat16)
+            outs[here][ROW_V:ROW_Q, :] = value.astype(jnp.bfloat16)
+            outs[here][ROW_Q:ROWS_A, :] = query.astype(jnp.bfloat16)
     gate = silu(jnp.dot(normed, w_ref[:, :D], preferred_element_type=jnp.float32)).astype(jnp.bfloat16)
     gate_ref[...] = gate
 
@@ -156,21 +163,23 @@
 
 
 def sort_kernel(*refs):
-    got_refs, kv_ref, queries_ref = refs[:4], refs[4], refs[5]
+    got_refs, kv_ref, queries_ref = refs[:-2], refs[-2], refs[-1]
     for at, got_ref in enumerate(got_refs):
         kv_ref[at] = got_ref[ROW_K:ROW_Q, :]
         queries_ref[at] = got_ref[ROW_Q:ROWS_A, :]
 
 
 def attend_first_kernel(
-    list_ref, bias_ref, near_ref, far_ref, cross_ref, near_q_ref, far_q_ref, acc_ref, queries_ref, keep, acc
+    list_ref, bias_ref, near_ref, late_ref, cross_ref, near_q_ref, late_q_ref, acc_ref, queries_ref, keep, acc
 ):
-    for at in range(4):
+    near, late = len(NEAR), len(LATE)
+    for at in range(near):
         keep[at] = near_ref[at]
-        keep[4 + at] = far_ref[at]
-        keep[8 + at] = cross_ref[at]
+        keep[HEADS + at] = cross_ref[at]
         queries_ref[at] = near_q_ref[at]
-        queries_ref[4 + at] = far_q_ref[at]
+    for at in range(late):
+        keep[near + at] = late_ref[at]
+        queries_ref[near + at] = late_q_ref[at]
     acc[...] = jnp.zeros_like(acc)
     run_pairs(
         list_ref,
@@ -192,7 +201,7 @@
     acc[8] = jnp.zeros((BLK, HD), jnp.float32)
 
     def at(slot):
-        return slot % 4
+        return jnp.maximum(slot - HEADS - len(NEAR), 0)
 
     run_pairs(
         list_ref,
@@ -347,37 +356,35 @@
         cost_estimate=cost(2 * BLK * D * 4 * D, 10 << 20),
         compiler_params=GRANT,
     )(hist_blocks, hist_tail, x_here, in_gain[None, :], w_proj)
-    far_got, near_got = [], [sent[4]]
-    for q, value in zip(FAR, sent[:4]):
-        far_got.append(seq_xor(value, spread(q)))
-    for q, value in zip(NEAR[1:], sent[5:]):
-        near_got.append(seq_xor(value, spread(q)))
+    got = []
+    for q, value in zip(NEAR + LATE, sent):
+        got.append(seq_xor(value, spread(q)) if q else value)
 
     def sort(got):
         return pl.pallas_call(
             sort_kernel,
-            in_specs=[vmem()] * 4,
+            in_specs=[vmem()] * len(got),
             out_specs=[vmem()] * 2,
-            out_shape=[sds((4, ROW_Q, HD)), sds((4, BLK, HD))],
+            out_shape=[sds((len(got), ROW_Q, HD)), sds((len(got), BLK, HD))],
             cost_estimate=cost(1 << 10, 1 << 19),
             compiler_params=GRANT,
         )(*got)
 
-    near_kv, near_q = sort(near_got)
+    near_kv, near_q = sort(got[: len(NEAR)])
     near_cross = seq_xor(near_kv, 4)
-    far_kv, far_q = sort(far_got)
-    far_cross = seq_xor(far_kv, 4)
+    late_kv, late_q = sort(got[len(NEAR) :])
+    late_cross = seq_xor(late_kv, 4)
 
     part, queries = pl.pallas_call(
         attend_first_kernel,
         in_specs=[smem()] + [vmem()] * 6,
         out_specs=[vmem(), vmem()],
         out_shape=[sds((8, BLK, HD), jnp.float32), sds((8, BLK, HD))],
-        scratch_shapes=[pltpu.VMEM((12, ROW_Q, HD), jnp.bfloat16), pltpu.VMEM((9, BLK, HD), jnp.float32)],
+        scratch_shapes=[pltpu.VMEM((HEADS + len(NEAR), ROW_Q, HD), jnp.bfloat16), pltpu.VMEM((9, BLK, HD), jnp.float32)],
         name="attend_first",
         cost_estimate=cost(1 << 31, 4 << 20),
         compiler_params=GRANT,
-    )(pairs, bias, near_kv, far_kv, near_cross, near_q, far_q)
+    )(pairs, bias, near_kv, late_kv, near_cross, near_q, late_q)
 
     back = pl.pallas_call(
         attend_last_kernel,
@@ -388,7 +395,7 @@
         name="attend_last",
         cost_estimate=cost(1 << 30, 2 << 20),
         compiler_params=GRANT,
-    )(hist_blocks, hist_tail, pairs, bias, queries, far_cross, part, extra)
+    )(hist_blocks, hist_tail, pairs, bias, queries, late_cross, part, extra)
 
     mixed = lax.all_to_all(back, "seq", 0, 0, tiled=True, axis_index_groups=SETS)
 

time: 96.9 us -> 93 us (0.960)
  starting transfers between devices: 46.7 us -> 42.3 us
  waiting for transfers between devices: 19.9 us -> 22 us
  Pallas kernels: 17.1 us -> 15.5 us
    all_to_all x1, starting transfers between devices: 8.74 us -> 5.77 us  [layer(): lax.all_to_all(back, 'seq', 0, 0, tiled=True, axis_index_groups=SETS)]
    ppermute x6, waiting for transfers between devices: 10.2 us -> 11.7 us  [dp_shift(): return lax.ppermute(value, 'dp', [(i, move(i)) for i in range(16)])]
    ppermute x9, starting transfers between devices: 18.4 us -> 17.2 us  [seq_xor(): return lax.ppermute(value, 'seq', [(i, i ^ apart) for i in range(NSEQ)])]
where the time goes in v5:
time: 93 us; the launch traced here: 92.5 us
  starting transfers between devices  42.3 us (45%)
  waiting for transfers between devices  22 us (24%)
  Pallas kernels  15.5 us (17%)
  local copies, waits for them, and re-layouts  10.9 us (12%)
  other arithmetic  0.96 us (1%)
    ppermute x9, starting transfers between devices, seq_xor(): return lax.ppermute(value, 'seq', [(i, i ^ apart) for i in range(NSEQ)])  17.2 us
    ppermute x6, starting transfers between devices, dp_shift(): return lax.ppermute(value, 'dp', [(i, move(i)) for i in range(16)])  12 us
    ppermute x6, waiting for transfers between devices, dp_shift(): return lax.ppermute(value, 'dp', [(i, move(i)) for i in range(16)])  11.7 us
    unnamed x50, local copies, waits for them, and re-layouts  10.9 us
    all_to_all x1, starting transfers between devices, layer(): scores = lax.all_to_all(sent, 'seq', 0, 0, tiled=True)  7.32 us
    all_to_all x1, waiting for transfers between devices, layer(): scores = lax.all_to_all(sent, 'seq', 0, 0, tiled=True)  6.08 us
    all_to_all x1, starting transfers between devices, layer(): lax.all_to_all(back, 'seq', 0, 0, tiled=True, axis_index_groups=SETS)  5.77 us
    ppermute x9, waiting for transfers between devices, seq_xor(): return lax.ppermute(value, 'seq', [(i, i ^ apart) for i in range(NSEQ)])  4.15 us
  transfers between devices with their start and end apart: 17, of which 7 were waited for; matrix products, arithmetic and copies ran while one was open for 1% of the time, Pallas kernels for 7%

profile of v5, /device:TPU:6, one launch (start us, length us, event | category | flops | bytes accessed | tf_op | source)
XLA Modules:
  0.0 92.5 jit_solution(8811480282988402729)
XLA Ops:
  0.6 0.0 copy-start
  0.7 0.0 slice-start
  0.7 2.7 %prepare.1 = (f32[10,128,128]{2,1,0:T(8,128)S(1)}, s32[256]{0:T(256)S(1)}, s32[8,64]{1,0:T(8,128)S(1)}) custom-call(s32[1,3]{1,0:T(1,128)} %blocks_ref.7, f32[8]{0:T(128)} %slope_ref.1, s32[3,64]{1,0:T(4,128)} %ids_ref.1, s32[1,64]{1,0:T(1,128)} %bitcast.13), custom_call_target="tpu_custom_call" | custom-call | flops 4294967296 | bytes 16777216 | tf_op jit(solution)/shard_map/prepare/pallas_call | solution.py:335
  3.4 0.9 copy-done.18
  4.3 0.1 slice-done.1
  4.4 3.4 %project.1 = (bf16[128,1024]{1,0:T(8,128)(2,1)}, bf16[16,128]{1,0:T(8,128)(2,1)S(1)}, bf16[384,128]{1,0:T(8,128)(2,1)S(1)}, bf16[384,128]{1,0:T(8,128)(2,1)}, bf...) custom-call(s32[1,3]{1,0:T(1,128)S(1)} %copy-done.14, ...), custom_call_target="tpu_custom_call" | custom-call | flops 1073741824 | bytes 10485760 | tf_op jit(solution)/shard_map/project/pallas_call | solution.py:350
  7.8 0.6 copy-done.16
  8.4 0.6 copy-done.17
  9.1 1.9 %collective-permute-start = (bf16[384,128]{1,0:T(8,128)(2,1)}, bf16[384,128]{1,0:T(8,128)(2,1)S(1)}, u32[]{:S(2)}, u32[]{:S(2)}) collective-permute-start(bf16[384,128]{1,0:T(8,128)(2,1)} %get-tuple-element.26), channel_id=1, source_target_pairs={{0,1},{1,0},{2,3},{3,2},{4,5},{5,4},{6,7},{7,6},{8,9},{9,8},{10,11... | collective-permute-start | bytes 294920 | tf_op jit(solution)/shard_map/ppermute | solution.py:298
  11.0 3.2 %collective-permute-start.1 = (bf16[384,128]{1,0:T(8,128)(2,1)}, bf16[384,128]{1,0:T(8,128)(2,1)S(1)}, u32[]{:S(2)}, u32[]{:S(2)}) collective-permute-start(bf16[384,128]{1,0:T(8,128)(2,1)} %get-tuple-element.27), channel_id=1, source_target_pairs={{0,8},{1,9},{2,10},{3,11},{4,12},{5,13},{6,14},{7,15},{8,0},{9,1},... | collective-permute-start | bytes 294920 | tf_op jit(solution)/shard_map/ppermute | solution.py:298
  14.1 3.3 %collective-permute-start.2 = (bf16[384,128]{1,0:T(8,128)(2,1)}, bf16[384,128]{1,0:T(8,128)(2,1)S(1)}, u32[]{:S(2)}, u32[]{:S(2)}) collective-permute-start(bf16[384,128]{1,0:T(8,128)(2,1)} %get-tuple-element.29), channel_id=1, source_target_pairs={{0,2},{1,3},{2,0},{3,1},{4,6},{5,7},{6,4},{7,5},{8,10},{9,11},{10,... | collective-permute-start | bytes 294920 | tf_op jit(solution)/shard_map/ppermute | solution.py:298
  17.4 1.3 %collective-permute-start.4 = (bf16[384,128]{1,0:T(8,128)(2,1)}, bf16[384,128]{1,0:T(8,128)(2,1)S(1)}, u32[]{:S(2)}, u32[]{:S(2)}) collective-permute-start(bf16[384,128]{1,0:T(8,128)(2,1)} %get-tuple-element.31), channel_id=1, source_target_pairs={{0,10},{1,11},{2,8},{3,9},{4,14},{5,15},{6,12},{7,13},{8,2},{9,3},... | collective-permute-start | bytes 294920 | tf_op jit(solution)/shard_map/ppermute | solution.py:298
  18.8 4.0 %collective-permute-start.5 = (bf16[384,128]{1,0:T(8,128)(2,1)}, bf16[384,128]{1,0:T(8,128)(2,1)S(1)}, u32[]{:S(2)}, u32[]{:S(2)}) collective-permute-start(bf16[384,128]{1,0:T(8,128)(2,1)} %copy-done.17), channel_id=1, source_target_pairs={{0,11},{1,10},{2,9},{3,8},{4,15},{5,14},{6,13},{7,12},{8,3},{9,2},... | collective-permute-start | bytes 294920 | tf_op jit(solution)/shard_map/ppermute | solution.py:298
  22.8 1.6 %collective-permute-start.6 = (bf16[384,128]{1,0:T(8,128)(2,1)}, bf16[384,128]{1,0:T(8,128)(2,1)S(1)}, u32[]{:S(2)}, u32[]{:S(2)}) collective-permute-start(bf16[384,128]{1,0:T(8,128)(2,1)} %copy-done.16), channel_id=1, source_target_pairs={{0,9},{1,8},{2,11},{3,10},{4,13},{5,12},{6,15},{7,14},{8,1},{9,0},... | collective-permute-start | bytes 294920 | tf_op jit(solution)/shard_map/ppermute | solution.py:298
  24.4 3.3 %collective-permute-done.2.refs_0_ = bf16[384,128]{1,0:T(8,128)(2,1)S(1)} collective-permute-done((bf16[384,128]{1,0:T(8,128)(2,1)}, bf16[384,128]{1,0:T(8,128)(2,1)S(1)}, u32[]{:S(2)}, u32[]{:S(2)}) %collective-permute-start.2) | collective-permute-done | bytes 98336 | tf_op jit(solution)/shard_map/ppermute | solution.py:298
  27.7 0.6 collective-permute-start.7
  28.3 7.2 %collective-permute-start.9 = (bf16[32,1024]{1,0:T(8,128)(2,1)S(1)}, bf16[32,1024]{1,0:T(8,128)(2,1)S(1)}, u32[]{:S(2)}, u32[]{:S(2)}) collective-permute-start(bf16[32,1024]{1,0:T(8,128)(2,1)S(1)} %constant_dynamic-slice_fusion), channel_id=1, source_target_pairs={{0,32},{16,48},{32,0},{48,16},{64,96},{80,112},{96,64},{112,80},{1... | collective-permute-start | bytes 196616 | tf_op jit(solution)/shard_map/ppermute | solution.py:294
  35.5 1.4 %collective-permute-start.8 = (bf16[5,256,128]{2,1,0:T(8,128)(2,1)S(1)}, bf16[5,256,128]{2,1,0:T(8,128)(2,1)S(1)}, u32[]{:S(2)}, u32[]{:S(2)}) collective-permute-start(bf16[5,256,128]{2,1,0:T(8,128)(2,1)S(1)} %get-tuple-element.34.late_ref), channel_id=1, source_target_pairs={{0,4},{1,5},{2,6},{3,7},{4,0},{5,1},{6,2},{7,3},{8,12},{9,13},{10,... | collective-permute-start | bytes 983048 | tf_op jit(solution)/shard_map/ppermute | solution.py:298
  36.9 0.9 %collective-permute-done.9 = bf16[32,1024]{1,0:T(8,128)(2,1)S(1)} collective-permute-done((bf16[32,1024]{1,0:T(8,128)(2,1)S(1)}, bf16[32,1024]{1,0:T(8,128)(2,1)S(1)}, u32[]{:S(2)}, u32[]{:S(2)}) %collective-permute-start.9) | collective-permute-done | bytes 65568 | tf_op jit(solution)/shard_map/ppermute | solution.py:294
  37.8 0.1 collective-permute-start.10
  37.9 0.5 copy-done.22
  38.4 1.1 %copy-done.19 = f32[10,128,128]{2,1,0:T(8,128)S(1)} copy-done((f32[10,128,128]{2,1,0:T(8,128)S(1)}, f32[10,128,128]{2,1,0:T(8,128)}, u32[]{:S(2)}) %copy-start.19) | copy-done | bytes 655384
  39.5 3.1 %attend_first.1 = (f32[8,128,128]{2,1,0:T(8,128)S(1)}, bf16[8,128,128]{2,1,0:T(8,128)(2,1)S(1)}) custom-call(s32[256]{0:T(256)S(1)} %get-tuple-element.22.list_ref, f32[10,128,128]{2,1,0:T(8,128)S(1)} %copy-done.19, bf16[3,256,128]{2,1,0:T(8,128)(2,1)S(1)} %get-tuple-element.28.near_ref, bf16[5,256,128]{2,1,0:T(8,128)(2,1)S(1)} %get-tuple-element.34.late_ref, ...), custom_call_target="tpu_custom_call" | custom-call | flops 2147483648 | bytes 4194304 | tf_op jit(solution)/shard_map/attend_first/pallas_call | solution.py:378
  42.6 0.8 collective-permute-done.8.cross_ref
  43.4 1.1 %copy-done.20 = f32[10,128,128]{2,1,0:T(8,128)S(1)} copy-done((f32[10,128,128]{2,1,0:T(8,128)S(1)}, f32[10,128,128]{2,1,0:T(8,128)}, u32[]{:S(2)}) %copy-start.20) | copy-done | bytes 655384
  44.5 1.8 %attend_last.1 = bf16[8,160,128]{2,1,0:T(8,128)(2,1)} custom-call(s32[1,3]{1,0:T(1,128)S(1)} %copy-done.14, s32[1,3]{1,0:T(1,128)S(1)} %copy-done.15, s32[256]{0:T(256)S(1)} %get-tuple-element.22.list_ref, f32[10,128,128]{2,1,0:T(8,128)S(1)} %copy-done.20, bf16[8,128,128]{2,1,0:T(8,128)(2,1)S(1)} %get-tuple-element.37.queries_ref, ...), custom_call_target="tpu_custom_call" | custom-call | flops 1073741824 | bytes 2097152 | tf_op jit(solution)/shard_map/attend_last/pallas_call | solution.py:389
  46.2 5.8 %all-to-all-start = ((bf16[8,160,128]{2,1,0:T(8,128)(2,1)}), bf16[8,160,128]{2,1,0:T(8,128)(2,1)S(1)}, u32[]{:S(2)}, u32[]{:S(2)}) async-start(bf16[8,160,128]{2,1,0:T(8,128)(2,1)} %attend_last.1), calls=%async_computation | async-start | bytes 655360 | tf_op jit(solution)/shard_map/all_to_all | solution.py:400
  52.0 1.0 %pad_maximum_fusion.ta_ref = bf16[128,1024]{1,0:T(8,128)(2,1)S(1)} fusion(bf16[64,1024]{1,0:T(8,128)(2,1)} %collective-permute-done.10, bf16[32,1024]{1,0:T(8,128)(2,1)} %copy-done.22, bf16[32,1024]{1,0:T(8,128)(2,1)} %copy-done.21), kind=kLoop, calls=%fused_computation | loop fusion | flops 786432 | bytes 524288 | tf_op jit(solution)/shard_map/concatenate | solution.py:328
  53.0 0.8 collective-permute-start.11
  53.7 1.4 %collective-permute-start.13 = (bf16[128,1024]{1,0:T(8,128)(2,1)S(1)}, bf16[128,1024]{1,0:T(8,128)(2,1)S(1)}, u32[]{:S(2)}, u32[]{:S(2)}) collective-permute-start(bf16[128,1024]{1,0:T(8,128)(2,1)S(1)} %pad_maximum_fusion.ta_ref), channel_id=1, source_target_pairs={{0,192},{16,208},{32,224},{48,240},{64,0},{80,16},{96,32},{112,48}... | collective-permute-start | bytes 786440 | tf_op jit(solution)/shard_map/ppermute | solution.py:294
  55.1 5.3 %collective-permute-done.11.tb_ref = bf16[128,1024]{1,0:T(8,128)(2,1)S(1)} collective-permute-done((bf16[128,1024]{1,0:T(8,128)(2,1)S(1)}, bf16[128,1024]{1,0:T(8,128)(2,1)S(1)}, u32[]{:S(2)}, u32[]{:S(2)}) %collective-permute-start.11) | collective-permute-done | bytes 262176 | tf_op jit(solution)/shard_map/ppermute | solution.py:294
  60.4 2.6 %collective-permute-start.12 = (bf16[64,1024]{1,0:T(8,128)(2,1)S(1)}, bf16[64,1024]{1,0:T(8,128)(2,1)S(1)}, u32[]{:S(2)}, u32[]{:S(2)}) collective-permute-start(bf16[64,1024]{1,0:T(8,128)(2,1)S(1)} %slice.8), channel_id=1, source_target_pairs={{0,64},{16,80},{32,96},{48,112},{64,128},{80,144},{96,160},{112,17... | collective-permute-start | bytes 393224 | tf_op jit(solution)/shard_map/ppermute | solution.py:294
  63.0 0.1 collective-permute-start.14
  63.0 2.5 %collective-permute-done.12.tc_ref = bf16[64,1024]{1,0:T(8,128)(2,1)S(1)} collective-permute-done((bf16[64,1024]{1,0:T(8,128)(2,1)S(1)}, bf16[64,1024]{1,0:T(8,128)(2,1)S(1)}, u32[]{:S(2)}, u32[]{:S(2)}) %collective-permute-start.12) | collective-permute-done | bytes 131104 | tf_op jit(solution)/shard_map/ppermute | solution.py:294
  65.6 0.7 copy-done.8
  66.2 3.0 %collective-permute-done.14.td_ref = bf16[64,1024]{1,0:T(8,128)(2,1)S(1)} collective-permute-done((bf16[64,1024]{1,0:T(8,128)(2,1)S(1)}, bf16[64,1024]{1,0:T(8,128)(2,1)S(1)}, u32[]{:S(2)}, u32[]{:S(2)}) %collective-permute-start.14) | collective-permute-done | bytes 131104 | tf_op jit(solution)/shard_map/ppermute | solution.py:294
  69.2 0.6 copy-done.10
  69.9 0.9 %copy-done.4 = bf16[128,1024]{1,0:T(8,128)(2,1)S(1)} copy-done((bf16[128,1024]{1,0:T(8,128)(2,1)S(1)}, bf16[128,1024]{1,0:T(8,128)(2,1)}, u32[]{:S(2)}) %copy-start.4) | copy-done | bytes 262168
  70.8 0.9 %copy-done.6 = bf16[128,1024]{1,0:T(8,128)(2,1)S(1)} copy-done((bf16[128,1024]{1,0:T(8,128)(2,1)S(1)}, bf16[128,1024]{1,0:T(8,128)(2,1)}, u32[]{:S(2)}) %copy-start.6) | copy-done | bytes 262168
  71.8 0.9 copy-done.9
  72.7 0.9 copy-done.11
  73.6 2.1 %state.1 = f32[16,16,128]{2,1,0:T(8,128)} custom-call(s32[1,3]{1,0:T(1,128)S(1)} %copy-done.14, bf16[8,160,128]{2,1,0:T(8,128)(2,1)S(1)} %all-to-all-done.mixed_ref, f32[1,1024]{1,0:T(1,128)S(1)} %bitcast.9, bf16[1024,1024]{1,0:T(8,128)(2,1)S(1)} %copy-done.1, bf16[128,1024]{1,0:T(8,128)(2,1)S(1)} %pad_maximum_fusion.ta_ref, ...), custom_call_target="tpu_custom_call" | custom-call | flops 33554432 | bytes 3145728 | tf_op jit(solution)/shard_map/state/pallas_call | solution.py:402
  75.7 7.3 %all-to-all-start.1 = ((f32[16,16,128]{2,1,0:T(8,128)}), f32[16,16,128]{2,1,0:T(8,128)S(1)}, u32[]{:S(2)}, u32[]{:S(2)}) async-start(f32[16,16,128]{2,1,0:T(8,128)} %state.1), calls=%async_computation.1 | async-start | bytes 262144 | tf_op jit(solution)/shard_map/all_to_all | solution.py:411
  83.0 0.0 copy-start.7
  83.0 0.9 %copy-done.7 = bf16[128,1024]{1,0:T(8,128)(2,1)S(1)} copy-done((bf16[128,1024]{1,0:T(8,128)(2,1)S(1)}, bf16[128,1024]{1,0:T(8,128)(2,1)}, u32[]{:S(2)}) %copy-start.7) | copy-done | bytes 262168
  84.0 1.4 %layer.1 = bf16[128,1024]{1,0:T(8,128)(2,1)} custom-call(bf16[8,160,128]{2,1,0:T(8,128)(2,1)S(1)} %all-to-all-done.mixed_ref, bf16[128,1024]{1,0:T(8,128)(2,1)S(1)} %copy-done.7, bf16[128,1024]{1,0:T(8,128)(2,1)S(1)} %bitcast.8, f32[1,1024]{1,0:T(1,128)S(1)} %bitcast.10, bf16[1024,1024]{1,0:T(8,128)(2,1)S(1)} %copy-done.1), custom_call_target="tpu_custom_call" | custom-call | flops 268435456 | bytes 3145728 | tf_op jit(solution)/shard_map/layer/pallas_call | solution.py:413
  85.3 6.1 %all-to-all-done.1.score_ref = f32[16,16,128]{2,1,0:T(8,128)S(1)} async-done(((f32[16,16,128]{2,1,0:T(8,128)}), f32[16,16,128]{2,1,0:T(8,128)S(1)}, u32[]{:S(2)}, u32[]{:S(2)}) %all-to-all-start.1) | async-done | bytes 131104 | tf_op jit(solution)/shard_map/all_to_all | solution.py:411
  91.4 1.1 %pick.1 = f32[3,64]{1,0:T(4,128)} custom-call(f32[16,16,128]{2,1,0:T(8,128)S(1)} %all-to-all-done.1.score_ref, s32[8,64]{1,0:T(8,128)S(1)} %get-tuple-element.41.place_ref), custom_call_target="tpu_custom_call" | custom-call | flops 1048576 | bytes 131072 | tf_op jit(solution)/shard_map/pick/pallas_call | solution.py:423
  (51 shorter events, 0.2 us)
Async XLA Ops:
  0.6 27.6 %copy-start = (bf16[256,1024]{1,0:T(8,128)(2,1)S(1)}, bf16[256,1024]{1,0:T(8,128)(2,1)}, u32[]{:S(2)}) copy-start(bf16[256,1024]{1,0:T(8,128)(2,1)} %param.19) | copy-start | bytes 1572868
  0.6 3.6 %copy-start.14 = (s32[1,3]{1,0:T(1,128)S(1)}, s32[1,3]{1,0:T(1,128)}, u32[]{:S(2)}) copy-start(s32[1,3]{1,0:T(1,128)} %blocks_ref.7) | copy-start | bytes 40
  0.7 3.6 %copy-start.2 = (bf16[1,128,1024]{2,1,0:T(8,128)(2,1)S(1)}, bf16[1,128,1024]{2,1,0:T(8,128)(2,1)}, u32[]{:S(2)}) copy-start(bf16[1,128,1024]{2,1,0:T(8,128)(2,1)} %param.11) | copy-start | bytes 786436
  0.7 3.6 %copy-start.13 = (f32[1024]{0:T(1024)S(1)}, f32[1024]{0:T(1024)}, u32[]{:S(2)}) copy-start(f32[1024]{0:T(1024)} %param.12) | copy-start | bytes 12292
  0.7 3.6 %slice-start = ((s8[8388608]{0:T(1024)(128)(4,1)}), s8[4194304]{0:T(1024)(128)(4,1)S(1)}, s32[]{:S(2)}) async-start(s8[8388608]{0:T(1024)(128)(4,1)} %bitcast.5), calls=%async_computation.2 | async-start | bytes 8388608
  0.7 3.6 %copy-start.15 = (s32[1,3]{1,0:T(1,128)S(1)}, s32[1,3]{1,0:T(1,128)}, u32[]{:S(2)}) copy-start(s32[1,3]{1,0:T(1,128)} %tail_ref.3) | copy-start | bytes 40
  0.7 3.7 %slice-start.1 = ((s8[8388608]{0:T(1024)(128)(4,1)}), s8[4194304]{0:T(1024)(128)(4,1)S(1)}, s32[]{:S(2)}) async-start(s8[8388608]{0:T(1024)(128)(4,1)} %bitcast.5), calls=%async_computation.3 | async-start | bytes 8388608
  3.4 0.9 copy-start.18
  7.8 0.6 copy-start.16
  8.4 0.7 copy-start.17
  9.0 60.8 %copy-start.1 = (bf16[1024,1024]{1,0:T(8,128)(2,1)S(1)}, bf16[1024,1024]{1,0:T(8,128)(2,1)}, u32[]{:S(2)}) copy-start(bf16[1024,1024]{1,0:T(8,128)(2,1)} %w_ref.5) | copy-start | bytes 6291460
  9.1 60.8 %copy-start.12 = (f32[1024]{0:T(1024)S(1)}, f32[1024]{0:T(1024)}, u32[]{:S(2)}) copy-start(f32[1024]{0:T(1024)} %param.14) | copy-start | bytes 12292
  9.1 9.7 %collective-permute-start = (bf16[384,128]{1,0:T(8,128)(2,1)}, bf16[384,128]{1,0:T(8,128)(2,1)S(1)}, u32[]{:S(2)}, u32[]{:S(2)}) collective-permute-start(bf16[384,128]{1,0:T(8,128)(2,1)} %get-tuple-element.26), channel_id=1, source_target_pairs={{0,1},{1,0},{2,3},{3,2},{4,5},{5,4},{6,7},{7,6},{8,9},{9,8},{10,11... | collective-permute-start | bytes 294920 | tf_op jit(solution)/shard_map/ppermute | solution.py:298
  11.0 11.8 %collective-permute-start.1 = (bf16[384,128]{1,0:T(8,128)(2,1)}, bf16[384,128]{1,0:T(8,128)(2,1)S(1)}, u32[]{:S(2)}, u32[]{:S(2)}) collective-permute-start(bf16[384,128]{1,0:T(8,128)(2,1)} %get-tuple-element.27), channel_id=1, source_target_pairs={{0,8},{1,9},{2,10},{3,11},{4,12},{5,13},{6,14},{7,15},{8,0},{9,1},... | collective-permute-start | bytes 294920 | tf_op jit(solution)/shard_map/ppermute | solution.py:298
  14.1 13.6 %collective-permute-start.2 = (bf16[384,128]{1,0:T(8,128)(2,1)}, bf16[384,128]{1,0:T(8,128)(2,1)S(1)}, u32[]{:S(2)}, u32[]{:S(2)}) collective-permute-start(bf16[384,128]{1,0:T(8,128)(2,1)} %get-tuple-element.29), channel_id=1, source_target_pairs={{0,2},{1,3},{2,0},{3,1},{4,6},{5,7},{6,4},{7,5},{8,10},{9,11},{10,... | collective-permute-start | bytes 294920 | tf_op jit(solution)/shard_map/ppermute | solution.py:298
  17.4 10.8 %collective-permute-start.3 = (bf16[384,128]{1,0:T(8,128)(2,1)}, bf16[384,128]{1,0:T(8,128)(2,1)S(1)}, u32[]{:S(2)}, u32[]{:S(2)}) collective-permute-start(bf16[384,128]{1,0:T(8,128)(2,1)} %get-tuple-element.30), channel_id=1, source_target_pairs={{0,3},{1,2},{2,1},{3,0},{4,7},{5,6},{6,5},{7,4},{8,11},{9,10},{10,... | collective-permute-start | bytes 294920 | tf_op jit(solution)/shard_map/ppermute | solution.py:298
  17.4 18.0 %collective-permute-start.4 = (bf16[384,128]{1,0:T(8,128)(2,1)}, bf16[384,128]{1,0:T(8,128)(2,1)S(1)}, u32[]{:S(2)}, u32[]{:S(2)}) collective-permute-start(bf16[384,128]{1,0:T(8,128)(2,1)} %get-tuple-element.31), channel_id=1, source_target_pairs={{0,10},{1,11},{2,8},{3,9},{4,14},{5,15},{6,12},{7,13},{8,2},{9,3},... | collective-permute-start | bytes 294920 | tf_op jit(solution)/shard_map/ppermute | solution.py:298
  18.8 16.7 %collective-permute-start.5 = (bf16[384,128]{1,0:T(8,128)(2,1)}, bf16[384,128]{1,0:T(8,128)(2,1)S(1)}, u32[]{:S(2)}, u32[]{:S(2)}) collective-permute-start(bf16[384,128]{1,0:T(8,128)(2,1)} %copy-done.17), channel_id=1, source_target_pairs={{0,11},{1,10},{2,9},{3,8},{4,15},{5,14},{6,13},{7,12},{8,3},{9,2},... | collective-permute-start | bytes 294920 | tf_op jit(solution)/shard_map/ppermute | solution.py:298
  22.8 12.7 %collective-permute-start.6 = (bf16[384,128]{1,0:T(8,128)(2,1)}, bf16[384,128]{1,0:T(8,128)(2,1)S(1)}, u32[]{:S(2)}, u32[]{:S(2)}) collective-permute-start(bf16[384,128]{1,0:T(8,128)(2,1)} %copy-done.16), channel_id=1, source_target_pairs={{0,9},{1,8},{2,11},{3,10},{4,13},{5,12},{6,15},{7,14},{8,1},{9,0},... | collective-permute-start | bytes 294920 | tf_op jit(solution)/shard_map/ppermute | solution.py:298
  27.7 10.2 %collective-permute-start.7 = (bf16[3,256,128]{2,1,0:T(8,128)(2,1)S(1)}, bf16[3,256,128]{2,1,0:T(8,128)(2,1)S(1)}, u32[]{:S(2)}, u32[]{:S(2)}) collective-permute-start(bf16[3,256,128]{2,1,0:T(8,128)(2,1)S(1)} %get-tuple-element.28.near_ref), channel_id=1, source_target_pairs={{0,4},{1,5},{2,6},{3,7},{4,0},{5,1},{6,2},{7,3},{8,12},{9,13},{10,... | collective-permute-start | bytes 589832 | tf_op jit(solution)/shard_map/ppermute | solution.py:298
  28.3 18.0 %copy-start.21 = (bf16[32,1024]{1,0:T(8,128)(2,1)}, bf16[32,1024]{1,0:T(8,128)(2,1)S(1)}, u32[]{:S(2)}) copy-start(bf16[32,1024]{1,0:T(8,128)(2,1)S(1)} %constant_dynamic-slice_fusion) | copy-start | bytes 196612
  28.3 9.5 %collective-permute-start.9 = (bf16[32,1024]{1,0:T(8,128)(2,1)S(1)}, bf16[32,1024]{1,0:T(8,128)(2,1)S(1)}, u32[]{:S(2)}, u32[]{:S(2)}) collective-permute-start(bf16[32,1024]{1,0:T(8,128)(2,1)S(1)} %constant_dynamic-slice_fusion), channel_id=1, source_target_pairs={{0,32},{16,48},{32,0},{48,16},{64,96},{80,112},{96,64},{112,80},{1... | collective-permute-start | bytes 196616 | tf_op jit(solution)/shard_map/ppermute | solution.py:294
  35.5 7.9 %collective-permute-start.8 = (bf16[5,256,128]{2,1,0:T(8,128)(2,1)S(1)}, bf16[5,256,128]{2,1,0:T(8,128)(2,1)S(1)}, u32[]{:S(2)}, u32[]{:S(2)}) collective-permute-start(bf16[5,256,128]{2,1,0:T(8,128)(2,1)S(1)} %get-tuple-element.34.late_ref), channel_id=1, source_target_pairs={{0,4},{1,5},{2,6},{3,7},{4,0},{5,1},{6,2},{7,3},{8,12},{9,13},{10,... | collective-permute-start | bytes 983048 | tf_op jit(solution)/shard_map/ppermute | solution.py:298
  37.8 0.6 copy-start.22
  37.8 14.2 %collective-permute-start.10 = (bf16[64,1024]{1,0:T(8,128)(2,1)S(1)}, bf16[64,1024]{1,0:T(8,128)(2,1)}, u32[]{:S(2)}, u32[]{:S(2)}) collective-permute-start(bf16[64,1024]{1,0:T(8,128)(2,1)S(1)} %pad_maximum_fusion.1), channel_id=1, source_target_pairs={{0,16},{16,0},{32,48},{48,32},{64,80},{80,64},{96,112},{112,96},{1... | collective-permute-start | bytes 393224 | tf_op jit(solution)/shard_map/ppermute | solution.py:294
  38.4 1.1 %copy-start.19 = (f32[10,128,128]{2,1,0:T(8,128)S(1)}, f32[10,128,128]{2,1,0:T(8,128)}, u32[]{:S(2)}) copy-start(f32[10,128,128]{2,1,0:T(8,128)} %copy-done.18) | copy-start | bytes 1966084
  43.4 1.1 %copy-start.20 = (f32[10,128,128]{2,1,0:T(8,128)S(1)}, f32[10,128,128]{2,1,0:T(8,128)}, u32[]{:S(2)}) copy-start(f32[10,128,128]{2,1,0:T(8,128)} %copy-done.18) | copy-start | bytes 1966084
  46.2 23.6 %all-to-all-start = ((bf16[8,160,128]{2,1,0:T(8,128)(2,1)}), bf16[8,160,128]{2,1,0:T(8,128)(2,1)S(1)}, u32[]{:S(2)}, u32[]{:S(2)}) async-start(bf16[8,160,128]{2,1,0:T(8,128)(2,1)} %attend_last.1), calls=%async_computation | async-start | bytes 655360 | tf_op jit(solution)/shard_map/all_to_all | solution.py:400
  53.0 7.4 %collective-permute-start.11 = (bf16[128,1024]{1,0:T(8,128)(2,1)S(1)}, bf16[128,1024]{1,0:T(8,128)(2,1)S(1)}, u32[]{:S(2)}, u32[]{:S(2)}) collective-permute-start(bf16[128,1024]{1,0:T(8,128)(2,1)S(1)} %pad_maximum_fusion.ta_ref), channel_id=1, source_target_pairs={{0,64},{16,80},{32,96},{48,112},{64,128},{80,144},{96,160},{112,17... | collective-permute-start | bytes 786440 | tf_op jit(solution)/shard_map/ppermute | solution.py:294
  53.7 9.2 %collective-permute-start.13 = (bf16[128,1024]{1,0:T(8,128)(2,1)S(1)}, bf16[128,1024]{1,0:T(8,128)(2,1)S(1)}, u32[]{:S(2)}, u32[]{:S(2)}) collective-permute-start(bf16[128,1024]{1,0:T(8,128)(2,1)S(1)} %pad_maximum_fusion.ta_ref), channel_id=1, source_target_pairs={{0,192},{16,208},{32,224},{48,240},{64,0},{80,16},{96,32},{112,48}... | collective-permute-start | bytes 786440 | tf_op jit(solution)/shard_map/ppermute | solution.py:294
  60.4 5.2 %copy-start.3 = (bf16[128,1024]{1,0:T(8,128)(2,1)}, bf16[128,1024]{1,0:T(8,128)(2,1)S(1)}, u32[]{:S(2)}) copy-start(bf16[128,1024]{1,0:T(8,128)(2,1)S(1)} %collective-permute-done.11.tb_ref) | copy-start | bytes 786436
  60.4 5.2 %collective-permute-start.12 = (bf16[64,1024]{1,0:T(8,128)(2,1)S(1)}, bf16[64,1024]{1,0:T(8,128)(2,1)S(1)}, u32[]{:S(2)}, u32[]{:S(2)}) collective-permute-start(bf16[64,1024]{1,0:T(8,128)(2,1)S(1)} %slice.8), channel_id=1, source_target_pairs={{0,64},{16,80},{32,96},{48,112},{64,128},{80,144},{96,160},{112,17... | collective-permute-start | bytes 393224 | tf_op jit(solution)/shard_map/ppermute | solution.py:294
  62.9 2.6 %copy-start.5 = (bf16[128,1024]{1,0:T(8,128)(2,1)}, bf16[128,1024]{1,0:T(8,128)(2,1)S(1)}, u32[]{:S(2)}) copy-start(bf16[128,1024]{1,0:T(8,128)(2,1)S(1)} %collective-permute-done.13.te_ref) | copy-start | bytes 786436
  63.0 6.3 %collective-permute-start.14 = (bf16[64,1024]{1,0:T(8,128)(2,1)S(1)}, bf16[64,1024]{1,0:T(8,128)(2,1)S(1)}, u32[]{:S(2)}, u32[]{:S(2)}) collective-permute-start(bf16[64,1024]{1,0:T(8,128)(2,1)S(1)} %slice.9), channel_id=1, source_target_pairs={{0,192},{16,208},{32,224},{48,240},{64,0},{80,16},{96,32},{112,48}... | collective-permute-start | bytes 393224 | tf_op jit(solution)/shard_map/ppermute | solution.py:294
  65.6 0.7 copy-start.8
  69.2 0.6 copy-start.10
  69.9 1.0 %copy-start.4 = (bf16[128,1024]{1,0:T(8,128)(2,1)S(1)}, bf16[128,1024]{1,0:T(8,128)(2,1)}, u32[]{:S(2)}) copy-start(bf16[128,1024]{1,0:T(8,128)(2,1)} %copy-done.3) | copy-start | bytes 786436
  70.8 0.9 %copy-start.6 = (bf16[128,1024]{1,0:T(8,128)(2,1)S(1)}, bf16[128,1024]{1,0:T(8,128)(2,1)}, u32[]{:S(2)}) copy-start(bf16[128,1024]{1,0:T(8,128)(2,1)} %copy-done.5) | copy-start | bytes 786436
  71.8 0.9 copy-start.9
  72.7 0.9 copy-start.11
  75.7 15.7 %all-to-all-start.1 = ((f32[16,16,128]{2,1,0:T(8,128)}), f32[16,16,128]{2,1,0:T(8,128)S(1)}, u32[]{:S(2)}, u32[]{:S(2)}) async-start(f32[16,16,128]{2,1,0:T(8,128)} %state.1), calls=%async_computation.1 | async-start | bytes 262144 | tf_op jit(solution)/shard_map/all_to_all | solution.py:411
  83.0 1.0 %copy-start.7 = (bf16[128,1024]{1,0:T(8,128)(2,1)S(1)}, bf16[128,1024]{1,0:T(8,128)(2,1)}, u32[]{:S(2)}) copy-start(bf16[128,1024]{1,0:T(8,128)(2,1)} %get-tuple-element.40.gate_ref) | copy-start | bytes 786436

commit v6 on v5

--- a/solution.py
+++ b/solution.py
@@ -58,15 +58,18 @@
     return (0, one, one + blocks_ref[0, 1])
 
 
-def prepare_kernel(blocks_ref, slope_ref, ids_ref, map_ref, bias_ref, list_ref, place_ref):
-    me, dp = lax.axis_index("seq"), lax.axis_index("dp")
-    starts = user_starts(blocks_ref)
-    slope = slope_ref[head_of(me)]
+def bias_kernel(slope_ref, bias_ref):
+    slope = slope_ref[head_of(lax.axis_index("seq"))]
     offset = lax.broadcasted_iota(jnp.int32, (BLK, BLK), 0) - lax.broadcasted_iota(jnp.int32, (BLK, BLK), 1)
     for d in range(MAXD):
         gap = offset + d * BLK
         table = slope * jnp.log(jnp.maximum(gap + 1, 1).astype(jnp.float32))
         bias_ref[d] = jnp.where(gap >= 0, table, MASKED) if d == 0 else table
+
+
+def prepare_kernel(blocks_ref, ids_ref, map_ref, list_ref, place_ref):
+    me, dp = lax.axis_index("seq"), lax.axis_index("dp")
+    starts = user_starts(blocks_ref)
 
     def fill(t, counts):
         b = (t // 4) * 8 + set_of(me) * 4 + t % 4
@@ -267,15 +270,12 @@
     scores = score_ref[...].reshape(NSEQ * 16, 128)
     row_at = lax.broadcasted_iota(jnp.int32, (NSEQ * 16, 64), 0)
     lane_at = lax.broadcasted_iota(jnp.int32, (128, 64), 0)
+    lanes = [place_ref[2 * user + 1 : 2 * user + 2, :] for user in range(USERS)]
+    hot = jnp.concatenate([(lane_at == lane).astype(jnp.float32) for lane in lanes], axis=1)
+    found = jnp.dot(scores, hot, preferred_element_type=jnp.float32, precision=lax.Precision.HIGHEST)
     for user in range(USERS):
-        row, lane = place_ref[2 * user : 2 * user + 1, :], place_ref[2 * user + 1 : 2 * user + 2, :]
-        found = jnp.dot(
-            scores,
-            (lane_at == lane).astype(jnp.float32),
-            preferred_element_type=jnp.float32,
-            precision=lax.Precision.HIGHEST,
-        )
-        out_ref[user : user + 1, :] = jnp.sum(jnp.where(row_at == row, found, 0.0), axis=0, keepdims=True)
+        mine = jnp.where(row_at == place_ref[2 * user : 2 * user + 1, :], found[:, user * 64 : (user + 1) * 64], 0.0)
+        out_ref[user : user + 1, :] = jnp.sum(mine, axis=0, keepdims=True)
 
 
 def vmem():
@@ -332,19 +332,15 @@
     opposite_last = dp_shift(above[64:], lambda i: (i + 12) % 16)
     table = [quad, below, opposite_first, opposite_last, above]
 
-    bias, pairs, places = pl.pallas_call(
+    pairs, places = pl.pallas_call(
         prepare_kernel,
-        in_specs=[smem(), smem(), vmem(), vmem()],
-        out_specs=[vmem(), smem(), vmem()],
-        out_shape=[
-            sds((MAXD, BLK, BLK), jnp.float32),
-            sds((2 * LIST,), jnp.int32),
-            sds((8, 64), jnp.int32),
-        ],
+        in_specs=[smem(), vmem(), vmem()],
+        out_specs=[smem(), vmem()],
+        out_shape=[sds((2 * LIST,), jnp.int32), sds((8, 64), jnp.int32)],
         name="prepare",
         cost_estimate=cost(1 << 32, 1 << 24),
         compiler_params=GRANT,
-    )(*(in_hbm(value) for value in (hist_blocks, rab_slope, beam_nodes, subtree_map[None, :])))
+    )(*(in_hbm(value) for value in (hist_blocks, beam_nodes, subtree_map[None, :])))
     x_here, _ = lax.optimization_barrier((x_rows, pairs))
 
     gate, extra, *sent = pl.pallas_call(
@@ -375,6 +371,15 @@
     late_kv, late_q = sort(got[len(NEAR) :])
     late_cross = seq_xor(late_kv, 4)
 
+    bias = pl.pallas_call(
+        bias_kernel,
+        in_specs=[smem()],
+        out_specs=vmem(),
+        out_shape=sds((MAXD, BLK, BLK), jnp.float32),
+        name="bias",
+        cost_estimate=cost(1 << 28, 1 << 20),
+        compiler_params=GRANT,
+    )(rab_slope)
     part, queries = pl.pallas_call(
         attend_first_kernel,
         in_specs=[smem()] + [vmem()] * 6,

time: 93 us -> 90.4 us (0.972)
  the two profiles are of different devices: /device:TPU:6 before, /device:TPU:128 now
where the time goes in v6:
time: 90.4 us; the launch traced here: 90 us
  starting transfers between devices  36.8 us (41%)
  waiting for transfers between devices  25.7 us (28%)
  Pallas kernels  17.2 us (19%)
  local copies, waits for them, and re-layouts  8.45 us (9%)
  other arithmetic  0.96 us (1%)
    ppermute x9, starting transfers between devices, seq_xor(): return lax.ppermute(value, 'seq', [(i, i ^ apart) for i in range(NSEQ)])  15.2 us
    ppermute x9, waiting for transfers between devices, seq_xor(): return lax.ppermute(value, 'seq', [(i, i ^ apart) for i in range(NSEQ)])  10.4 us
    ppermute x6, waiting for transfers between devices, dp_shift(): return lax.ppermute(value, 'dp', [(i, move(i)) for i in range(16)])  9.19 us
    unnamed x46, local copies, waits for them, and re-layouts  8.43 us
    all_to_all x1, starting transfers between devices, layer(): scores = lax.all_to_all(sent, 'seq', 0, 0, tiled=True)  7.6 us
    all_to_all x1, starting transfers between devices, layer(): lax.all_to_all(back, 'seq', 0, 0, tiled=True, axis_index_groups=SETS)  7.17 us
    ppermute x6, starting transfers between devices, dp_shift(): return lax.ppermute(value, 'dp', [(i, move(i)) for i in range(16)])  6.89 us
    all_to_all x1, waiting for transfers between devices, layer(): scores = lax.all_to_all(sent, 'seq', 0, 0, tiled=True)  6.09 us
  transfers between devices with their start and end apart: 17, of which 7 were waited for; matrix products, arithmetic and copies ran while one was open for 1% of the time, Pallas kernels for 8%

profile of v6, /device:TPU:128, one launch (start us, length us, event | category | flops | bytes accessed | tf_op | source)
XLA Modules:
  0.0 90.0 jit_solution(11934440831318759870)
XLA Ops:
  0.6 0.0 copy-start
  0.7 0.0 slice-start
  0.7 3.0 %prepare.1 = (s32[256]{0:T(256)S(1)}, s32[8,64]{1,0:T(8,128)S(1)}) custom-call(s32[1,3]{1,0:T(1,128)} %blocks_ref.7, s32[3,64]{1,0:T(4,128)} %ids_ref.1, s32[1,64]{1,0:T(1,128)} %bitcast.13), custom_call_target="tpu_custom_call" | custom-call | flops 4294967296 | bytes 16777216 | tf_op jit(solution)/shard_map/prepare/pallas_call | solution.py:335
  3.7 0.0 copy-start.18
  3.8 0.6 slice-done.1
  4.4 3.3 %project.1 = (bf16[128,1024]{1,0:T(8,128)(2,1)}, bf16[16,128]{1,0:T(8,128)(2,1)S(1)}, bf16[384,128]{1,0:T(8,128)(2,1)S(1)}, bf16[384,128]{1,0:T(8,128)(2,1)}, bf...) custom-call(s32[1,3]{1,0:T(1,128)S(1)} %copy-done.14, ...), custom_call_target="tpu_custom_call" | custom-call | flops 1073741824 | bytes 10485760 | tf_op jit(solution)/shard_map/project/pallas_call | solution.py:346
  7.7 0.6 copy-done.16
  8.4 0.6 copy-done.17
  9.0 1.0 %collective-permute-start = (bf16[384,128]{1,0:T(8,128)(2,1)}, bf16[384,128]{1,0:T(8,128)(2,1)S(1)}, u32[]{:S(2)}, u32[]{:S(2)}) collective-permute-start(bf16[384,128]{1,0:T(8,128)(2,1)} %get-tuple-element.24), channel_id=1, source_target_pairs={{0,1},{1,0},{2,3},{3,2},{4,5},{5,4},{6,7},{7,6},{8,9},{9,8},{10,11... | collective-permute-start | bytes 294920 | tf_op jit(solution)/shard_map/ppermute | solution.py:298
  10.0 3.2 %collective-permute-start.1 = (bf16[384,128]{1,0:T(8,128)(2,1)}, bf16[384,128]{1,0:T(8,128)(2,1)S(1)}, u32[]{:S(2)}, u32[]{:S(2)}) collective-permute-start(bf16[384,128]{1,0:T(8,128)(2,1)} %get-tuple-element.25), channel_id=1, source_target_pairs={{0,8},{1,9},{2,10},{3,11},{4,12},{5,13},{6,14},{7,15},{8,0},{9,1},... | collective-permute-start | bytes 294920 | tf_op jit(solution)/shard_map/ppermute | solution.py:298
  13.3 1.5 %collective-permute-start.2 = (bf16[384,128]{1,0:T(8,128)(2,1)}, bf16[384,128]{1,0:T(8,128)(2,1)S(1)}, u32[]{:S(2)}, u32[]{:S(2)}) collective-permute-start(bf16[384,128]{1,0:T(8,128)(2,1)} %get-tuple-element.27), channel_id=1, source_target_pairs={{0,2},{1,3},{2,0},{3,1},{4,6},{5,7},{6,4},{7,5},{8,10},{9,11},{10,... | collective-permute-start | bytes 294920 | tf_op jit(solution)/shard_map/ppermute | solution.py:298
  14.7 1.9 %collective-permute-start.3 = (bf16[384,128]{1,0:T(8,128)(2,1)}, bf16[384,128]{1,0:T(8,128)(2,1)S(1)}, u32[]{:S(2)}, u32[]{:S(2)}) collective-permute-start(bf16[384,128]{1,0:T(8,128)(2,1)} %get-tuple-element.28), channel_id=1, source_target_pairs={{0,3},{1,2},{2,1},{3,0},{4,7},{5,6},{6,5},{7,4},{8,11},{9,10},{10,... | collective-permute-start | bytes 294920 | tf_op jit(solution)/shard_map/ppermute | solution.py:298
  16.6 0.3 collective-permute-start.4
  17.0 4.5 %collective-permute-start.5 = (bf16[384,128]{1,0:T(8,128)(2,1)}, bf16[384,128]{1,0:T(8,128)(2,1)S(1)}, u32[]{:S(2)}, u32[]{:S(2)}) collective-permute-start(bf16[384,128]{1,0:T(8,128)(2,1)} %copy-done.17), channel_id=1, source_target_pairs={{0,11},{1,10},{2,9},{3,8},{4,15},{5,14},{6,13},{7,12},{8,3},{9,2},... | collective-permute-start | bytes 294920 | tf_op jit(solution)/shard_map/ppermute | solution.py:298
  21.5 0.8 collective-permute-start.6
  22.3 5.1 %collective-permute-done.2.refs_0_ = bf16[384,128]{1,0:T(8,128)(2,1)S(1)} collective-permute-done((bf16[384,128]{1,0:T(8,128)(2,1)}, bf16[384,128]{1,0:T(8,128)(2,1)S(1)}, u32[]{:S(2)}, u32[]{:S(2)}) %collective-permute-start.2) | collective-permute-done | bytes 98336 | tf_op jit(solution)/shard_map/ppermute | solution.py:298
  27.4 0.7 collective-permute-start.7
  28.1 0.1 collective-permute-start.9
  28.2 4.3 %collective-permute-done.4.refs_2_ = bf16[384,128]{1,0:T(8,128)(2,1)S(1)} collective-permute-done((bf16[384,128]{1,0:T(8,128)(2,1)}, bf16[384,128]{1,0:T(8,128)(2,1)S(1)}, u32[]{:S(2)}, u32[]{:S(2)}) %collective-permute-start.4) | collective-permute-done | bytes 98336 | tf_op jit(solution)/shard_map/ppermute | solution.py:298
  32.5 1.3 %collective-permute-start.8 = (bf16[5,256,128]{2,1,0:T(8,128)(2,1)S(1)}, bf16[5,256,128]{2,1,0:T(8,128)(2,1)S(1)}, u32[]{:S(2)}, u32[]{:S(2)}) collective-permute-start(bf16[5,256,128]{2,1,0:T(8,128)(2,1)S(1)} %get-tuple-element.32.late_ref), channel_id=1, source_target_pairs={{0,4},{1,5},{2,6},{3,7},{4,0},{5,1},{6,2},{7,3},{8,12},{9,13},{10,... | collective-permute-start | bytes 983048 | tf_op jit(solution)/shard_map/ppermute | solution.py:298
  33.8 0.7 bias.1.bias_ref
  34.5 2.0 %collective-permute-done.9 = bf16[32,1024]{1,0:T(8,128)(2,1)S(1)} collective-permute-done((bf16[32,1024]{1,0:T(8,128)(2,1)S(1)}, bf16[32,1024]{1,0:T(8,128)(2,1)S(1)}, u32[]{:S(2)}, u32[]{:S(2)}) %collective-permute-start.9) | collective-permute-done | bytes 65568 | tf_op jit(solution)/shard_map/ppermute | solution.py:294
  36.5 0.1 collective-permute-start.10
  36.6 0.5 copy-done.20
  37.1 3.4 %attend_first.1 = (f32[8,128,128]{2,1,0:T(8,128)S(1)}, bf16[8,128,128]{2,1,0:T(8,128)(2,1)S(1)}) custom-call(s32[256]{0:T(256)S(1)} %get-tuple-element.21.list_ref, f32[10,128,128]{2,1,0:T(8,128)S(1)} %bias.1.bias_ref, bf16[3,256,128]{2,1,0:T(8,128)(2,1)S(1)} %get-tuple-element.26.near_ref, bf16[5,256,128]{2,1,0:T(8,128)(2,1)S(1)} %get-tuple-element.32.late_ref, ...), custom_call_target="tpu_custom_call" | custom-call | flops 2147483648 | bytes 4194304 | tf_op jit(solution)/shard_map/attend_first/pallas_call | solution.py:383
  40.5 1.0 %collective-permute-done.8.cross_ref = bf16[5,256,128]{2,1,0:T(8,128)(2,1)S(1)} collective-permute-done((bf16[5,256,128]{2,1,0:T(8,128)(2,1)S(1)}, bf16[5,256,128]{2,1,0:T(8,128)(2,1)S(1)}, u32[]{:S(2)}, u32[]{:S(2)}) %collective-permute-start.8) | collective-permute-done | bytes 327712 | tf_op jit(solution)/shard_map/ppermute | solution.py:298
  41.6 2.1 %attend_last.1 = bf16[8,160,128]{2,1,0:T(8,128)(2,1)} custom-call(s32[1,3]{1,0:T(1,128)S(1)} %copy-done.14, s32[1,3]{1,0:T(1,128)S(1)} %copy-done.15, s32[256]{0:T(256)S(1)} %get-tuple-element.21.list_ref, f32[10,128,128]{2,1,0:T(8,128)S(1)} %bias.1.bias_ref, bf16[8,128,128]{2,1,0:T(8,128)(2,1)S(1)} %get-tuple-element.35.queries_ref, ...), custom_call_target="tpu_custom_call" | custom-call | flops 1073741824 | bytes 2097152 | tf_op jit(solution)/shard_map/attend_last/pallas_call | solution.py:394
  43.7 7.2 %all-to-all-start = ((bf16[8,160,128]{2,1,0:T(8,128)(2,1)}), bf16[8,160,128]{2,1,0:T(8,128)(2,1)S(1)}, u32[]{:S(2)}, u32[]{:S(2)}) async-start(bf16[8,160,128]{2,1,0:T(8,128)(2,1)} %attend_last.1), calls=%async_computation | async-start | bytes 655360 | tf_op jit(solution)/shard_map/all_to_all | solution.py:405
  50.8 1.0 %pad_maximum_fusion.ta_ref = bf16[128,1024]{1,0:T(8,128)(2,1)S(1)} fusion(bf16[64,1024]{1,0:T(8,128)(2,1)} %collective-permute-done.10, bf16[32,1024]{1,0:T(8,128)(2,1)} %copy-done.20, bf16[32,1024]{1,0:T(8,128)(2,1)} %copy-done.19), kind=kLoop, calls=%fused_computation | loop fusion | flops 786432 | bytes 524288 | tf_op jit(solution)/shard_map/concatenate | solution.py:328
  51.8 1.2 %collective-permute-start.11 = (bf16[128,1024]{1,0:T(8,128)(2,1)S(1)}, bf16[128,1024]{1,0:T(8,128)(2,1)S(1)}, u32[]{:S(2)}, u32[]{:S(2)}) collective-permute-start(bf16[128,1024]{1,0:T(8,128)(2,1)S(1)} %pad_maximum_fusion.ta_ref), channel_id=1, source_target_pairs={{0,64},{16,80},{32,96},{48,112},{64,128},{80,144},{96,160},{112,17... | collective-permute-start | bytes 786440 | tf_op jit(solution)/shard_map/ppermute | solution.py:294
  53.0 2.1 %collective-permute-start.13 = (bf16[128,1024]{1,0:T(8,128)(2,1)S(1)}, bf16[128,1024]{1,0:T(8,128)(2,1)S(1)}, u32[]{:S(2)}, u32[]{:S(2)}) collective-permute-start(bf16[128,1024]{1,0:T(8,128)(2,1)S(1)} %pad_maximum_fusion.ta_ref), channel_id=1, source_target_pairs={{0,192},{16,208},{32,224},{48,240},{64,0},{80,16},{96,32},{112,48}... | collective-permute-start | bytes 786440 | tf_op jit(solution)/shard_map/ppermute | solution.py:294
  55.1 4.3 %collective-permute-done.11.tb_ref = bf16[128,1024]{1,0:T(8,128)(2,1)S(1)} collective-permute-done((bf16[128,1024]{1,0:T(8,128)(2,1)S(1)}, bf16[128,1024]{1,0:T(8,128)(2,1)S(1)}, u32[]{:S(2)}, u32[]{:S(2)}) %collective-permute-start.11) | collective-permute-done | bytes 262176 | tf_op jit(solution)/shard_map/ppermute | solution.py:294
  59.5 0.5 collective-permute-start.12
  60.0 2.8 %collective-permute-start.14 = (bf16[64,1024]{1,0:T(8,128)(2,1)S(1)}, bf16[64,1024]{1,0:T(8,128)(2,1)S(1)}, u32[]{:S(2)}, u32[]{:S(2)}) collective-permute-start(bf16[64,1024]{1,0:T(8,128)(2,1)S(1)} %slice.9), channel_id=1, source_target_pairs={{0,192},{16,208},{32,224},{48,240},{64,0},{80,16},{96,32},{112,48}... | collective-permute-start | bytes 393224 | tf_op jit(solution)/shard_map/ppermute | solution.py:294
  62.9 2.8 %collective-permute-done.12.tc_ref = bf16[64,1024]{1,0:T(8,128)(2,1)S(1)} collective-permute-done((bf16[64,1024]{1,0:T(8,128)(2,1)S(1)}, bf16[64,1024]{1,0:T(8,128)(2,1)S(1)}, u32[]{:S(2)}, u32[]{:S(2)}) %collective-permute-start.12) | collective-permute-done | bytes 131104 | tf_op jit(solution)/shard_map/ppermute | solution.py:294
  65.7 0.7 copy-done.8
  66.4 0.6 copy-done.10
  67.1 0.9 %copy-done.4 = bf16[128,1024]{1,0:T(8,128)(2,1)S(1)} copy-done((bf16[128,1024]{1,0:T(8,128)(2,1)S(1)}, bf16[128,1024]{1,0:T(8,128)(2,1)}, u32[]{:S(2)}) %copy-start.4) | copy-done | bytes 262168
  68.0 0.9 %copy-done.6 = bf16[128,1024]{1,0:T(8,128)(2,1)S(1)} copy-done((bf16[128,1024]{1,0:T(8,128)(2,1)S(1)}, bf16[128,1024]{1,0:T(8,128)(2,1)}, u32[]{:S(2)}) %copy-start.6) | copy-done | bytes 262168
  69.0 0.9 %copy-done.9 = bf16[64,1024]{1,0:T(8,128)(2,1)S(1)} copy-done((bf16[64,1024]{1,0:T(8,128)(2,1)S(1)}, bf16[64,1024]{1,0:T(8,128)(2,1)}, u32[]{:S(2)}) %copy-start.9) | copy-done | bytes 131096
  69.9 0.9 %copy-done.11 = bf16[64,1024]{1,0:T(8,128)(2,1)S(1)} copy-done((bf16[64,1024]{1,0:T(8,128)(2,1)S(1)}, bf16[64,1024]{1,0:T(8,128)(2,1)}, u32[]{:S(2)}) %copy-start.11) | copy-done | bytes 131096
  70.8 2.1 %state.1 = f32[16,16,128]{2,1,0:T(8,128)} custom-call(s32[1,3]{1,0:T(1,128)S(1)} %copy-done.14, bf16[8,160,128]{2,1,0:T(8,128)(2,1)S(1)} %all-to-all-done.mixed_ref, f32[1,1024]{1,0:T(1,128)S(1)} %bitcast.9, bf16[1024,1024]{1,0:T(8,128)(2,1)S(1)} %copy-done.1, bf16[128,1024]{1,0:T(8,128)(2,1)S(1)} %pad_maximum_fusion.ta_ref, ...), custom_call_target="tpu_custom_call" | custom-call | flops 33554432 | bytes 3145728 | tf_op jit(solution)/shard_map/state/pallas_call | solution.py:407
  72.9 7.6 %all-to-all-start.1 = ((f32[16,16,128]{2,1,0:T(8,128)}), f32[16,16,128]{2,1,0:T(8,128)S(1)}, u32[]{:S(2)}, u32[]{:S(2)}) async-start(f32[16,16,128]{2,1,0:T(8,128)} %state.1), calls=%async_computation.1 | async-start | bytes 262144 | tf_op jit(solution)/shard_map/all_to_all | solution.py:416
  80.5 0.0 copy-start.7
  80.5 0.9 %copy-done.7 = bf16[128,1024]{1,0:T(8,128)(2,1)S(1)} copy-done((bf16[128,1024]{1,0:T(8,128)(2,1)S(1)}, bf16[128,1024]{1,0:T(8,128)(2,1)}, u32[]{:S(2)}) %copy-start.7) | copy-done | bytes 262168
  81.5 1.4 %layer.1 = bf16[128,1024]{1,0:T(8,128)(2,1)} custom-call(bf16[8,160,128]{2,1,0:T(8,128)(2,1)S(1)} %all-to-all-done.mixed_ref, bf16[128,1024]{1,0:T(8,128)(2,1)S(1)} %copy-done.7, bf16[128,1024]{1,0:T(8,128)(2,1)S(1)} %bitcast.8, f32[1,1024]{1,0:T(1,128)S(1)} %bitcast.10, bf16[1024,1024]{1,0:T(8,128)(2,1)S(1)} %copy-done.1), custom_call_target="tpu_custom_call" | custom-call | flops 268435456 | bytes 3145728 | tf_op jit(solution)/shard_map/layer/pallas_call | solution.py:418
  82.8 6.1 %all-to-all-done.1.score_ref = f32[16,16,128]{2,1,0:T(8,128)S(1)} async-done(((f32[16,16,128]{2,1,0:T(8,128)}), f32[16,16,128]{2,1,0:T(8,128)S(1)}, u32[]{:S(2)}, u32[]{:S(2)}) %all-to-all-start.1) | async-done | bytes 131104 | tf_op jit(solution)/shard_map/all_to_all | solution.py:416
  88.9 1.1 %pick.1 = f32[3,64]{1,0:T(4,128)} custom-call(f32[16,16,128]{2,1,0:T(8,128)S(1)} %all-to-all-done.1.score_ref, s32[8,64]{1,0:T(8,128)S(1)} %get-tuple-element.39.place_ref), custom_call_target="tpu_custom_call" | custom-call | flops 1048576 | bytes 131072 | tf_op jit(solution)/shard_map/pick/pallas_call | solution.py:428
  (48 shorter events, 0.2 us)
Async XLA Ops:
  0.6 27.5 %copy-start = (bf16[256,1024]{1,0:T(8,128)(2,1)S(1)}, bf16[256,1024]{1,0:T(8,128)(2,1)}, u32[]{:S(2)}) copy-start(bf16[256,1024]{1,0:T(8,128)(2,1)} %param.19) | copy-start | bytes 1572868
  0.6 3.1 %copy-start.14 = (s32[1,3]{1,0:T(1,128)S(1)}, s32[1,3]{1,0:T(1,128)}, u32[]{:S(2)}) copy-start(s32[1,3]{1,0:T(1,128)} %blocks_ref.7) | copy-start | bytes 40
  0.7 3.1 %copy-start.2 = (bf16[1,128,1024]{2,1,0:T(8,128)(2,1)S(1)}, bf16[1,128,1024]{2,1,0:T(8,128)(2,1)}, u32[]{:S(2)}) copy-start(bf16[1,128,1024]{2,1,0:T(8,128)(2,1)} %param.11) | copy-start | bytes 786436
  0.7 3.1 %copy-start.13 = (f32[1024]{0:T(1024)S(1)}, f32[1024]{0:T(1024)}, u32[]{:S(2)}) copy-start(f32[1024]{0:T(1024)} %param.12) | copy-start | bytes 12292
  0.7 3.1 %slice-start = ((s8[8388608]{0:T(1024)(128)(4,1)}), s8[4194304]{0:T(1024)(128)(4,1)S(1)}, s32[]{:S(2)}) async-start(s8[8388608]{0:T(1024)(128)(4,1)} %bitcast.5), calls=%async_computation.2 | async-start | bytes 8388608
  0.7 3.1 %copy-start.15 = (s32[1,3]{1,0:T(1,128)S(1)}, s32[1,3]{1,0:T(1,128)}, u32[]{:S(2)}) copy-start(s32[1,3]{1,0:T(1,128)} %tail_ref.3) | copy-start | bytes 40
  0.7 3.7 %slice-start.1 = ((s8[8388608]{0:T(1024)(128)(4,1)}), s8[4194304]{0:T(1024)(128)(4,1)S(1)}, s32[]{:S(2)}) async-start(s8[8388608]{0:T(1024)(128)(4,1)} %bitcast.5), calls=%async_computation.3 | async-start | bytes 8388608
  3.7 30.1 %copy-start.18 = (f32[8]{0:T(128)S(1)}, f32[8]{0:T(128)}, u32[]{:S(2)}) copy-start(f32[8]{0:T(128)} %slope_ref.1) | copy-start | bytes 100
  7.7 0.6 copy-start.16
  8.4 0.6 copy-start.17
  9.0 58.0 %copy-start.1 = (bf16[1024,1024]{1,0:T(8,128)(2,1)S(1)}, bf16[1024,1024]{1,0:T(8,128)(2,1)}, u32[]{:S(2)}) copy-start(bf16[1024,1024]{1,0:T(8,128)(2,1)} %w_ref.5) | copy-start | bytes 6291460
  9.0 58.0 %copy-start.12 = (f32[1024]{0:T(1024)S(1)}, f32[1024]{0:T(1024)}, u32[]{:S(2)}) copy-start(f32[1024]{0:T(1024)} %param.14) | copy-start | bytes 12292
  9.0 7.9 %collective-permute-start = (bf16[384,128]{1,0:T(8,128)(2,1)}, bf16[384,128]{1,0:T(8,128)(2,1)S(1)}, u32[]{:S(2)}, u32[]{:S(2)}) collective-permute-start(bf16[384,128]{1,0:T(8,128)(2,1)} %get-tuple-element.24), channel_id=1, source_target_pairs={{0,1},{1,0},{2,3},{3,2},{4,5},{5,4},{6,7},{7,6},{8,9},{9,8},{10,11... | collective-permute-start | bytes 294920 | tf_op jit(solution)/shard_map/ppermute | solution.py:298
  10.0 11.5 %collective-permute-start.1 = (bf16[384,128]{1,0:T(8,128)(2,1)}, bf16[384,128]{1,0:T(8,128)(2,1)S(1)}, u32[]{:S(2)}, u32[]{:S(2)}) collective-permute-start(bf16[384,128]{1,0:T(8,128)(2,1)} %get-tuple-element.25), channel_id=1, source_target_pairs={{0,8},{1,9},{2,10},{3,11},{4,12},{5,13},{6,14},{7,15},{8,0},{9,1},... | collective-permute-start | bytes 294920 | tf_op jit(solution)/shard_map/ppermute | solution.py:298
  13.3 14.1 %collective-permute-start.2 = (bf16[384,128]{1,0:T(8,128)(2,1)}, bf16[384,128]{1,0:T(8,128)(2,1)S(1)}, u32[]{:S(2)}, u32[]{:S(2)}) collective-permute-start(bf16[384,128]{1,0:T(8,128)(2,1)} %get-tuple-element.27), channel_id=1, source_target_pairs={{0,2},{1,3},{2,0},{3,1},{4,6},{5,7},{6,4},{7,5},{8,10},{9,11},{10,... | collective-permute-start | bytes 294920 | tf_op jit(solution)/shard_map/ppermute | solution.py:298
  14.7 13.4 %collective-permute-start.3 = (bf16[384,128]{1,0:T(8,128)(2,1)}, bf16[384,128]{1,0:T(8,128)(2,1)S(1)}, u32[]{:S(2)}, u32[]{:S(2)}) collective-permute-start(bf16[384,128]{1,0:T(8,128)(2,1)} %get-tuple-element.28), channel_id=1, source_target_pairs={{0,3},{1,2},{2,1},{3,0},{4,7},{5,6},{6,5},{7,4},{8,11},{9,10},{10,... | collective-permute-start | bytes 294920 | tf_op jit(solution)/shard_map/ppermute | solution.py:298
  16.6 15.9 %collective-permute-start.4 = (bf16[384,128]{1,0:T(8,128)(2,1)}, bf16[384,128]{1,0:T(8,128)(2,1)S(1)}, u32[]{:S(2)}, u32[]{:S(2)}) collective-permute-start(bf16[384,128]{1,0:T(8,128)(2,1)} %get-tuple-element.29), channel_id=1, source_target_pairs={{0,10},{1,11},{2,8},{3,9},{4,14},{5,15},{6,12},{7,13},{8,2},{9,3},... | collective-permute-start | bytes 294920 | tf_op jit(solution)/shard_map/ppermute | solution.py:298
  17.0 15.5 %collective-permute-start.5 = (bf16[384,128]{1,0:T(8,128)(2,1)}, bf16[384,128]{1,0:T(8,128)(2,1)S(1)}, u32[]{:S(2)}, u32[]{:S(2)}) collective-permute-start(bf16[384,128]{1,0:T(8,128)(2,1)} %copy-done.17), channel_id=1, source_target_pairs={{0,11},{1,10},{2,9},{3,8},{4,15},{5,14},{6,13},{7,12},{8,3},{9,2},... | collective-permute-start | bytes 294920 | tf_op jit(solution)/shard_map/ppermute | solution.py:298
  21.5 11.0 %collective-permute-start.6 = (bf16[384,128]{1,0:T(8,128)(2,1)}, bf16[384,128]{1,0:T(8,128)(2,1)S(1)}, u32[]{:S(2)}, u32[]{:S(2)}) collective-permute-start(bf16[384,128]{1,0:T(8,128)(2,1)} %copy-done.16), channel_id=1, source_target_pairs={{0,9},{1,8},{2,11},{3,10},{4,13},{5,12},{6,15},{7,14},{8,1},{9,0},... | collective-permute-start | bytes 294920 | tf_op jit(solution)/shard_map/ppermute | solution.py:298
  27.4 9.2 %collective-permute-start.7 = (bf16[3,256,128]{2,1,0:T(8,128)(2,1)S(1)}, bf16[3,256,128]{2,1,0:T(8,128)(2,1)S(1)}, u32[]{:S(2)}, u32[]{:S(2)}) collective-permute-start(bf16[3,256,128]{2,1,0:T(8,128)(2,1)S(1)} %get-tuple-element.26.near_ref), channel_id=1, source_target_pairs={{0,4},{1,5},{2,6},{3,7},{4,0},{5,1},{6,2},{7,3},{8,12},{9,13},{10,... | collective-permute-start | bytes 589832 | tf_op jit(solution)/shard_map/ppermute | solution.py:298
  28.1 15.6 %copy-start.19 = (bf16[32,1024]{1,0:T(8,128)(2,1)}, bf16[32,1024]{1,0:T(8,128)(2,1)S(1)}, u32[]{:S(2)}) copy-start(bf16[32,1024]{1,0:T(8,128)(2,1)S(1)} %constant_dynamic-slice_fusion) | copy-start | bytes 196612
  28.1 8.4 %collective-permute-start.9 = (bf16[32,1024]{1,0:T(8,128)(2,1)S(1)}, bf16[32,1024]{1,0:T(8,128)(2,1)S(1)}, u32[]{:S(2)}, u32[]{:S(2)}) collective-permute-start(bf16[32,1024]{1,0:T(8,128)(2,1)S(1)} %constant_dynamic-slice_fusion), channel_id=1, source_target_pairs={{0,32},{16,48},{32,0},{48,16},{64,96},{80,112},{96,64},{112,80},{1... | collective-permute-start | bytes 196616 | tf_op jit(solution)/shard_map/ppermute | solution.py:294
  32.5 9.0 %collective-permute-start.8 = (bf16[5,256,128]{2,1,0:T(8,128)(2,1)S(1)}, bf16[5,256,128]{2,1,0:T(8,128)(2,1)S(1)}, u32[]{:S(2)}, u32[]{:S(2)}) collective-permute-start(bf16[5,256,128]{2,1,0:T(8,128)(2,1)S(1)} %get-tuple-element.32.late_ref), channel_id=1, source_target_pairs={{0,4},{1,5},{2,6},{3,7},{4,0},{5,1},{6,2},{7,3},{8,12},{9,13},{10,... | collective-permute-start | bytes 983048 | tf_op jit(solution)/shard_map/ppermute | solution.py:298
  36.5 0.6 copy-start.20
  36.5 14.3 %collective-permute-start.10 = (bf16[64,1024]{1,0:T(8,128)(2,1)S(1)}, bf16[64,1024]{1,0:T(8,128)(2,1)}, u32[]{:S(2)}, u32[]{:S(2)}) collective-permute-start(bf16[64,1024]{1,0:T(8,128)(2,1)S(1)} %pad_maximum_fusion.1), channel_id=1, source_target_pairs={{0,16},{16,0},{32,48},{48,32},{64,80},{80,64},{96,112},{112,96},{1... | collective-permute-start | bytes 393224 | tf_op jit(solution)/shard_map/ppermute | solution.py:294
  43.7 23.4 %all-to-all-start = ((bf16[8,160,128]{2,1,0:T(8,128)(2,1)}), bf16[8,160,128]{2,1,0:T(8,128)(2,1)S(1)}, u32[]{:S(2)}, u32[]{:S(2)}) async-start(bf16[8,160,128]{2,1,0:T(8,128)(2,1)} %attend_last.1), calls=%async_computation | async-start | bytes 655360 | tf_op jit(solution)/shard_map/all_to_all | solution.py:405
  51.8 7.7 %collective-permute-start.11 = (bf16[128,1024]{1,0:T(8,128)(2,1)S(1)}, bf16[128,1024]{1,0:T(8,128)(2,1)S(1)}, u32[]{:S(2)}, u32[]{:S(2)}) collective-permute-start(bf16[128,1024]{1,0:T(8,128)(2,1)S(1)} %pad_maximum_fusion.ta_ref), channel_id=1, source_target_pairs={{0,64},{16,80},{32,96},{48,112},{64,128},{80,144},{96,160},{112,17... | collective-permute-start | bytes 786440 | tf_op jit(solution)/shard_map/ppermute | solution.py:294
  53.0 7.0 %collective-permute-start.13 = (bf16[128,1024]{1,0:T(8,128)(2,1)S(1)}, bf16[128,1024]{1,0:T(8,128)(2,1)S(1)}, u32[]{:S(2)}, u32[]{:S(2)}) collective-permute-start(bf16[128,1024]{1,0:T(8,128)(2,1)S(1)} %pad_maximum_fusion.ta_ref), channel_id=1, source_target_pairs={{0,192},{16,208},{32,224},{48,240},{64,0},{80,16},{96,32},{112,48}... | collective-permute-start | bytes 786440 | tf_op jit(solution)/shard_map/ppermute | solution.py:294
  59.5 6.3 %copy-start.3 = (bf16[128,1024]{1,0:T(8,128)(2,1)}, bf16[128,1024]{1,0:T(8,128)(2,1)S(1)}, u32[]{:S(2)}) copy-start(bf16[128,1024]{1,0:T(8,128)(2,1)S(1)} %collective-permute-done.11.tb_ref) | copy-start | bytes 786436
  59.5 6.3 %collective-permute-start.12 = (bf16[64,1024]{1,0:T(8,128)(2,1)S(1)}, bf16[64,1024]{1,0:T(8,128)(2,1)S(1)}, u32[]{:S(2)}, u32[]{:S(2)}) collective-permute-start(bf16[64,1024]{1,0:T(8,128)(2,1)S(1)} %slice.8), channel_id=1, source_target_pairs={{0,64},{16,80},{32,96},{48,112},{64,128},{80,144},{96,160},{112,17... | collective-permute-start | bytes 393224 | tf_op jit(solution)/shard_map/ppermute | solution.py:294
  60.0 5.7 %copy-start.5 = (bf16[128,1024]{1,0:T(8,128)(2,1)}, bf16[128,1024]{1,0:T(8,128)(2,1)S(1)}, u32[]{:S(2)}) copy-start(bf16[128,1024]{1,0:T(8,128)(2,1)S(1)} %collective-permute-done.13.te_ref) | copy-start | bytes 786436
  60.0 6.4 %collective-permute-start.14 = (bf16[64,1024]{1,0:T(8,128)(2,1)S(1)}, bf16[64,1024]{1,0:T(8,128)(2,1)S(1)}, u32[]{:S(2)}, u32[]{:S(2)}) collective-permute-start(bf16[64,1024]{1,0:T(8,128)(2,1)S(1)} %slice.9), channel_id=1, source_target_pairs={{0,192},{16,208},{32,224},{48,240},{64,0},{80,16},{96,32},{112,48}... | collective-permute-start | bytes 393224 | tf_op jit(solution)/shard_map/ppermute | solution.py:294
  65.7 0.7 copy-start.8
  66.4 0.6 copy-start.10
  67.0 1.0 %copy-start.4 = (bf16[128,1024]{1,0:T(8,128)(2,1)S(1)}, bf16[128,1024]{1,0:T(8,128)(2,1)}, u32[]{:S(2)}) copy-start(bf16[128,1024]{1,0:T(8,128)(2,1)} %copy-done.3) | copy-start | bytes 786436
  68.0 0.9 %copy-start.6 = (bf16[128,1024]{1,0:T(8,128)(2,1)S(1)}, bf16[128,1024]{1,0:T(8,128)(2,1)}, u32[]{:S(2)}) copy-start(bf16[128,1024]{1,0:T(8,128)(2,1)} %copy-done.5) | copy-start | bytes 786436
  69.0 0.9 %copy-start.9 = (bf16[64,1024]{1,0:T(8,128)(2,1)S(1)}, bf16[64,1024]{1,0:T(8,128)(2,1)}, u32[]{:S(2)}) copy-start(bf16[64,1024]{1,0:T(8,128)(2,1)} %copy-done.8) | copy-start | bytes 393220
  69.9 0.9 %copy-start.11 = (bf16[64,1024]{1,0:T(8,128)(2,1)S(1)}, bf16[64,1024]{1,0:T(8,128)(2,1)}, u32[]{:S(2)}) copy-start(bf16[64,1024]{1,0:T(8,128)(2,1)} %copy-done.10) | copy-start | bytes 393220
  72.9 16.0 %all-to-all-start.1 = ((f32[16,16,128]{2,1,0:T(8,128)}), f32[16,16,128]{2,1,0:T(8,128)S(1)}, u32[]{:S(2)}, u32[]{:S(2)}) async-start(f32[16,16,128]{2,1,0:T(8,128)} %state.1), calls=%async_computation.1 | async-start | bytes 262144 | tf_op jit(solution)/shard_map/all_to_all | solution.py:416
  80.5 1.0 %copy-start.7 = (bf16[128,1024]{1,0:T(8,128)(2,1)S(1)}, bf16[128,1024]{1,0:T(8,128)(2,1)}, u32[]{:S(2)}) copy-start(bf16[128,1024]{1,0:T(8,128)(2,1)} %get-tuple-element.38.gate_ref) | copy-start | bytes 786436
